TPU v7x, 32 devices: a whole 2x2x4 slice. The times are simulated.
32 devices in a mesh: dp: 8 (over y, x, core), seq: 4 (over z).
Axes of the slice: x: 2, y: 2, z: 4, core: 2. Of those that a mesh axis runs over, the one named last changes fastest.
Arguments:
- tokens: bfloat16 [16, 1024, 1536], P('dp', 'seq'), may hold values from -6 to 6
- cotangent: bfloat16 [16, 1024, 1536], P('dp', 'seq'), may hold values from -6 to 6
- in_proj: float32 [1536, 6448], P(('dp', 'seq')), may hold values from -0.15625 to 0.15625
- in_proj_mom: float32 [1536, 6448], P(('dp', 'seq')), may hold values from -6 to 6
- in_proj_var: float32 [1536, 6448], P(('dp', 'seq')), may hold values from 0.5 to 50
- out_proj: float32 [3072, 1536], P(('dp', 'seq')), may hold values from -0.109375 to 0.109375
- out_proj_mom: float32 [3072, 1536], P(('dp', 'seq')), may hold values from -6 to 6
- out_proj_var: float32 [3072, 1536], P(('dp', 'seq')), may hold values from 0.5 to 50
- conv_params: float32 [5, 3328], P(None, ('dp', 'seq')), may hold values from -0.6 to 0.6
- conv_mom: float32 [5, 3328], P(None, ('dp', 'seq')), may hold values from -6 to 6
- conv_var: float32 [5, 3328], P(None, ('dp', 'seq')), may hold values from 0.5 to 50
- norm_gain: float32 [1536], P(('dp', 'seq')), may hold values from 0.5 to 1.5
- norm_mom: float32 [1536], P(('dp', 'seq')), may hold values from -6 to 6
- norm_var: float32 [1536], P(('dp', 'seq')), may hold values from 0.5 to 50
- gate_gain: float32 [3072], P(('dp', 'seq')), may hold values from 0.5 to 1.5
- gate_mom: float32 [3072], P(('dp', 'seq')), may hold values from -6 to 6
- gate_var: float32 [3072], P(('dp', 'seq')), may hold values from 0.5 to 50
- head_params: float32 [3, 48], replicated, may hold values from -5 to 1.5, as said below
- head_mom: float32 [3, 48], replicated, may hold values from -6 to 6
- head_var: float32 [3, 48], replicated, may hold values from 0.5 to 50
Outputs:
- block_out: bfloat16 [16, 1024, 1536], P('dp', 'seq')
- tokens_grad: float32 [16, 1024, 1536], P('dp', 'seq')
- in_proj_grad: float32 [1536, 6448], P(('dp', 'seq'))
- out_proj_grad: float32 [3072, 1536], P(('dp', 'seq'))
- conv_grad: float32 [5, 3328], P(None, ('dp', 'seq'))
- norm_grad: float32 [1536], P(('dp', 'seq'))
- gate_grad: float32 [3072], P(('dp', 'seq'))
- head_grad: float32 [3, 48], replicated
- in_proj_new: float32 [1536, 6448], P(('dp', 'seq'))
- in_proj_mom_new: float32 [1536, 6448], P(('dp', 'seq'))
- in_proj_var_new: float32 [1536, 6448], P(('dp', 'seq'))
- out_proj_new: float32 [3072, 1536], P(('dp', 'seq'))
- out_proj_mom_new: float32 [3072, 1536], P(('dp', 'seq'))
- out_proj_var_new: float32 [3072, 1536], P(('dp', 'seq'))
- conv_new: float32 [5, 3328], P(None, ('dp', 'seq'))
- conv_mom_new: float32 [5, 3328], P(None, ('dp', 'seq'))
- conv_var_new: float32 [5, 3328], P(None, ('dp', 'seq'))
- norm_new: float32 [1536], P(('dp', 'seq'))
- norm_mom_new: float32 [1536], P(('dp', 'seq'))
- norm_var_new: float32 [1536], P(('dp', 'seq'))
- gate_new: float32 [3072], P(('dp', 'seq'))
- gate_mom_new: float32 [3072], P(('dp', 'seq'))
- gate_var_new: float32 [3072], P(('dp', 'seq'))
- head_new: float32 [3, 48], replicated
- head_mom_new: float32 [3, 48], replicated
- head_var_new: float32 [3, 48], replicated
Inputs may be any that keep to these rules, and one draw needn't show every extreme that they name: `head_params`: row 0 holds the logarithms of decay rates, row 1 skip weights, row 2 step biases.
All inputs are finite; a program needn't handle non-finite values.
Results may differ from a plain program's by a relative error of at most 0.0044.
The roundings to bfloat16 on the way count: a program that leaves them out, or rounds other values in their place, can miss the bound.
Values may be sent and summed in bfloat16 or wider, within the bound.
A program may use at most 256 MiB of HBM per device.

v0:
```python
import jax
import jax.numpy as jnp
from jax import lax
from jax.sharding import PartitionSpec as P

DI = 3072
HEADS = 48
HEAD_DIM = 64
STATE = 128
KERNEL = 4
STEP = 3
CONV = 3328


highest = lax.Precision.HIGHEST
norm_eps = 1e-05
beta_one = 0.9
beta_two = 0.95
learn_rate = 0.01
decay_rate = 0.1
adam_eps = 1e-08


def from_behind(array, axis, by):
    size = lax.axis_size(axis)
    pairs = [(i, i + by) for i in range(size) if 0 <= i + by < size]
    return lax.ppermute(array, axis, pairs)


def entering(part, axis, combine, identity):
    place = lax.axis_index(axis)
    gathered = jax.tree.map(lambda a: lax.all_gather(a, axis), part)
    state = jax.tree.map(lambda a, e: jnp.zeros_like(a) + jnp.asarray(e, a.dtype), part, identity)

    def one(lap, state):
        return combine(
            state, jax.tree.map(lambda a: lax.dynamic_index_in_dim(a, lap, 0, False), gathered)
        )

    return lax.fori_loop(0, place, one, state)


def prefix(array, axis, combine, identity):
    size, here = (lax.axis_size(axis), lax.axis_index(axis))
    everything = jax.tree.map(
        lambda part, kind: lax.all_gather(part.astype(kind), axis),
        array,
        jax.tree.map(lambda a: jnp.bfloat16 if a.dtype == jnp.float32 else a.dtype, array),
    )
    start = jax.tree.map(
        lambda part, zero: jnp.broadcast_to(jnp.asarray(zero, part.dtype), part.shape),
        array,
        identity,
    )

    def lap(k, before):
        at = size - 1 - k
        reached = at > here
        new = combine(
            before, jax.tree.map(lambda part, own: part[at].astype(own.dtype), everything, array)
        )
        return jax.tree.map(lambda a, b: jnp.where(reached, a, b), new, before)

    return lax.fori_loop(0, size, lap, start)


def rms_scale(values, gain):
    return values * lax.rsqrt(jnp.mean(values * values, axis=-1, keepdims=True) + norm_eps) * gain


def adamw(weight, moment_one, moment_two, gradient, decay_on):
    one_new = beta_one * moment_one + (1.0 - beta_one) * gradient
    two_new = beta_two * moment_two + (1.0 - beta_two) * gradient * gradient
    mean_hat = one_new / (1.0 - beta_one**STEP)
    var_hat = two_new / (1.0 - beta_two**STEP)
    weight_new = weight - learn_rate * (
        mean_hat / (jnp.sqrt(var_hat) + adam_eps) + decay_on * weight
    )
    return (weight_new, one_new, two_new)


def fold_pair(earlier, later):
    decay_early, state_early = earlier
    decay_later, state_later = later
    return (decay_early * decay_later, decay_later[:, :, None, None] * state_early + state_later)


def intra_item(pieces):
    head_x, b_proj, c_proj, step_size, decay_sum = pieces
    length = decay_sum.shape[0]
    scores = jnp.dot(c_proj, b_proj.T, precision=highest)
    row_ids = lax.broadcasted_iota(jnp.int32, (length, length), 0)
    col_ids = lax.broadcasted_iota(jnp.int32, (length, length), 1)
    causal = (col_ids <= row_ids)[None, :, :]
    sums_by_head = decay_sum.T
    gap_sums = sums_by_head[:, :, None] - sums_by_head[:, None, :]
    decay_mat = jnp.exp(jnp.where(causal, gap_sums, -1e30))
    weights = scores[None, :, :] * decay_mat * step_size.T[:, None, :]
    return jnp.einsum("hts,shp->thp", weights, head_x, precision=highest)


def front(conv_in, previous, conv_weight, step_raw, head_weight):
    seq_count = conv_in.shape[0]
    length = conv_in.shape[1]
    padded = jnp.concatenate([previous, conv_in], axis=1)
    conv_out = conv_weight[KERNEL]
    for tap_index in range(KERNEL):
        conv_out = conv_out + conv_weight[tap_index] * padded[:, tap_index : tap_index + length, :]
    activated = jax.nn.silu(conv_out)
    head_x = activated[:, :, :DI].reshape(seq_count, length, HEADS, HEAD_DIM)
    b_proj = activated[:, :, DI : DI + STATE]
    c_proj = activated[:, :, DI + STATE :]
    step_size = jax.nn.softplus(step_raw + head_weight[2])
    decay_sum = jnp.cumsum(step_size * -jnp.exp(head_weight[0]), axis=1)
    last_sum = decay_sum[:, -1, :]
    tail_weight = jnp.exp(last_sum[:, None, :] - decay_sum) * step_size
    local_state = jnp.einsum("gsh,gshp,gsn->ghpn", tail_weight, head_x, b_proj, precision=highest)
    return (local_state, jnp.exp(last_sum), head_x, b_proj, c_proj, step_size, decay_sum)


def back(head_x, b_proj, c_proj, step_size, decay_sum, head_weight, gate_z, gate_weight, state_in):
    seq_count = gate_z.shape[0]
    length = gate_z.shape[1]
    inner_out = lax.map(jax.checkpoint(intra_item), (head_x, b_proj, c_proj, step_size, decay_sum))
    carried = jnp.exp(decay_sum)[..., None] * jnp.einsum(
        "gtn,ghpn->gthp", c_proj, state_in, precision=highest
    )
    mixed_y = inner_out + carried + head_weight[1][:, None] * head_x
    gated = mixed_y.reshape(seq_count, length, DI) * jax.nn.silu(gate_z)
    return rms_scale(gated, gate_weight)


def body(
    tokens,
    cotangent,
    in_proj,
    in_proj_mom,
    in_proj_var,
    out_proj,
    out_proj_mom,
    out_proj_var,
    conv_params,
    conv_mom,
    conv_var,
    norm_gain,
    norm_mom,
    norm_var,
    gate_gain,
    gate_mom,
    gate_var,
    head_params,
    head_mom,
    head_var,
):
    in_full, out_full = (
        lax.all_gather(in_proj.astype(jnp.bfloat16), ("dp", "seq"), axis=0, tiled=True),
        lax.all_gather(out_proj.astype(jnp.bfloat16), ("dp", "seq"), axis=0, tiled=True),
    )
    conv_full, norm_full, gate_full = (
        lax.all_gather(conv_params, ("dp", "seq"), axis=1, tiled=True),
        lax.all_gather(norm_gain, ("dp", "seq"), axis=0, tiled=True),
        lax.all_gather(gate_gain, ("dp", "seq"), axis=0, tiled=True),
    )
    length = tokens.shape[1]
    rim_start = length - (KERNEL - 1)
    inputs = tokens.astype(jnp.float32)
    normed_in, norm_pull = jax.vjp(rms_scale, inputs, norm_full)
    lowered = normed_in.astype(jnp.bfloat16)
    projected = jnp.einsum("gtd,dp->gtp", lowered, in_full, preferred_element_type=jnp.float32)
    gate_z = projected[:, :, :DI]
    conv_in = projected[:, :, DI : DI + CONV]
    step_raw = projected[:, :, DI + CONV :]
    previous = from_behind(conv_in[:, rim_start:, :], "seq", 1)
    front_out, front_pull = jax.vjp(front, conv_in, previous, conv_full, step_raw, head_params)
    local_state, decays, head_x, b_proj, c_proj, step_size, decay_sum = front_out
    unit_decay = jnp.ones_like(decays)
    zero_state = jnp.zeros_like(local_state)
    reached, state_in = entering((decays, local_state), "seq", fold_pair, (unit_decay, zero_state))
    out_normed, back_pull = jax.vjp(
        back, head_x, b_proj, c_proj, step_size, decay_sum, head_params, gate_z, gate_full, state_in
    )
    out_lowered = out_normed.astype(jnp.bfloat16)
    branch = jnp.einsum("gti,id->gtd", out_lowered, out_full, preferred_element_type=jnp.float32)
    block_out = (inputs + branch).astype(jnp.bfloat16)
    out_grad_local = jnp.einsum(
        "gti,gtd->id", out_lowered, cotangent, preferred_element_type=jnp.float32
    )
    d_normed = jnp.einsum("gtd,id->gti", cotangent, out_full, preferred_element_type=jnp.float32)
    (
        d_head_x,
        d_b_proj,
        d_c_proj,
        d_step,
        d_decay_sum,
        d_head_back,
        d_gate_z,
        d_gate_gain,
        d_state_in,
    ) = back_pull(d_normed)
    later_decay, d_state_out = prefix(
        (decays, d_state_in), "seq", fold_pair, (unit_decay, zero_state)
    )
    d_decays = jnp.sum(d_state_out * state_in, axis=(2, 3))
    d_conv_in, d_previous, d_conv, d_step_raw, d_head_front = front_pull(
        (d_state_out, d_decays, d_head_x, d_b_proj, d_c_proj, d_step, d_decay_sum)
    )
    returned = from_behind(d_previous.astype(jnp.bfloat16), "seq", -1).astype(d_previous.dtype)
    d_conv_in = jnp.concatenate(
        [d_conv_in[:, :rim_start, :], d_conv_in[:, rim_start:, :] + returned], axis=1
    )
    d_projected = jnp.concatenate([d_gate_z, d_conv_in, d_step_raw], axis=-1).astype(jnp.bfloat16)
    in_grad_local = jnp.einsum(
        "gtd,gtp->dp", lowered, d_projected, preferred_element_type=jnp.float32
    )
    d_normed_in = jnp.einsum(
        "gtp,dp->gtd", d_projected, in_full, preferred_element_type=jnp.float32
    )
    d_inputs, norm_grad_local = norm_pull(d_normed_in)
    tokens_grad = cotangent.astype(jnp.float32) + d_inputs
    head_grad = lax.psum(d_head_back + d_head_front, ("dp", "seq"))
    in_grad, out_grad, conv_grad, norm_grad, gate_grad = (
        lax.psum_scatter(in_grad_local, ("dp", "seq"), scatter_dimension=0, tiled=True),
        lax.psum_scatter(out_grad_local, ("dp", "seq"), scatter_dimension=0, tiled=True),
        lax.psum_scatter(d_conv, ("dp", "seq"), scatter_dimension=1, tiled=True),
        lax.psum_scatter(norm_grad_local, ("dp", "seq"), scatter_dimension=0, tiled=True),
        lax.psum_scatter(d_gate_gain, ("dp", "seq"), scatter_dimension=0, tiled=True),
    )
    in_new, in_mom_new, in_var_new = adamw(in_proj, in_proj_mom, in_proj_var, in_grad, decay_rate)
    out_new, out_mom_new, out_var_new = adamw(
        out_proj, out_proj_mom, out_proj_var, out_grad, decay_rate
    )
    conv_new, conv_mom_new, conv_var_new = adamw(
        conv_params, conv_mom, conv_var, conv_grad, decay_rate
    )
    norm_new, norm_mom_new, norm_var_new = adamw(norm_gain, norm_mom, norm_var, norm_grad, 0.0)
    gate_new, gate_mom_new, gate_var_new = adamw(gate_gain, gate_mom, gate_var, gate_grad, 0.0)
    head_new, head_mom_new, head_var_new = adamw(head_params, head_mom, head_var, head_grad, 0.0)
    return (
        block_out,
        tokens_grad,
        in_grad,
        out_grad,
        conv_grad,
        norm_grad,
        gate_grad,
        head_grad,
        in_new,
        in_mom_new,
        in_var_new,
        out_new,
        out_mom_new,
        out_var_new,
        conv_new,
        conv_mom_new,
        conv_var_new,
        norm_new,
        norm_mom_new,
        norm_var_new,
        gate_new,
        gate_mom_new,
        gate_var_new,
        head_new,
        head_mom_new,
        head_var_new,
    )


def solution(mesh):
    in_specs = (
        P("dp", "seq", None),
        P("dp", "seq", None),
        P(("dp", "seq"), None),
        P(("dp", "seq"), None),
        P(("dp", "seq"), None),
        P(("dp", "seq"), None),
        P(("dp", "seq"), None),
        P(("dp", "seq"), None),
        P(None, ("dp", "seq")),
        P(None, ("dp", "seq")),
        P(None, ("dp", "seq")),
        P(("dp", "seq")),
        P(("dp", "seq")),
        P(("dp", "seq")),
        P(("dp", "seq")),
        P(("dp", "seq")),
        P(("dp", "seq")),
        P(),
        P(),
        P(),
    )
    out_specs = (
        P("dp", "seq", None),
        P("dp", "seq", None),
        P(("dp", "seq"), None),
        P(("dp", "seq"), None),
        P(None, ("dp", "seq")),
        P(("dp", "seq")),
        P(("dp", "seq")),
        P(),
        P(("dp", "seq"), None),
        P(("dp", "seq"), None),
        P(("dp", "seq"), None),
        P(("dp", "seq"), None),
        P(("dp", "seq"), None),
        P(("dp", "seq"), None),
        P(None, ("dp", "seq")),
        P(None, ("dp", "seq")),
        P(None, ("dp", "seq")),
        P(("dp", "seq")),
        P(("dp", "seq")),
        P(("dp", "seq")),
        P(("dp", "seq")),
        P(("dp", "seq")),
        P(("dp", "seq")),
        P(),
        P(),
        P(),
    )
    return jax.shard_map(body, mesh=mesh, in_specs=in_specs, out_specs=out_specs, check_vma=False)
```

profile of v0, /device:TPU:0, one launch (start us, length us, event | category | flops | bytes accessed | tf_op | source)
XLA Modules:
  0.0 1521.6 jit_solution(3277926250303956575)
XLA Ops:
  11.4 74.2 %all-gather.4 = f32[32,104,5]{1,2,0:T(8,128)S(1)} all-gather(f32[1,104,5]{1,2,0:T(8,128)} %bitcast.265), channel_id=1, replica_groups=mesh['dp'=8,'seq'=4] {'dp','seq'}, dimensions={0}, use_global_device_ids=true | all-gather | bytes 68640 | tf_op jit(solution)/shard_map/all_gather | solution.py:160
  87.5 42.4 %all-reduce.22 = (f32[1536]{0:T(1024)S(1)}, f32[3072]{0:T(1024)}) all-reduce(f32[1536]{0:T(1024)S(1)} %dynamic-update-slice, f32[3072]{0:T(1024)S(1)} %dynamic-update-slice.1), channel_id=1, replica_groups=mesh['dp'=8,'seq'=4] {'dp','seq'}, use_global_device_ids=true, to_apply=%add.16 | all-reduce | flops 4608 | bytes 36864
  133.8 11.8 all-gather.10.cloned.1.call-done
  145.7 18.2 %fusion.51 = f32[2,256,6448]{1,2,0:T(8,128)} fusion(bf16[1536,6448]{1,0:T(8,128)(2,1)} %all-gather.10.cloned.1.call-done, bf16[2,256,1536]{2,1,0:T(8,128)(2,1)} %param.28, f32[1536]{0:T(1024)S(1)} %get-tuple-element.805, f32[2,256]{1,0:T(2,128)S(1)} %fusion.116), kind=kOutput, calls=%fused_computation.63 | convolution fusion | flops 10144972800 | bytes 34594816 | tf_op jit(solution)/shard_map/gtd,dp->gtp/dot_general | solution.py:169
  163.9 3.0 slice.106
  181.2 2.7 collective-permute-start
  186.4 6.1 slice.107
  192.7 11.3 copy.381
  204.1 17.7 %fusion.123 = (f32[2,256,3328]{2,0,1:T(2,128)}, f32[2,256,3328]{2,0,1:T(2,128)}) fusion(f32[2,256,3328]{2,0,1:T(2,128)} %copy.381, f32[3328]{0:T(1024)S(1)} %get-tuple-element.738, f32[2,3,3328]{2,0,1:T(2,128)S(1)} %collective-permute-done, f32[3328]{0:T(1024)S(1)} %get-tuple-element.739, f32[3328]{0:T(1024)S(1)} %get-tuple-element.740, ...), kind=kLoop, calls=%fused_computation.219 | loop fusion | flops 25559040 | bytes 20593664 | tf_op jit(solution)/shard_map/jvp(jit(silu))/mul | solution.py:109
  221.8 7.6 slice.115
  229.4 10.2 copy.307
  242.3 8.4 fusion.70
  250.9 10.6 fusion.53
  261.8 6.5 slice.122
  268.4 10.5 copy.383
  278.9 10.1 all-gather
  289.0 3.5 broadcast.145.clone
  292.5 33.9 %while.64 = (s32[]{:T(128)}, f32[2,256,48,64]{1,3,2,0:T(8,128)}, f32[2,256,48,64]{1,3,2,0:T(8,128)}, f32[2,256,128]{2,1,0:T(8,128)S(1)}, f32[2,256,128]{2,1,0:T(...) while((s32[]{:T(128)}, f32[2,256,48,64]{1,3,2,0:T(8,128)}, ...), condition=%wide.region_4.5_spmd.clone, body=%wide.region_3.4_spmd.clone.sunk | while | flops 2529165312 | bytes 7489633 | solution.py:124
  292.9 16.5 %bitcast_dynamic-update-slice_fusion.11 = f32[2,256,48,64]{1,3,2,0:T(8,128)} fusion(f32[2,256,48,64]{1,3,2,0:T(8,128)} %get-tuple-element.1110, s32[]{:T(128)} %get-tuple-element.1109, f32[48,256]{1,0:T(8,128)S(1)} %get-tuple-element.1093, f32[48,256]{1,0:T(8,128)S(1)} %get-tuple-element.1094, f32[256,256]{1,0:T(8,128)S(1)} %fusion.194, ...), kind=kOutput, calls=%fused_computation.44.clone.1 | convolution fusion | flops 2428502016 | bytes 6767616 | tf_op jit(solution)/shard_map/jvp()/while/body/eval_jaxpr/hts,shp->thp/dot_general | solution.py:99
  309.9 16.6 %bitcast_dynamic-update-slice_fusion.11 = f32[2,256,48,64]{1,3,2,0:T(8,128)} fusion(f32[2,256,48,64]{1,3,2,0:T(8,128)} %get-tuple-element.1110, s32[]{:T(128)} %get-tuple-element.1109, f32[48,256]{1,0:T(8,128)S(1)} %get-tuple-element.1093, f32[48,256]{1,0:T(8,128)S(1)} %get-tuple-element.1094, f32[256,256]{1,0:T(8,128)S(1)} %fusion.194, ...), kind=kOutput, calls=%fused_computation.44.clone.1 | convolution fusion | flops 2428502016 | bytes 6767616 | tf_op jit(solution)/shard_map/jvp()/while/body/eval_jaxpr/hts,shp->thp/dot_general | solution.py:99
  326.5 141.3 %all-gather.14.cloned.1.call-done = f32[8,48,64,128]{3,2,1,0:T(8,128)} async-done(((f32[2,48,64,128]{3,2,1,0:T(8,128)}), f32[8,48,64,128]{3,2,1,0:T(8,128)}) %all-gather.14.cloned.1.call-update) | async-done | bytes 12582928 | tf_op jit(solution)/shard_map/all_gather | solution.py:32
  468.8 12.1 multiply_add_fusion.2
  480.9 10.5 copy.321
  491.4 13.4 multiply_reduce_fusion.11
  506.6 15.8 %multiply_reduce_fusion.8 = (f32[3072]{0:T(1024)}, f32[2,256]{0,1:T(8,128)}) fusion(f32[2,256,3072]{2,1,0:T(8,128)} %fusion.53, f32[2,256,3072]{2,0,1:T(2,128)} %get-tuple-element.838, f32[2,256]{0,1:T(8,128)} %copy.323, f32[3072]{0:T(1024)S(1)} %copy-done.54), kind=kLoop, calls=%fused_computation.92 | loop fusion | flops 9433600 | bytes 12611584 | tf_op jit(solution)/shard_map/transpose(jvp())/reduce_sum | solution.py:68
  524.2 28.3 %multiply_reduce_fusion.7 = (f32[3072]{0:T(1024)}, f32[2,256,3072]{2,0,1:T(2,128)}, bf16[2,256,3072]{2,0,1:T(2,128)(2,1)}, bf16[2,256,3072]{2,0,1:T(2,128)(2,1)}) fusion(f32[2,256,3328]{2,0,1:T(2,128)} %get-tuple-element.841, f32[2,256,3072]{2,0,1:T(2,128)} %copy.383, f32[2,256,3072]{2,0,1:T(2,128)} %get-tuple-element.838, f32[2,256]{0,1:T(8,128)} %copy.327, ...), kind=kLoop, calls=%fused_computation.91 | loop fusion | flops 36172800 | bytes 44068864 | tf_op jit(solution)/shard_map/transpose(jvp())/reduce_sum | solution.py:128
  552.5 10.3 copy.329
  562.7 8.7 fusion.88
  571.5 15.4 %all-gather.3 = bf16[8,1,48]{2,1,0:T(2,128)(2,1)S(1)} all-gather(bf16[2,1,48]{2,1,0:T(2,128)(2,1)S(1)} %copy.338), channel_id=5, replica_groups=mesh['dp'=8,'seq'=4] {'seq'}, dimensions={0}, use_global_device_ids=true | all-gather | bytes 960 | tf_op jit(solution)/shard_map/all_gather | solution.py:46
  587.5 8.7 copy.352
  596.2 12.8 fusion.97
  609.0 3.4 broadcast.145
  615.2 99.9 %while.63 = (s32[]{:T(128)}, f32[2,256,48,64]{1,3,2,0:T(8,128)}, f32[2,256,128]{2,0,1:T(2,128)}, f32[2,256,128]{2,0,1:T(2,128)}, f32[2,256,48]{1,2,0:T(8,128)}, ...) while((s32[]{:T(128)}, f32[2,256,48,64]{1,3,2,0:T(8,128)}, ...), condition=%wide.region_14.15_spmd, body=%wide.region_9.14_spmd.sunk | while | flops 5187293184 | bytes 48611840 | solution.py:124
  615.6 3.9 dynamic-slice_bitcast_fusion.15
  620.1 19.5 %fusion.187 = (f32[48,256]{1,0:T(8,128)S(1)}, f32[48,256]{1,0:T(8,128)S(1)}, f32[48,256]{1,0:T(8,128)}, f32[256,256]{1,0:T(8,128)S(1)}) fusion(f32[48,256]{1,0:T(8,128)S(1)} %bitcast.259, f32[48,256]{1,0:T(8,128)S(1)} %bitcast.257, f32[256,256]{1,0:T(8,128)S(1)} %fusion.186, pred[256,256]{1,0:T(8,128)(4,1)S(1)} %iota_compare_fusion.3, ...), kind=kOutput, calls=%fused_computation.11.clone.1 | convolution fusion | flops 2456711168 | bytes 7127040 | tf_op jit(solution)/shard_map/transpose(jvp())/while/body/eval_jaxpr/checkpoint/hts,shp->thp/dot_general | solution.py:99
  640.6 4.4 dynamic_update_slice.68
  646.2 4.4 dynamic_update_slice.67
  652.0 13.4 bitcast_dynamic-update-slice_fusion.8
  665.4 3.7 dynamic-slice_bitcast_fusion.15
  669.7 19.5 %fusion.187 = (f32[48,256]{1,0:T(8,128)S(1)}, f32[48,256]{1,0:T(8,128)S(1)}, f32[48,256]{1,0:T(8,128)}, f32[256,256]{1,0:T(8,128)S(1)}) fusion(f32[48,256]{1,0:T(8,128)S(1)} %bitcast.259, f32[48,256]{1,0:T(8,128)S(1)} %bitcast.257, f32[256,256]{1,0:T(8,128)S(1)} %fusion.186, pred[256,256]{1,0:T(8,128)(4,1)S(1)} %iota_compare_fusion.3, ...), kind=kOutput, calls=%fused_computation.11.clone.1 | convolution fusion | flops 2456711168 | bytes 7127040 | tf_op jit(solution)/shard_map/transpose(jvp())/while/body/eval_jaxpr/checkpoint/hts,shp->thp/dot_general | solution.py:99
  690.3 4.4 dynamic_update_slice.68
  695.9 4.4 dynamic_update_slice.67
  701.7 13.4 bitcast_dynamic-update-slice_fusion.8
  716.5 11.7 while.65
  728.2 14.2 fusion.94
  742.5 13.3 multiply_add_fusion.1
  755.7 10.5 copy.343
  766.5 37.1 %multiply_reduce_fusion.4 = (f32[3328]{0:T(1024)S(1)}, f32[3328]{0:T(1024)S(1)}, f32[3328]{0:T(1024)S(1)}, f32[3328]{0:T(1024)S(1)}, f32[3328]{0:T(1024)S(1)}, /*index=5*/f32[2,256,3328]{2,0,1:T(2,128)}) fusion(f32[2,256,3328]{2,0,1:T(2,128)} %copy.381, f32[2,3,3328]{2,0,1:T(2,128)S(1)} %copy-done.43, f32[2,256,3328]{2,0,1:T(2,128)} %get-tuple-element.842, ...), kind=kLoop, calls=%fused_computation.83 | loop fusion | flops 39173888 | bytes 27409408 | tf_op jit(solution)/shard_map/transpose(jvp())/reduce_sum | solution.py:108
  804.5 10.6 convolution_bitcast_fusion.1
  822.9 2.4 multiply_reduce_fusion.12
  825.7 5.0 reduce-window.16
  831.2 8.9 broadcast_multiply_fusion
  840.2 11.3 fusion.135
  858.7 30.4 %pad_maximum_fusion.1 = bf16[2,256,6448]{2,0,1:T(2,128)(2,1)} fusion(bf16[2,256,48]{2,0,1:T(2,128)(2,1)S(1)} %get-tuple-element.831, bf16[2,3,3328]{2,0,1:T(2,128)(2,1)S(1)} %fusion.112, bf16[2,253,3328]{2,0,1:T(2,128)(2,1)S(1)} %slice.123, bf16[2,256,3072]{2,0,1:T(2,128)(2,1)S(1)} %copy-done.6), kind=kLoop, calls=%fused_computation.87 | loop fusion | flops 26411008 | bytes 13205504 | tf_op jit(solution)/shard_map/concatenate | solution.py:211
  889.1 17.3 %copy.349 = bf16[2,256,6448]{1,2,0:T(8,128)(2,1)} copy(bf16[2,256,6448]{2,0,1:T(2,128)(2,1)} %pad_maximum_fusion.1) | data formatting | bytes 13205504 | tf_op jit(solution)/shard_map/concatenate | solution.py:211
  906.4 20.3 %convolution_bitcast_fusion = f32[1536,6448]{1,0:T(8,128)} fusion(bf16[2,256,6448]{1,2,0:T(8,128)(2,1)} %copy.349, bf16[2,256,1536]{2,1,0:T(8,128)(2,1)S(1)} %copy-done.16, f32[1536]{0:T(1024)S(1)} %copy-done.64, f32[2,256]{1,0:T(2,128)S(1)} %copy-done.66), kind=kOutput, calls=%fused_computation.60 | convolution fusion | flops 10144972800 | bytes 47800320 | tf_op jit(solution)/shard_map/gtd,gtp->dp/dot_general | solution.py:212
  927.6 10.3 fusion.85
  939.5 19.8 %fusion.77 = (f32[1536]{0:T(1024)S(1)}, f32[2,256]{1,0:T(2,128)S(1)}, f32[2,256,1536]{2,1,0:T(8,128)}) fusion(bf16[2,256,1536]{2,1,0:T(8,128)(2,1)S(1)} %copy-done.16, f32[2,256]{1,0:T(2,128)S(1)} %copy-done.66, f32[1536]{0:T(1024)S(1)} %copy-done.64, bf16[2,256,6448]{1,2,0:T(8,128)(2,1)} %copy.349, bf16[1536,6448]{1,0:T(8,128)(2,1)} %all-gather.10.cloned.1.call-done), kind=kOutput, calls=%fused_computation.123 | convolution fusion | flops 10147330048 | bytes 31145984 | tf_op jit(solution)/shard_map/gtp,dp->gtd/dot_general | solution.py:215
  959.3 40.7 %all-reduce.21 = (f32[1536]{0:T(1024)S(1)}, f32[3072]{0:T(1024)S(1)}, f32[3,48]{1,0:T(4,128)S(1)}) all-reduce(f32[1536]{0:T(1024)S(1)} %get-tuple-element.735, f32[3072]{0:T(1024)S(1)} %copy-done.55, f32[3,48]{1,0:T(4,128)S(1)} %add_add_fusion.2), channel_id=9, replica_groups=mesh['dp'=8,'seq'=4] {'dp','seq'}, use_global_device_ids=true, to_apply=%region_32.33.clone | all-reduce | flops 4752 | bytes 38016
  1001.9 5.0 fusion.78
  1007.0 133.3 %reduce-scatter.6.cloned.1.call-done = f32[96,1536]{1,0:T(8,128)} async-done(((f32[3072,1536]{1,0:T(8,128)}), f32[96,1536]{1,0:T(8,128)}) %reduce-scatter.6.cloned.1.call-update) | async-done | bytes 589840 | tf_op jit(solution)/shard_map/reduce_scatter | solution.py:223
  1140.3 2.9 multiply_subtract_fusion.1
  1143.2 366.8 %reduce-scatter.4.cloned.1.call-done = f32[48,6448]{1,0:T(8,128)} async-done(((f32[1536,6448]{1,0:T(8,128)}), f32[48,6448]{1,0:T(8,128)}) %reduce-scatter.4.cloned.1.call-update) | async-done | bytes 1238032 | tf_op jit(solution)/shard_map/reduce_scatter | solution.py:222
  1510.0 4.5 multiply_subtract_fusion
  (319 shorter events, 81.3 us)
Async XLA Ops:
  7.2 138.5 %all-gather.10.cloned.1.call-start = ((), (), s32[]{:S(2)}) async-start(), calls=%async_computation.2 | async-start | bytes 20680704 | tf_op jit(solution)/shard_map/all_gather | solution.py:156
  9.5 241.4 %all-gather.12.cloned.1.call-start = ((), (), s32[]{:S(2)}) async-start(), calls=%async_computation.3 | async-start | bytes 9732096 | tf_op jit(solution)/shard_map/all_gather | solution.py:157
  11.3 456.4 %all-gather.14.cloned.1.call-start = ((), (), s32[]{:S(2)}) async-start(), calls=%async_computation.6 | async-start | bytes 15728640 | tf_op jit(solution)/shard_map/all_gather | solution.py:32
  129.9 15.8 %copy-start.63 = (f32[1536]{0:T(1024)}, f32[1536]{0:T(1024)S(1)}, u32[]{:S(2)}) copy-start(f32[1536]{0:T(1024)S(1)} %get-tuple-element.805) | copy-start | bytes 18436
  130.7 73.3 %copy-start.44 = (f32[3328]{0:T(1024)}, f32[3328]{0:T(1024)S(1)}, u32[]{:S(2)}) copy-start(f32[3328]{0:T(1024)S(1)} %get-tuple-element.738) | copy-start | bytes 39940
  130.7 73.4 %copy-start.46 = (f32[3328]{0:T(1024)}, f32[3328]{0:T(1024)S(1)}, u32[]{:S(2)}) copy-start(f32[3328]{0:T(1024)S(1)} %get-tuple-element.739) | copy-start | bytes 39940
  130.7 73.4 %copy-start.48 = (f32[3328]{0:T(1024)}, f32[3328]{0:T(1024)S(1)}, u32[]{:S(2)}) copy-start(f32[3328]{0:T(1024)S(1)} %get-tuple-element.740) | copy-start | bytes 39940
  181.2 22.8 %collective-permute-start = (f32[2,3,3328]{2,0,1:T(2,128)}, f32[2,3,3328]{2,0,1:T(2,128)S(1)}, u32[]{:S(2)}, u32[]{:S(2)}) collective-permute-start(f32[2,3,3328]{2,0,1:T(2,128)} %copy.305), channel_id=1, source_target_pairs={{0,1},{1,2},{2,3},{4,5},{5,6},{6,7},{8,9},{9,10},{10,11},{12,13},{... | collective-permute-start | bytes 239624 | tf_op jit(solution)/shard_map/ppermute | solution.py:27
  192.7 48.9 %copy-start.30 = (f32[2,256,48]{1,2,0:T(8,128)}, f32[2,256,48]{1,2,0:T(8,128)S(1)}, u32[]{:S(2)}) copy-start(f32[2,256,48]{1,2,0:T(8,128)S(1)} %copy.317) | copy-start | bytes 294916
  204.0 17.8 %copy-start.42 = (f32[2,3,3328]{2,0,1:T(2,128)}, f32[2,3,3328]{2,0,1:T(2,128)S(1)}, u32[]{:S(2)}) copy-start(f32[2,3,3328]{2,0,1:T(2,128)S(1)} %collective-permute-done) | copy-start | bytes 239620
  250.8 465.7 %all-gather.16.cloned.1.call-start = ((), (), s32[]{:S(2)}) async-start(), calls=%async_computation.7 | async-start | bytes 7864320 | tf_op jit(solution)/shard_map/all_gather | solution.py:46
  326.5 141.3 %copy-start.11 = (f32[2,256,128]{2,1,0:T(8,128)}, f32[2,256,128]{2,1,0:T(8,128)S(1)}, u32[]{:S(2)}) copy-start(f32[2,256,128]{2,1,0:T(8,128)S(1)} %get-tuple-element.1239) | copy-start | bytes 786436
  326.5 141.3 %copy-start.18 = (f32[2,256,48]{1,2,0:T(8,128)}, f32[2,256,48]{1,2,0:T(8,128)S(1)}, u32[]{:S(2)}) copy-start(f32[2,256,48]{1,2,0:T(8,128)S(1)} %get-tuple-element.1242) | copy-start | bytes 294916
  326.5 141.3 %copy-start.20 = (f32[2,256,48]{1,2,0:T(8,128)}, f32[2,256,48]{1,2,0:T(8,128)S(1)}, u32[]{:S(2)}) copy-start(f32[2,256,48]{1,2,0:T(8,128)S(1)} %get-tuple-element.1243) | copy-start | bytes 294916
  468.2 128.0 %copy-start.1 = (f32[2,48,64,128]{3,2,1,0:T(8,128)}, f32[2,48,64,128]{3,2,1,0:T(8,128)S(1)}, u32[]{:S(2)}) copy-start(f32[2,48,64,128]{3,2,1,0:T(8,128)S(1)} %get-tuple-element.520) | copy-start | bytes 9437188
  491.4 15.2 copy-start.54
  571.4 366.6 %all-reduce.25.cloned.1.call-start = ((), (), s32[]{:S(2)}) async-start(), calls=%async_computation.8 | async-start | bytes 212992
  615.2 101.3 %copy-start.3 = (f32[2,48,64,128]{3,2,1,0:T(8,128)S(1)}, f32[2,48,64,128]{3,2,1,0:T(8,128)}, u32[]{:S(2)}) copy-start(f32[2,48,64,128]{3,2,1,0:T(8,128)} %custom-call) | copy-start | bytes 9437188
  619.5 20.0 %copy-start.5 = (f32[256,48,64]{0,2,1:T(8,128)}, f32[256,48,64]{0,2,1:T(8,128)S(1)}, u32[]{:S(2)}) copy-start(f32[256,48,64]{0,2,1:T(8,128)S(1)} %get-tuple-element.1079) | copy-start | bytes 9437188 | tf_op jit(solution)/shard_map/transpose(jvp())/while
  619.6 19.9 %copy-start.32 = (f32[256,48]{0,1:T(8,128)}, f32[256,48]{0,1:T(8,128)S(1)}, u32[]{:S(2)}) copy-start(f32[256,48]{0,1:T(8,128)S(1)} %get-tuple-element.1076) | copy-start | bytes 147460 | tf_op jit(solution)/shard_map/transpose(jvp())/while
  619.6 19.9 %copy-start.33 = (f32[256,48]{0,1:T(8,128)}, f32[256,48]{0,1:T(8,128)S(1)}, u32[]{:S(2)}) copy-start(f32[256,48]{0,1:T(8,128)S(1)} %get-tuple-element.1075) | copy-start | bytes 147460 | tf_op jit(solution)/shard_map/transpose(jvp())/while
  620.0 19.5 %copy-start.13 = (f32[256,256]{1,0:T(8,128)}, f32[256,256]{1,0:T(8,128)S(1)}, u32[]{:S(2)}) copy-start(f32[256,256]{1,0:T(8,128)S(1)} %fusion.186) | copy-start | bytes 786436 | tf_op jit(solution)/shard_map/transpose(jvp())/while
  620.0 19.5 %copy-start.28 = (pred[256,256]{1,0:T(8,128)(4,1)}, pred[256,256]{1,0:T(8,128)(4,1)S(1)}, u32[]{:S(2)}) copy-start(pred[256,256]{1,0:T(8,128)(4,1)S(1)} %iota_compare_fusion.3) | copy-start | bytes 196612 | tf_op jit(solution)/shard_map/transpose(jvp())/while
  620.0 19.5 %copy-start.40 = (f32[2,256,48]{1,2,0:T(8,128)S(1)}, f32[2,256,48]{1,2,0:T(8,128)}, u32[]{:S(2)}) copy-start(f32[2,256,48]{1,2,0:T(8,128)} %get-tuple-element.1170) | copy-start | bytes 294916 | tf_op jit(solution)/shard_map/transpose(jvp())/while
  652.0 13.4 copy-start.10
  669.1 20.0 %copy-start.5 = (f32[256,48,64]{0,2,1:T(8,128)}, f32[256,48,64]{0,2,1:T(8,128)S(1)}, u32[]{:S(2)}) copy-start(f32[256,48,64]{0,2,1:T(8,128)S(1)} %get-tuple-element.1079) | copy-start | bytes 9437188 | tf_op jit(solution)/shard_map/transpose(jvp())/while
  669.2 19.9 %copy-start.32 = (f32[256,48]{0,1:T(8,128)}, f32[256,48]{0,1:T(8,128)S(1)}, u32[]{:S(2)}) copy-start(f32[256,48]{0,1:T(8,128)S(1)} %get-tuple-element.1076) | copy-start | bytes 147460 | tf_op jit(solution)/shard_map/transpose(jvp())/while
  669.2 19.9 %copy-start.33 = (f32[256,48]{0,1:T(8,128)}, f32[256,48]{0,1:T(8,128)S(1)}, u32[]{:S(2)}) copy-start(f32[256,48]{0,1:T(8,128)S(1)} %get-tuple-element.1075) | copy-start | bytes 147460 | tf_op jit(solution)/shard_map/transpose(jvp())/while
  669.6 19.5 %copy-start.13 = (f32[256,256]{1,0:T(8,128)}, f32[256,256]{1,0:T(8,128)S(1)}, u32[]{:S(2)}) copy-start(f32[256,256]{1,0:T(8,128)S(1)} %fusion.186) | copy-start | bytes 786436 | tf_op jit(solution)/shard_map/transpose(jvp())/while
  669.7 19.5 %copy-start.28 = (pred[256,256]{1,0:T(8,128)(4,1)}, pred[256,256]{1,0:T(8,128)(4,1)S(1)}, u32[]{:S(2)}) copy-start(pred[256,256]{1,0:T(8,128)(4,1)S(1)} %iota_compare_fusion.3) | copy-start | bytes 196612 | tf_op jit(solution)/shard_map/transpose(jvp())/while
  669.7 19.5 %copy-start.40 = (f32[2,256,48]{1,2,0:T(8,128)S(1)}, f32[2,256,48]{1,2,0:T(8,128)}, u32[]{:S(2)}) copy-start(f32[2,256,48]{1,2,0:T(8,128)} %get-tuple-element.1170) | copy-start | bytes 294916 | tf_op jit(solution)/shard_map/transpose(jvp())/while
  701.7 13.4 copy-start.10
  728.2 27.6 %copy-start.4 = (f32[2,48,64,128]{3,2,1,0:T(8,128)}, f32[2,48,64,128]{3,2,1,0:T(8,128)S(1)}, u32[]{:S(2)}) copy-start(f32[2,48,64,128]{3,2,1,0:T(8,128)S(1)} %get-tuple-element.523) | copy-start | bytes 9437188
  728.2 14.3 copy-start
  728.2 14.3 copy-start.24
  728.2 14.3 copy-start.62
  766.5 38.0 %copy-start.22 = (bf16[2,256,3072]{1,2,0:T(8,128)(2,1)S(1)}, bf16[2,256,3072]{1,2,0:T(8,128)(2,1)}, u32[]{:S(2)}) copy-start(bf16[2,256,3072]{1,2,0:T(8,128)(2,1)} %copy.352) | copy-start | bytes 9437188
  804.4 335.9 %reduce-scatter.6.cloned.1.call-start = ((), (), s32[]{:S(2)}) async-start(), calls=%async_computation.5 | async-start | bytes 19464192 | tf_op jit(solution)/shard_map/reduce_scatter | solution.py:223
  815.2 16.0 %copy-start.45 = (f32[3328]{0:T(1024)S(1)}, f32[3328]{0:T(1024)}, u32[]{:S(2)}) copy-start(f32[3328]{0:T(1024)} %copy-done.44) | copy-start | bytes 39940
  815.2 16.0 %copy-start.47 = (f32[3328]{0:T(1024)S(1)}, f32[3328]{0:T(1024)}, u32[]{:S(2)}) copy-start(f32[3328]{0:T(1024)} %copy-done.46) | copy-start | bytes 39940
  815.2 16.0 %copy-start.49 = (f32[3328]{0:T(1024)S(1)}, f32[3328]{0:T(1024)}, u32[]{:S(2)}) copy-start(f32[3328]{0:T(1024)} %copy-done.48) | copy-start | bytes 39940
  815.2 694.8 %reduce-scatter.4.cloned.1.call-start = ((), (), s32[]{:S(2)}) async-start(), calls=%async_computation.4 | async-start | bytes 41361408 | tf_op jit(solution)/shard_map/reduce_scatter | solution.py:222
  818.0 13.2 copy-start.51
  840.1 13.0 copy-start.15
  840.2 13.0 copy-start.26
  840.2 13.0 copy-start.27
  840.2 13.0 copy-start.36
  851.6 6.2 collective-permute-start.1
  889.1 17.3 %copy-start.16 = (bf16[2,256,1536]{2,1,0:T(8,128)(2,1)S(1)}, bf16[2,256,1536]{2,1,0:T(8,128)(2,1)}, u32[]{:S(2)}) copy-start(bf16[2,256,1536]{2,1,0:T(8,128)(2,1)} %param.28) | copy-start | bytes 4718596
  889.1 17.3 %copy-start.64 = (f32[1536]{0:T(1024)S(1)}, f32[1536]{0:T(1024)}, u32[]{:S(2)}) copy-start(f32[1536]{0:T(1024)} %copy-done.63) | copy-start | bytes 18436
  889.1 17.3 %copy-start.66 = (f32[2,256]{1,0:T(2,128)S(1)}, f32[2,256]{1,0:T(2,128)}, u32[]{:S(2)}) copy-start(f32[2,256]{1,0:T(2,128)} %copy-done.65) | copy-start | bytes 6148
  939.5 19.9 %copy-start.55 = (f32[3072]{0:T(1024)S(1)}, f32[3072]{0:T(1024)}, u32[]{:S(2)}) copy-start(f32[3072]{0:T(1024)} %get-tuple-element.732) | copy-start | bytes 36868
  939.5 60.6 %copy-start.75 = (f32[96]{0:T(128)S(1)}, f32[96]{0:T(128)}, u32[]{:S(2)}) copy-start(f32[96]{0:T(128)} %param.42) | copy-start | bytes 1156
  939.5 60.6 %copy-start.76 = (f32[96]{0:T(128)S(1)}, f32[96]{0:T(128)}, u32[]{:S(2)}) copy-start(f32[96]{0:T(128)} %param.43) | copy-start | bytes 1156
  939.5 60.6 %copy-start.77 = (f32[96]{0:T(128)S(1)}, f32[96]{0:T(128)}, u32[]{:S(2)}) copy-start(f32[96]{0:T(128)} %param.44) | copy-start | bytes 1156
  939.5 61.2 %copy-start.78 = (f32[48]{0:T(128)S(1)}, f32[48]{0:T(128)}, u32[]{:S(2)}) copy-start(f32[48]{0:T(128)} %param.39) | copy-start | bytes 580
  939.5 61.2 %copy-start.79 = (f32[48]{0:T(128)S(1)}, f32[48]{0:T(128)}, u32[]{:S(2)}) copy-start(f32[48]{0:T(128)} %param.40) | copy-start | bytes 580
  939.5 61.2 %copy-start.80 = (f32[48]{0:T(128)S(1)}, f32[48]{0:T(128)}, u32[]{:S(2)}) copy-start(f32[48]{0:T(128)} %param.41) | copy-start | bytes 580
  939.5 61.8 %copy-start.57 = (f32[2,256]{1,0:T(2,128)S(1)}, f32[2,256]{1,0:T(2,128)}, u32[]{:S(2)}) copy-start(f32[2,256]{1,0:T(2,128)} %copy-done.56) | copy-start | bytes 6148
  939.5 61.8 %copy-start.72 = (f32[3,48]{1,0:T(4,128)S(1)}, f32[3,48]{1,0:T(4,128)}, u32[]{:S(2)}) copy-start(f32[3,48]{1,0:T(4,128)} %param.46) | copy-start | bytes 1732
  939.5 61.8 %copy-start.73 = (f32[3,48]{1,0:T(4,128)S(1)}, f32[3,48]{1,0:T(4,128)}, u32[]{:S(2)}) copy-start(f32[3,48]{1,0:T(4,128)} %param.47) | copy-start | bytes 1732
  959.3 181.0 %copy-start.25 = (f32[96,1536]{1,0:T(8,128)S(1)}, f32[96,1536]{1,0:T(8,128)}, u32[]{:S(2)}) copy-start(f32[96,1536]{1,0:T(8,128)} %param.33) | copy-start | bytes 1769476
  1000.0 143.2 %copy-start.74 = (f32[3,48]{1,0:T(4,128)}, f32[3,48]{1,0:T(4,128)S(1)}, u32[]{:S(2)}) copy-start(f32[3,48]{1,0:T(4,128)S(1)} %get-tuple-element.804) | copy-start | bytes 1732
  1001.9 508.1 %copy-start.17 = (f32[48,6448]{1,0:T(8,128)S(1)}, f32[48,6448]{1,0:T(8,128)}, u32[]{:S(2)}) copy-start(f32[48,6448]{1,0:T(8,128)} %param.30) | copy-start | bytes 3714052
  (40 other events, 275.0 us)
Sparse Core Ops, SparseCore 0:
  11.4 134.2 all-gather.9
  149.0 80.9 all-gather.11
  250.9 216.8 all-gather.13
  571.6 120.9 all-gather.15
  804.6 121.0 all-reduce.24
  932.5 207.7 reduce-scatter.5
  1147.3 362.6 reduce-scatter.3
where the time goes:
time: 1530 us; the launch traced here: 1520 us
  waiting for transfers between devices  655 us (43%)
  matrix products  264 us (17%)
  other arithmetic  220 us (14%)
  blocking collectives  183 us (12%)
  local copies, waits for them, and re-layouts  179 us (12%)
  between operations  15.3 us (1%)
    reduce_scatter x1, waiting for transfers between devices, body(): lax.psum_scatter(in_grad_local, ('dp', 'seq'), scatter_dimension=0, tiled...  367 us
    all_gather x1, waiting for transfers between devices, entering(): gathered = jax.tree.map(lambda a: lax.all_gather(a, axis), part)  141 us
    reduce_scatter x1, waiting for transfers between devices, body(): lax.psum_scatter(out_grad_local, ('dp', 'seq'), scatter_dimension=0, tile...  133 us
    dot_general x6, matrix products, intra_item(): return jnp.einsum('hts,shp->thp', weights, head_x, precision=highest)  98.9 us
    unnamed x2, blocking collectives  83.1 us
    all_gather x1, blocking collectives, body(): lax.all_gather(conv_params, ('dp', 'seq'), axis=1, tiled=True)  74.2 us
    reduce_sum x1, other arithmetic, front(): conv_weight[tap_index] * padded[:, tap_index:tap_index + length, :]  37.1 us
    dot_general x3, matrix products, front(): jnp.einsum('gsh,gshp,gsn->ghpn', tail_weight, head_x, b_proj, precision=h...  35.9 us
  transfers between devices with their start and end apart: 9, of which 5 were waited for; matrix products, arithmetic and copies ran while one was open for 30% of the time, Pallas kernels for 0%

commit v1 on v0

--- a/solution.py
+++ b/solution.py
@@ -1,7 +1,13 @@
+import functools
+
 import jax
 import jax.numpy as jnp
 from jax import lax
+from jax.experimental import pallas as pl
+from jax.experimental.pallas import tpu as pltpu
 from jax.sharding import PartitionSpec as P
+
+MESH = pl.DeviceIdType.MESH
 
 DI = 3072
 HEADS = 48
@@ -130,7 +136,145 @@
     return rms_scale(gated, gate_weight)
 
 
+TM, TN = 1536, 256
+HT = TN // 2
+
+def rs_call(lhs, rhs, lhs_of, rhs_of, n, skew, collective_id):
+    SK = skew
+    NS = SK + 1
+    def kernel(lhs_ref, rhs_ref, out_ref, own0, own1, own2, own3, s0, s1, s2, s3, r0, r1, r2, r3,
+               ss0, ss1, ss2, ss3, rr0, rr1, rr2, rr3):
+        dp = lax.axis_index("dp"); z = lax.axis_index("seq")
+        c = lax.rem(dp, 2); x = lax.rem(dp // 2, 2); y = dp // 4
+        core_peer = {"dp": dp + 1 - 2 * c}
+        x_peer = {"dp": dp + 2 - 4 * x}
+        y_peer = {"dp": dp + 4 - 8 * y}
+        def zp(k): return {"seq": lax.rem(z + k, 4)}
+        bar = pltpu.get_barrier_semaphore()
+        for d in (core_peer, x_peer, y_peer, zp(1), zp(2), zp(3)):
+            pl.semaphore_signal(bar, inc=1, device_id=d, device_id_type=MESH)
+        pl.semaphore_wait(bar, 6)
+
+        def c0(i, sl): return pltpu.make_async_remote_copy(src_ref=s0.at[sl], dst_ref=r0.at[i], send_sem=ss0.at[sl], recv_sem=rr0.at[i], device_id=core_peer, device_id_type=MESH)
+        def c1(i, sl, h): return pltpu.make_async_remote_copy(src_ref=s1.at[sl, h], dst_ref=r1.at[i, h], send_sem=ss1.at[sl, h], recv_sem=rr1.at[i, h], device_id=(x_peer, y_peer)[h], device_id_type=MESH)
+        def c2(i, sl, h): return pltpu.make_async_remote_copy(src_ref=s2.at[sl, h], dst_ref=r2.at[i, h], send_sem=ss2.at[sl, h], recv_sem=rr2.at[i, h], device_id=(y_peer, x_peer)[h], device_id_type=MESH)
+        def c3(i, sl, k): return pltpu.make_async_remote_copy(src_ref=s3.at[sl, k - 1], dst_ref=r3.at[i, k - 1], send_sem=ss3.at[sl, k - 1], recv_sem=rr3.at[i, k - 1], device_id=zp(k), device_id_type=MESH)
+        bf = jnp.bfloat16; f32 = jnp.float32
+
+        def step(it, _):
+            @pl.when(it < n)
+            def _():
+                i = it; sl = lax.rem(i, NS)
+                @pl.when(i >= NS)
+                def _(): c0(i, sl).wait_send()
+                li, ri = lhs_of(i), rhs_of(i)
+                part = jnp.dot(lhs_ref[li, 1 - c], rhs_ref[ri], preferred_element_type=f32).astype(bf).reshape(2, 2, 192, TN)
+                for h in range(2):
+                    s0[sl, h] = part[..., h * HT:(h + 1) * HT]
+                c0(i, sl).start()
+                part = jnp.dot(lhs_ref[li, c], rhs_ref[ri], preferred_element_type=f32).reshape(2, 2, 192, TN)
+                for h in range(2):
+                    own0[sl, h] = part[..., h * HT:(h + 1) * HT]
+            @pl.when((it >= SK) & (it < n + SK))
+            def _():
+                i = it - SK; sl = lax.rem(i, NS)
+                @pl.when(i >= NS)
+                def _():
+                    for h in range(2): c1(i, sl, h).wait_send()
+                c0(i, sl).wait_recv()
+                s1[sl, 0] = (own0[sl, 0, 1 - x] + r0[i, 0, 1 - x].astype(f32)).astype(bf)
+                c1(i, sl, 0).start()
+                for a in range(2):
+                    s1[sl, 1, a] = (own0[sl, 1, a, 1 - y] + r0[i, 1, a, 1 - y].astype(f32)).astype(bf)
+                c1(i, sl, 1).start()
+                own1[sl, 0] = own0[sl, 0, x] + r0[i, 0, x].astype(f32)
+                for a in range(2):
+                    own1[sl, 1, a] = own0[sl, 1, a, y] + r0[i, 1, a, y].astype(f32)
+            @pl.when((it >= 2 * SK) & (it < n + 2 * SK))
+            def _():
+                i = it - 2 * SK; sl = lax.rem(i, NS)
+                @pl.when(i >= NS)
+                def _():
+                    for h in range(2): c2(i, sl, h).wait_send()
+                for h, g in ((0, y), (1, x)):
+                    c1(i, sl, h).wait_recv()
+                    s2[sl, h] = (own1[sl, h, 1 - g] + r1[i, h, 1 - g].astype(f32)).astype(bf)
+                    c2(i, sl, h).start()
+                    own2[sl, h] = own1[sl, h, g] + r1[i, h, g].astype(f32)
+            @pl.when((it >= 3 * SK) & (it < n + 3 * SK))
+            def _():
+                i = it - 3 * SK; sl = lax.rem(i, NS)
+                @pl.when(i >= NS)
+                def _():
+                    for k in range(1, 4): c3(i, sl, k).wait_send()
+                for h in range(2): c2(i, sl, h).wait_recv()
+                for k in (2, 1, 3):
+                    zz = lax.rem(z + k, 4) * 48
+                    for h in range(2):
+                        rows = pl.ds(pl.multiple_of(zz, 16), 48)
+                        s3[sl, k - 1, h] = (own2[sl, h, rows] + r2[i, h, rows].astype(f32)).astype(bf)
+                    c3(i, sl, k).start()
+                rows = pl.ds(pl.multiple_of(z * 48, 16), 48)
+                for h in range(2):
+                    own3[sl, h] = own2[sl, h, rows] + r2[i, h, rows].astype(f32)
+            @pl.when(it >= 4 * SK)
+            def _():
+                i = it - 4 * SK; sl = lax.rem(i, NS)
+                for k in range(1, 4): c3(i, sl, k).wait_recv()
+                acc = own3[sl]
+                for k in range(3): acc = acc + r3[i, k].astype(f32)
+                out_ref[i] = acc
+            return 0
+        lax.fori_loop(0, n + 4 * SK, step, 0)
+        for j in range(NS):
+            i = n - NS + j; sl = i % NS
+            c0(i, sl).wait_send()
+            for h in range(2): c1(i, sl, h).wait_send(); c2(i, sl, h).wait_send()
+            for k in range(1, 4): c3(i, sl, k).wait_send()
+    bf = jnp.bfloat16; f32 = jnp.float32
+    V = pltpu.VMEM; D = pltpu.SemaphoreType.DMA
+    return pl.pallas_call(
+        kernel, out_shape=jax.ShapeDtypeStruct((n, 2, 48, HT), f32),
+        in_specs=[pl.BlockSpec(memory_space=pltpu.VMEM)] * 2, out_specs=pl.BlockSpec(memory_space=pltpu.VMEM),
+        scratch_shapes=[V((NS, 2, 2, 2, 192, HT), f32), V((NS, 2, 2, 192, HT), f32), V((NS, 2, 192, HT), f32), V((NS, 2, 48, HT), f32),
+            V((NS, 2, 2, 2, 192, HT), bf), V((NS, 2, 2, 192, HT), bf), V((NS, 2, 192, HT), bf), V((NS, 3, 2, 48, HT), bf),
+            V((n, 2, 2, 2, 192, HT), bf), V((n, 2, 2, 192, HT), bf), V((n, 2, 192, HT), bf), V((n, 3, 2, 48, HT), bf),
+            D((NS,)), D((NS, 2)), D((NS, 2)), D((NS, 3)), D((n,)), D((n, 2)), D((n, 2)), D((n, 3))],
+        compiler_params=pltpu.CompilerParams(collective_id=collective_id, has_side_effects=True, vmem_limit_bytes=63 << 20),
+        name="rs",
+    )(lhs, rhs)
+
+
+def by_owner(rows):
+    per = rows.shape[0] // 32
+    subs = per // 48
+    rows = rows.reshape(2, 2, 2, 4, subs, 48, rows.shape[1])
+    return rows.transpose(4, 2, 1, 0, 3, 5, 6).reshape(subs, 2, 768, rows.shape[-1])
+
+
+def in_columns(columns):
+    tokens, width = columns.shape
+    return columns.reshape(tokens, width // TN, TN).transpose(1, 0, 2)
+
+
+def reduce_out(out_lowered, cotangent):
+    sums = rs_call(
+        by_owner(out_lowered.T), in_columns(cotangent), lambda i: lax.rem(i, 2), lambda i: i // 2, 12, 2, 1
+    )
+    sums = sums.reshape(6, 2, 2, 48, HT).transpose(1, 3, 0, 2, 4)
+    return sums.reshape(96, 6 * TN)
+
+
+def reduce_in(lowered, d_projected):
+    width = d_projected.shape[1]
+    tasks = -(-width // TN)
+    padded = jnp.pad(d_projected, ((0, 0), (0, tasks * TN - width)))
+    sums = rs_call(by_owner(lowered.T), in_columns(padded), lambda i: 0, lambda i: i, tasks, 2, 2)
+    return sums.transpose(2, 0, 1, 3).reshape(48, tasks * TN)[:, :width]
+
+
 def body(
+    own_reduce,
     tokens,
     cotangent,
     in_proj,
@@ -156,11 +300,13 @@
         lax.all_gather(in_proj.astype(jnp.bfloat16), ("dp", "seq"), axis=0, tiled=True),
         lax.all_gather(out_proj.astype(jnp.bfloat16), ("dp", "seq"), axis=0, tiled=True),
     )
-    conv_full, norm_full, gate_full = (
-        lax.all_gather(conv_params, ("dp", "seq"), axis=1, tiled=True),
-        lax.all_gather(norm_gain, ("dp", "seq"), axis=0, tiled=True),
-        lax.all_gather(gate_gain, ("dp", "seq"), axis=0, tiled=True),
-    )
+    taps = conv_params.shape[1]
+    small = lax.all_gather(
+        jnp.concatenate([conv_params.reshape(-1), norm_gain, gate_gain]), ("dp", "seq"), axis=0
+    )
+    conv_full = small[:, : 5 * taps].reshape(-1, 5, taps).transpose(1, 0, 2).reshape(5, -1)
+    norm_full = small[:, 5 * taps : 5 * taps + norm_gain.shape[0]].reshape(-1)
+    gate_full = small[:, 5 * taps + norm_gain.shape[0] :].reshape(-1)
     length = tokens.shape[1]
     rim_start = length - (KERNEL - 1)
     inputs = tokens.astype(jnp.float32)
@@ -182,9 +328,16 @@
     out_lowered = out_normed.astype(jnp.bfloat16)
     branch = jnp.einsum("gti,id->gtd", out_lowered, out_full, preferred_element_type=jnp.float32)
     block_out = (inputs + branch).astype(jnp.bfloat16)
-    out_grad_local = jnp.einsum(
-        "gti,gtd->id", out_lowered, cotangent, preferred_element_type=jnp.float32
-    )
+    flat = tokens.shape[0] * length
+    if own_reduce:
+        out_grad = reduce_out(out_lowered.reshape(flat, -1), cotangent.reshape(flat, -1))
+    else:
+        out_grad_local = jnp.einsum(
+            "gti,gtd->id", out_lowered, cotangent, preferred_element_type=jnp.float32
+        )
+        out_grad = lax.psum_scatter(
+            out_grad_local, ("dp", "seq"), scatter_dimension=0, tiled=True
+        )
     d_normed = jnp.einsum("gtd,id->gti", cotangent, out_full, preferred_element_type=jnp.float32)
     (
         d_head_x,
@@ -209,18 +362,20 @@
         [d_conv_in[:, :rim_start, :], d_conv_in[:, rim_start:, :] + returned], axis=1
     )
     d_projected = jnp.concatenate([d_gate_z, d_conv_in, d_step_raw], axis=-1).astype(jnp.bfloat16)
-    in_grad_local = jnp.einsum(
-        "gtd,gtp->dp", lowered, d_projected, preferred_element_type=jnp.float32
-    )
+    if own_reduce:
+        in_grad = reduce_in(lowered.reshape(flat, -1), d_projected.reshape(flat, -1))
+    else:
+        in_grad_local = jnp.einsum(
+            "gtd,gtp->dp", lowered, d_projected, preferred_element_type=jnp.float32
+        )
+        in_grad = lax.psum_scatter(in_grad_local, ("dp", "seq"), scatter_dimension=0, tiled=True)
     d_normed_in = jnp.einsum(
         "gtp,dp->gtd", d_projected, in_full, preferred_element_type=jnp.float32
     )
     d_inputs, norm_grad_local = norm_pull(d_normed_in)
     tokens_grad = cotangent.astype(jnp.float32) + d_inputs
     head_grad = lax.psum(d_head_back + d_head_front, ("dp", "seq"))
-    in_grad, out_grad, conv_grad, norm_grad, gate_grad = (
-        lax.psum_scatter(in_grad_local, ("dp", "seq"), scatter_dimension=0, tiled=True),
-        lax.psum_scatter(out_grad_local, ("dp", "seq"), scatter_dimension=0, tiled=True),
+    conv_grad, norm_grad, gate_grad = (
         lax.psum_scatter(d_conv, ("dp", "seq"), scatter_dimension=1, tiled=True),
         lax.psum_scatter(norm_grad_local, ("dp", "seq"), scatter_dimension=0, tiled=True),
         lax.psum_scatter(d_gate_gain, ("dp", "seq"), scatter_dimension=0, tiled=True),
@@ -316,4 +471,6 @@
         P(),
         P(),
     )
-    return jax.shard_map(body, mesh=mesh, in_specs=in_specs, out_specs=out_specs, check_vma=False)
+    own_reduce = tuple(mesh.shape[a] for a in ("dp", "seq")) == (8, 4)
+    step = functools.partial(body, own_reduce)
+    return jax.shard_map(step, mesh=mesh, in_specs=in_specs, out_specs=out_specs, check_vma=False)

time: 1530 us -> 1310 us (0.86)
  Pallas kernels: 0 us -> 159 us
  blocking collectives: 183 us -> 65.8 us
  waiting for transfers between devices: 655 us -> 553 us
  other arithmetic: 220 us -> 156 us
  matrix products: 264 us -> 217 us
  local copies, waits for them, and re-layouts: 179 us -> 133 us
    reduce_scatter x2 -> x0, waiting for transfers between devices: 500 us -> none  [the longest x1 367 us: body(): lax.psum_scatter(in_grad_local, ('dp', 'seq'), scatter_dimension=0, tiled...]
    unnamed x8, waiting for transfers between devices: 0.14 us -> 220 us
    pallas_call x0 -> x2, Pallas kernels: none -> 159 us  [rs_call(): pl.pallas_call(kernel, out_shape=jax.ShapeDtypeStruct((n, 2, 48, HT), f32...]
    all_gather x1, waiting for transfers between devices: 11.8 us -> 131 us  [body(): lax.all_gather(in_proj.astype(jnp.bfloat16), ('dp', 'seq'), axis=0, tiled...]
    all_gather x1 -> x0, blocking collectives: 74.2 us -> none  [body(): lax.all_gather(conv_params, ('dp', 'seq'), axis=1, tiled=True)]
    all_gather x1, waiting for transfers between devices: 0.02 us -> 62.6 us  [body(): lax.all_gather(out_proj.astype(jnp.bfloat16), ('dp', 'seq'), axis=0, tile...]
    unnamed x2 -> x1, blocking collectives: 83.1 us -> 38.8 us
    dot_general x2 -> x0, matrix products: 31 us -> none  [the longest x1 20.3 us: body(): jnp.einsum('gtd,gtp->dp', lowered, d_projected, preferred_element_type=jn...]
  transfers between devices with their start and end apart: 9 -> 8, of which waited for: 5 -> 5; matrix products, arithmetic and copies ran while one was open for 30% -> 17% of each run, Pallas kernels for 0% -> 4%
where the time goes in v1:
time: 1310 us
  waiting for transfers between devices  553 us (42%)
  matrix products  217 us (17%)
  Pallas kernels  159 us (12%)
  other arithmetic  156 us (12%)
  local copies, waits for them, and re-layouts  133 us (10%)
  blocking collectives  65.8 us (5%)
  between operations  15.6 us (1%)
    unnamed x8, waiting for transfers between devices  220 us
    pallas_call x2, Pallas kernels, rs_call(): pl.pallas_call(kernel, out_shape=jax.ShapeDtypeStruct((n, 2, 48, HT), f32...  159 us
    all_gather x1, waiting for transfers between devices, entering(): gathered = jax.tree.map(lambda a: lax.all_gather(a, axis), part)  138 us
    all_gather x1, waiting for transfers between devices, body(): lax.all_gather(in_proj.astype(jnp.bfloat16), ('dp', 'seq'), axis=0, tiled...  131 us
    dot_general x6, matrix products, intra_item(): return jnp.einsum('hts,shp->thp', weights, head_x, precision=highest)  92.3 us
    all_gather x1, waiting for transfers between devices, body(): lax.all_gather(out_proj.astype(jnp.bfloat16), ('dp', 'seq'), axis=0, tile...  62.6 us
    unnamed x1, blocking collectives  38.8 us
    dot_general x3, matrix products, front(): jnp.einsum('gsh,gshp,gsn->ghpn', tail_weight, head_x, b_proj, precision=h...  31.1 us
  transfers between devices with their start and end apart: 8, of which 5 were waited for; matrix products, arithmetic and copies ran while one was open for 17% of the time, Pallas kernels for 4%

profile of v1, /device:TPU:0, one launch (start us, length us, event | category | flops | bytes accessed | tf_op | source)
XLA Modules:
  0.0 1305.6 jit_solution(1704563945608147233)
XLA Ops:
  15.1 123.3 %all-reduce.25.cloned.1.call-done = f32[21248]{0:T(1024)} async-done(((f32[21248]{0:T(1024)}), f32[21248]{0:T(1024)}) %all-reduce.25.cloned.1.call-update) | async-done | bytes 85008
  142.1 131.3 %all-gather.10.cloned.1.call-done = bf16[1536,6448]{1,0:T(8,128)(2,1)} async-done(((bf16[48,6448]{1,0:T(8,128)(2,1)}), bf16[1536,6448]{1,0:T(8,128)(2,1)}) %all-gather.10.cloned.1.call-update) | async-done | bytes 19808272 | tf_op jit(solution)/shard_map/all_gather | solution.py:300
  273.3 17.6 %fusion.53 = f32[2,256,6448]{1,2,0:T(8,128)} fusion(bf16[2,256,1536]{2,1,0:T(8,128)(2,1)S(1)} %fusion.85, bf16[1536,6448]{1,0:T(8,128)(2,1)} %all-gather.10.cloned.1.call-done), kind=kOutput, calls=%fused_computation.66 | convolution fusion | flops 10141827072 | bytes 34586624 | tf_op jit(solution)/shard_map/gtd,dp->gtp/dot_general | solution.py:315
  290.9 4.8 slice.128
  295.7 2.5 copy.248
  298.2 3.1 collective-permute-start
  305.6 6.1 slice.129
  313.8 17.2 %fusion.63 = (f32[2,256,3328]{1,2,0:T(8,128)S(1)}, f32[2,256,3328]{1,2,0:T(8,128)}) fusion(f32[2,256,3328]{1,2,0:T(8,128)} %slice.129, f32[3328]{0:T(1024)S(1)} %mul.709, f32[2,3,3328]{1,2,0:T(8,128)S(1)} %copy.249, f32[3328]{0:T(1024)S(1)} %mul.706, f32[3328]{0:T(1024)S(1)} %mul.703, f32[3328]{0:T(1024)} %mul.694, f32[3328]{0:T(1024)} %add.288), kind=kLoop, calls=%fused_computation.91 | loop fusion | flops 25559040 | bytes 20593664 | tf_op jit(solution)/shard_map/jvp(jit(silu))/mul | solution.py:115
  335.8 7.2 fusion.79
  344.5 3.4 reshape.357
  354.7 9.1 all-gather.4
  364.3 17.9 %all-gather.1 = f32[8,1,48]{2,1,0:T(1,128)S(1)} all-gather(f32[2,1,48]{2,1,0:T(1,128)S(1)} %bitcast.319), channel_id=3, replica_groups=mesh['dp'=8,'seq'=4] {'seq'}, dimensions={0}, use_global_device_ids=true | all-gather | bytes 1920 | tf_op jit(solution)/shard_map/all_gather | solution.py:38
  383.6 3.4 broadcast.145.clone
  387.1 33.9 %while.64 = (s32[]{:T(128)}, f32[2,256,48,64]{1,3,2,0:T(8,128)}, f32[2,256,48,64]{1,3,2,0:T(8,128)}, f32[2,256,128]{2,1,0:T(8,128)S(1)}, f32[2,256,128]{2,1,0:T(...) while((s32[]{:T(128)}, f32[2,256,48,64]{1,3,2,0:T(8,128)}, ...), condition=%wide.region_4.5_spmd.clone, body=%wide.region_3.4_spmd.clone.sunk | while | flops 2529165312 | bytes 7489641 | solution.py:130
  387.5 16.6 %bitcast_dynamic-update-slice_fusion.11 = f32[2,256,48,64]{1,3,2,0:T(8,128)} fusion(f32[2,256,48,64]{1,3,2,0:T(8,128)} %get-tuple-element.1069, s32[]{:T(128)S(6)} %copy.387, f32[48,256]{1,0:T(8,128)S(1)} %get-tuple-element.1052, f32[48,256]{1,0:T(8,128)S(1)} %get-tuple-element.1053, f32[256,256]{1,0:T(8,128)S(1)} %fusion.202, ...), kind=kOutput, calls=%fused_computation.48.clone.1 | convolution fusion | flops 2428502016 | bytes 6767616 | tf_op jit(solution)/shard_map/jvp()/while/body/eval_jaxpr/hts,shp->thp/dot_general | solution.py:105
  404.4 16.5 %bitcast_dynamic-update-slice_fusion.11 = f32[2,256,48,64]{1,3,2,0:T(8,128)} fusion(f32[2,256,48,64]{1,3,2,0:T(8,128)} %get-tuple-element.1069, s32[]{:T(128)S(6)} %copy.387, f32[48,256]{1,0:T(8,128)S(1)} %get-tuple-element.1052, f32[48,256]{1,0:T(8,128)S(1)} %get-tuple-element.1053, f32[256,256]{1,0:T(8,128)S(1)} %fusion.202, ...), kind=kOutput, calls=%fused_computation.48.clone.1 | convolution fusion | flops 2428502016 | bytes 6767616 | tf_op jit(solution)/shard_map/jvp()/while/body/eval_jaxpr/hts,shp->thp/dot_general | solution.py:105
  421.0 138.4 %all-gather.14.cloned.1.call-done = f32[8,48,64,128]{3,2,1,0:T(8,128)} async-done(((f32[2,48,64,128]{3,2,1,0:T(8,128)}), f32[8,48,64,128]{3,2,1,0:T(8,128)}) %all-gather.14.cloned.1.call-update) | async-done | bytes 12582928 | tf_op jit(solution)/shard_map/all_gather | solution.py:38
  560.4 11.2 multiply_add_fusion.2
  571.6 8.0 multiply_reduce_fusion.11
  579.6 62.6 %all-gather.12.cloned.1.call-done = bf16[3072,1536]{1,0:T(8,128)(2,1)} async-done(((bf16[96,1536]{1,0:T(8,128)(2,1)}), bf16[3072,1536]{1,0:T(8,128)(2,1)}) %all-gather.12.cloned.1.call-update) | async-done | bytes 9437200 | tf_op jit(solution)/shard_map/all_gather | solution.py:301
  642.3 12.9 multiply_reduce_fusion.8
  655.3 12.6 multiply_reduce_fusion.7
  667.9 2.6 copy-done.1
  670.4 6.1 fusion.98
  676.6 3.4 broadcast.145
  682.8 73.5 %while.63 = (s32[]{:T(128)}, f32[2,256,48,64]{1,3,2,0:T(8,128)}, f32[2,256,128]{1,2,0:T(8,128)}, f32[2,256,128]{1,2,0:T(8,128)}, f32[2,256,48]{1,2,0:T(8,128)}, ...) while((s32[]{:T(128)}, f32[2,256,48,64]{1,3,2,0:T(8,128)}, ...), condition=%wide.region_14.15_spmd, body=%wide.region_9.14_spmd.sunk | while | flops 5187293184 | bytes 86622728 | solution.py:130
  683.0 4.3 dynamic-slice_bitcast_fusion.15
  688.9 10.7 bitcast_dynamic-update-slice_fusion.8
  699.7 18.8 %fusion.195 = (f32[48,256]{1,0:T(8,128)S(1)}, f32[48,256]{1,0:T(8,128)S(1)}, f32[48,256]{1,0:T(8,128)S(1)}, f32[256,256]{1,0:T(8,128)S(1)}) fusion(f32[48,256]{1,0:T(8,128)S(1)} %bitcast.312, f32[48,256]{1,0:T(8,128)S(1)} %bitcast.310, f32[256,256]{1,0:T(8,128)S(1)} %fusion.194, pred[256,256]{1,0:T(8,128)(4,1)S(1)} %iota_compare_fusion.3, ...), kind=kOutput, calls=%fused_computation.11.clone.1 | convolution fusion | flops 2456711168 | bytes 7127040 | tf_op jit(solution)/shard_map/transpose(jvp())/while/body/eval_jaxpr/checkpoint/hts,shp->thp/dot_general | solution.py:105
  720.2 3.7 dynamic-slice_bitcast_fusion.15
  725.0 10.7 bitcast_dynamic-update-slice_fusion.8
  735.8 18.9 %fusion.195 = (f32[48,256]{1,0:T(8,128)S(1)}, f32[48,256]{1,0:T(8,128)S(1)}, f32[48,256]{1,0:T(8,128)S(1)}, f32[256,256]{1,0:T(8,128)S(1)}) fusion(f32[48,256]{1,0:T(8,128)S(1)} %bitcast.312, f32[48,256]{1,0:T(8,128)S(1)} %bitcast.310, f32[256,256]{1,0:T(8,128)S(1)} %fusion.194, pred[256,256]{1,0:T(8,128)(4,1)S(1)} %iota_compare_fusion.3, ...), kind=kOutput, calls=%fused_computation.11.clone.1 | convolution fusion | flops 2456711168 | bytes 7127040 | tf_op jit(solution)/shard_map/transpose(jvp())/while/body/eval_jaxpr/checkpoint/hts,shp->thp/dot_general | solution.py:105
  759.8 3.0 copy.287
  762.8 4.7 copy.294
  767.5 3.2 copy.295
  772.7 55.9 %rs.3 = f32[12,2,48,128]{3,2,1,0:T(8,128)} custom-call(bf16[2,2,768,512]{3,2,1,0:T(8,128)(2,1)} %bitcast.298, bf16[6,512,256]{2,1,0:T(8,128)(2,1)} %bitcast.306), custom_call_target="tpu_custom_call" | custom-call | tf_op jit(solution)/shard_map/rs/pallas_call | solution.py:236
  830.9 10.3 fusion.108
  842.7 9.9 fusion.95
  852.6 20.2 %while.65 = (s32[]{:T(128)}, f32[2,48,64,128]{3,2,1,0:T(8,128)}, s32[]{:T(128)}, bf16[4,2,48]{2,1,0:T(2,128)(2,1)}, bf16[4,2,48,64,128]{4,3,2,1,0:T(8,128)(2,1)}...) while((s32[]{:T(128)}, f32[2,48,64,128]{3,2,1,0:T(8,128)}, s32[]{:T(128)}, ...), condition=%wide.region_16.17_spmd.clone, body=%wide.region_15.16_spmd.clone.sunk | while | flops 3932264 | bytes 7865455 | solution.py:70
  853.4 3.8 fusion.203
  857.8 4.6 fusion.203
  863.0 4.6 fusion.203
  868.2 4.6 fusion.203
  872.8 2.5 multiply_reduce_fusion.12
  875.6 14.5 %multiply_add_fusion.1 = (f32[2,256,48,64]{1,3,2,0:T(8,128)}, f32[2,256,48]{1,2,0:T(8,128)}, f32[2,256,48]{1,2,0:T(8,128)}) fusion(f32[2,256,48,64]{1,3,2,0:T(8,128)} %get-tuple-element.524, f32[2,256,48,64]{1,3,2,0:T(8,128)} %get-tuple-element.1184, f32[48]{0:T(128)S(1)} %copy-done.77, f32[2,256,48]{1,2,0:T(8,128)S(1)} %copy-done.41, ...), kind=kOutput, calls=%fused_computation.108 | convolution fusion | flops 2428452864 | bytes 35160256 | tf_op jit(solution)/shard_map/transpose(jvp(gsh,gshp,gsn->ghpn))/dot_general | solution.py:123
  899.6 6.3 reduce-window.16
  910.4 9.4 fusion.111
  919.8 22.2 %multiply_reduce_fusion.5 = (f32[3328]{0:T(1024)S(1)}, f32[3328]{0:T(1024)S(1)}, f32[3328]{0:T(1024)S(1)}, f32[3328]{0:T(1024)S(1)}, f32[3328]{0:T(1024)S(1)}, /*index=5*/f32[2,256,3328]{1,2,0:T(8,128)S(1)}) fusion(f32[2,256,6448]{1,2,0:T(8,128)} %fusion.53, f32[2,256,3328]{1,2,0:T(8,128)} %slice.129, f32[2,3,3328]{1,2,0:T(8,128)S(1)} %copy-done.11, ...), kind=kLoop, calls=%fused_computation.89 | loop fusion | flops 39173888 | bytes 34225152 | tf_op jit(solution)/shard_map/transpose(jvp())/reduce_sum | solution.py:114
  942.2 9.7 broadcast_multiply_fusion
  954.6 12.8 pad_add_fusion
  967.7 3.6 copy-done.9
  971.3 3.0 slice.146
  977.1 97.1 %all-reduce.27.cloned.1.call-done = f32[5,3328]{1,0:T(8,128)} async-done(((f32[5,3328]{1,0:T(8,128)}), f32[5,3328]{1,0:T(8,128)}) %all-reduce.27.cloned.1.call-update) | async-done | bytes 66576
  1079.8 4.9 maximum_convert_fusion
  1084.7 5.6 copy.288
  1090.3 21.9 %fusion.86 = (f32[1536]{0:T(1024)S(1)}, f32[2,256]{1,0:T(2,128)S(1)}, f32[2,256,1536]{2,1,0:T(8,128)}) fusion(bf16[2,256,1536]{2,1,0:T(8,128)(2,1)S(1)} %copy-done.16, f32[2,256]{1,0:T(2,128)S(1)} %copy-done.72, f32[1536]{0:T(1024)S(1)} %copy-done.66, bf16[1536,6448]{1,0:T(8,128)(2,1)} %all-gather.10.cloned.1.call-done, ...), kind=kOutput, calls=%fused_computation.138 | convolution fusion | flops 10167138304 | bytes 31145984 | tf_op jit(solution)/shard_map/gtp,dp->gtd/dot_general | solution.py:372
  1112.3 5.2 pad_maximum_fusion.1
  1117.5 9.7 copy.374
  1127.2 6.2 pad.60.clone
  1133.3 9.9 copy.292
  1143.2 103.5 %rs.2 = f32[26,2,48,128]{3,2,1,0:T(8,128)} custom-call(bf16[1,2,768,512]{3,2,1,0:T(8,128)(2,1)} %bitcast.303, bf16[26,512,256]{2,1,0:T(8,128)(2,1)} %bitcast.290), custom_call_target="tpu_custom_call" | custom-call | tf_op jit(solution)/shard_map/rs/pallas_call | solution.py:236
  1249.8 5.5 fusion.87
  1255.4 2.6 multiply_subtract_fusion
  1258.0 38.8 %all-reduce.21 = (f32[1536]{0:T(1024)S(1)}, f32[3072]{0:T(1024)S(1)}, f32[3,48]{1,0:T(4,128)S(1)}) all-reduce(f32[1536]{0:T(1024)S(1)} %get-tuple-element.698, f32[3072]{0:T(1024)S(1)} %copy-done.78, f32[3,48]{1,0:T(4,128)S(1)} %add_add_fusion.2), channel_id=8, replica_groups=mesh['dp'=8,'seq'=4] {'dp','seq'}, use_global_device_ids=true, to_apply=%region_30.31.clone | all-reduce | flops 4752 | bytes 38016
  (361 shorter events, 85.2 us)
Async XLA Ops:
  7.2 134.4 %copy-start.14 = (bf16[2,256,1536]{2,1,0:T(8,128)(2,1)S(1)}, bf16[2,256,1536]{2,1,0:T(8,128)(2,1)}, u32[]{:S(2)}) copy-start(bf16[2,256,1536]{2,1,0:T(8,128)(2,1)} %param.28) | copy-start | bytes 4718596
  7.2 131.2 %all-reduce.25.cloned.1.call-start = ((), (), s32[]{:S(2)}) async-start(), calls=%async_computation.4 | async-start | bytes 172032
  9.7 263.6 %all-gather.10.cloned.1.call-start = ((), (), s32[]{:S(2)}) async-start(), calls=%async_computation | async-start | bytes 20680704 | tf_op jit(solution)/shard_map/all_gather | solution.py:300
  11.9 547.4 %all-gather.14.cloned.1.call-start = ((), (), s32[]{:S(2)}) async-start(), calls=%async_computation.2 | async-start | bytes 15728640 | tf_op jit(solution)/shard_map/all_gather | solution.py:38
  15.1 286.4 %copy-start.80 = (f32[48]{0:T(128)}, f32[48]{0:T(128)S(1)}, u32[]{:S(2)}) copy-start(f32[48]{0:T(128)S(1)} %get-tuple-element.829) | copy-start | bytes 580
  15.1 286.4 %copy-start.82 = (f32[48]{0:T(128)}, f32[48]{0:T(128)S(1)}, u32[]{:S(2)}) copy-start(f32[48]{0:T(128)S(1)} %get-tuple-element.830) | copy-start | bytes 580
  15.1 258.2 %copy-start.71 = (f32[2,256]{1,0:T(2,128)}, f32[2,256]{1,0:T(2,128)S(1)}, u32[]{:S(2)}) copy-start(f32[2,256]{1,0:T(2,128)S(1)} %fusion.129) | copy-start | bytes 6148
  139.6 133.7 %copy-start.65 = (f32[1536]{0:T(1024)}, f32[1536]{0:T(1024)S(1)}, u32[]{:S(2)}) copy-start(f32[1536]{0:T(1024)S(1)} %mul.699) | copy-start | bytes 18436
  140.0 173.7 %copy-start.58 = (f32[3328]{0:T(1024)}, f32[3328]{0:T(1024)S(1)}, u32[]{:S(2)}) copy-start(f32[3328]{0:T(1024)S(1)} %mul.709) | copy-start | bytes 39940
  140.1 173.7 %copy-start.60 = (f32[3328]{0:T(1024)}, f32[3328]{0:T(1024)S(1)}, u32[]{:S(2)}) copy-start(f32[3328]{0:T(1024)S(1)} %mul.706) | copy-start | bytes 39940
  140.2 173.6 %copy-start.62 = (f32[3328]{0:T(1024)}, f32[3328]{0:T(1024)S(1)}, u32[]{:S(2)}) copy-start(f32[3328]{0:T(1024)S(1)} %mul.703) | copy-start | bytes 39940
  142.0 148.9 %copy-start.28 = (bf16[2,256,1536]{2,1,0:T(8,128)(2,1)}, bf16[2,256,1536]{2,1,0:T(8,128)(2,1)S(1)}, u32[]{:S(2)}) copy-start(bf16[2,256,1536]{2,1,0:T(8,128)(2,1)S(1)} %fusion.85) | copy-start | bytes 4718596
  298.2 13.7 %collective-permute-start = (f32[2,3,3328]{2,0,1:T(2,128)S(1)}, f32[2,3,3328]{2,0,1:T(2,128)}, u32[]{:S(2)}, u32[]{:S(2)}) collective-permute-start(f32[2,3,3328]{2,0,1:T(2,128)S(1)} %copy.248), channel_id=1, source_target_pairs={{0,1},{1,2},{2,3},{4,5},{5,6},{6,7},{8,9},{9,10},{10,11},{12,13},{... | collective-permute-start | bytes 239624 | tf_op jit(solution)/shard_map/ppermute | solution.py:33
  311.8 19.6 %copy-start.40 = (f32[2,256,48]{1,2,0:T(8,128)}, f32[2,256,48]{1,2,0:T(8,128)S(1)}, u32[]{:S(2)}) copy-start(f32[2,256,48]{1,2,0:T(8,128)S(1)} %copy.259) | copy-start | bytes 294916
  313.8 17.2 %copy-start.10 = (f32[2,3,3328]{1,2,0:T(8,128)}, f32[2,3,3328]{1,2,0:T(8,128)S(1)}, u32[]{:S(2)}) copy-start(f32[2,3,3328]{1,2,0:T(8,128)S(1)} %copy.249) | copy-start | bytes 239620
  343.0 299.2 %all-gather.12.cloned.1.call-start = ((), (), s32[]{:S(2)}) async-start(), calls=%async_computation.1 | async-start | bytes 9732096 | tf_op jit(solution)/shard_map/all_gather | solution.py:301
  343.9 508.7 %all-gather.16.cloned.1.call-start = ((), (), s32[]{:S(2)}) async-start(), calls=%async_computation.3 | async-start | bytes 7864320 | tf_op jit(solution)/shard_map/all_gather | solution.py:52
  347.9 16.4 %copy-start.84 = (f32[2,1,48]{2,0,1:T(2,128)S(1)}, f32[2,1,48]{2,0,1:T(2,128)}, u32[]{:S(2)}) copy-start(f32[2,1,48]{2,0,1:T(2,128)} %get-tuple-element.824) | copy-start | bytes 1156
  421.0 138.4 %copy-start.23 = (f32[2,256,128]{2,1,0:T(8,128)}, f32[2,256,128]{2,1,0:T(8,128)S(1)}, u32[]{:S(2)}) copy-start(f32[2,256,128]{2,1,0:T(8,128)S(1)} %get-tuple-element.1190) | copy-start | bytes 786436
  421.0 138.4 %copy-start.30 = (f32[2,256,48]{1,2,0:T(8,128)}, f32[2,256,48]{1,2,0:T(8,128)S(1)}, u32[]{:S(2)}) copy-start(f32[2,256,48]{1,2,0:T(8,128)S(1)} %get-tuple-element.1194) | copy-start | bytes 294916
  571.6 83.6 %slice-start.1 = ((s8[6815744]{0:T(1024)(128)(4,1)}), s8[2621440]{0:T(1024)(128)(4,1)S(1)}, s32[]{:S(2)}) async-start(s8[6815744]{0:T(1024)(128)(4,1)} %bitcast.288), calls=%async_computation.7 | async-start | bytes 5242880
  642.3 13.0 slice-start.2
  642.3 13.0 copy-start.8
  655.2 15.2 %copy-start.38 = (f32[2,256,48]{1,2,0:T(8,128)S(1)}, f32[2,256,48]{1,2,0:T(8,128)}, u32[]{:S(2)}) copy-start(f32[2,256,48]{1,2,0:T(8,128)} %copy.257) | copy-start | bytes 294916
  676.6 397.6 %all-reduce.27.cloned.1.call-start = ((), (), s32[]{:S(2)}) async-start(), calls=%async_computation.5 | async-start | bytes 212992
  682.8 77.0 %copy-start.18 = (bf16[2,256,3072]{1,2,0:T(8,128)(2,1)S(1)}, bf16[2,256,3072]{1,2,0:T(8,128)(2,1)}, u32[]{:S(2)}) copy-start(bf16[2,256,3072]{1,2,0:T(8,128)(2,1)} %get-tuple-element.811) | copy-start | bytes 9437188
  699.6 18.9 %copy-start.13 = (f32[2,256,48,64]{1,3,2,0:T(8,128)}, f32[2,256,48,64]{1,3,2,0:T(8,128)S(1)}, u32[]{:S(2)}) copy-start(f32[2,256,48,64]{1,3,2,0:T(8,128)S(1)} %bitcast_dynamic-update-slice_fusion.8) | copy-start | bytes 18874372 | tf_op jit(solution)/shard_map/transpose(jvp())/while
  699.6 18.9 %copy-start.45 = (f32[2,256,128]{1,2,0:T(8,128)S(1)}, f32[2,256,128]{1,2,0:T(8,128)}, u32[]{:S(2)}) copy-start(f32[2,256,128]{1,2,0:T(8,128)} %get-tuple-element.1125) | copy-start | bytes 786436 | tf_op jit(solution)/shard_map/transpose(jvp())/while
  699.6 19.3 %copy-start.47 = (f32[2,256,128]{1,2,0:T(8,128)S(1)}, f32[2,256,128]{1,2,0:T(8,128)}, u32[]{:S(2)}) copy-start(f32[2,256,128]{1,2,0:T(8,128)} %get-tuple-element.1126) | copy-start | bytes 786436 | tf_op jit(solution)/shard_map/transpose(jvp())/while
  699.6 19.8 %copy-start.53 = (f32[2,256,48]{1,2,0:T(8,128)S(1)}, f32[2,256,48]{1,2,0:T(8,128)}, u32[]{:S(2)}) copy-start(f32[2,256,48]{1,2,0:T(8,128)} %get-tuple-element.1127) | copy-start | bytes 294916 | tf_op jit(solution)/shard_map/transpose(jvp())/while
  699.7 19.8 %copy-start.55 = (f32[2,256,48]{1,2,0:T(8,128)S(1)}, f32[2,256,48]{1,2,0:T(8,128)}, u32[]{:S(2)}) copy-start(f32[2,256,48]{1,2,0:T(8,128)} %get-tuple-element.1128) | copy-start | bytes 294916 | tf_op jit(solution)/shard_map/transpose(jvp())/while
  735.7 18.9 %copy-start.13 = (f32[2,256,48,64]{1,3,2,0:T(8,128)}, f32[2,256,48,64]{1,3,2,0:T(8,128)S(1)}, u32[]{:S(2)}) copy-start(f32[2,256,48,64]{1,3,2,0:T(8,128)S(1)} %bitcast_dynamic-update-slice_fusion.8) | copy-start | bytes 18874372 | tf_op jit(solution)/shard_map/transpose(jvp())/while
  735.7 18.9 %copy-start.45 = (f32[2,256,128]{1,2,0:T(8,128)S(1)}, f32[2,256,128]{1,2,0:T(8,128)}, u32[]{:S(2)}) copy-start(f32[2,256,128]{1,2,0:T(8,128)} %get-tuple-element.1125) | copy-start | bytes 786436 | tf_op jit(solution)/shard_map/transpose(jvp())/while
  735.8 19.3 %copy-start.47 = (f32[2,256,128]{1,2,0:T(8,128)S(1)}, f32[2,256,128]{1,2,0:T(8,128)}, u32[]{:S(2)}) copy-start(f32[2,256,128]{1,2,0:T(8,128)} %get-tuple-element.1126) | copy-start | bytes 786436 | tf_op jit(solution)/shard_map/transpose(jvp())/while
  735.8 19.8 %copy-start.53 = (f32[2,256,48]{1,2,0:T(8,128)S(1)}, f32[2,256,48]{1,2,0:T(8,128)}, u32[]{:S(2)}) copy-start(f32[2,256,48]{1,2,0:T(8,128)} %get-tuple-element.1127) | copy-start | bytes 294916 | tf_op jit(solution)/shard_map/transpose(jvp())/while
  735.8 19.8 %copy-start.55 = (f32[2,256,48]{1,2,0:T(8,128)S(1)}, f32[2,256,48]{1,2,0:T(8,128)}, u32[]{:S(2)}) copy-start(f32[2,256,48]{1,2,0:T(8,128)} %get-tuple-element.1128) | copy-start | bytes 294916 | tf_op jit(solution)/shard_map/transpose(jvp())/while
  770.7 60.0 %copy-start.67 = (f32[3072]{0:T(1024)S(1)}, f32[3072]{0:T(1024)}, u32[]{:S(2)}) copy-start(f32[3072]{0:T(1024)} %get-tuple-element.790) | copy-start | bytes 36868
  770.7 60.2 %copy-start.39 = (f32[2,256,48]{1,2,0:T(8,128)S(1)}, f32[2,256,48]{1,2,0:T(8,128)}, u32[]{:S(2)}) copy-start(f32[2,256,48]{1,2,0:T(8,128)} %copy.257) | copy-start | bytes 294916
  770.7 60.2 %copy-start.49 = (f32[2,256,128]{1,2,0:T(8,128)S(1)}, f32[2,256,128]{1,2,0:T(8,128)}, u32[]{:S(2)}) copy-start(f32[2,256,128]{1,2,0:T(8,128)} %get-tuple-element.521) | copy-start | bytes 786436
  828.7 12.5 copy-start.33
  828.7 12.5 copy-start.50
  828.7 12.5 copy-start.51
  852.6 20.2 %copy-start.3 = (f32[2,48,64,128]{3,2,1,0:T(8,128)S(1)}, f32[2,48,64,128]{3,2,1,0:T(8,128)}, u32[]{:S(2)}) copy-start(f32[2,48,64,128]{3,2,1,0:T(8,128)} %copy-done.2) | copy-start | bytes 9437188
  875.6 16.4 %copy-start.22 = (f32[2,48,2,128]{1,0,3,2:T(2,128)S(1)}, f32[2,48,2,128]{1,0,3,2:T(2,128)}, u32[]{:S(2)}) copy-start(f32[2,48,2,128]{1,0,3,2:T(2,128)} %copy-done.20) | copy-start | bytes 294916
  875.6 16.4 %copy-start.75 = (f32[2,48]{1,0:T(2,128)S(1)}, f32[2,48]{1,0:T(2,128)}, u32[]{:S(2)}) copy-start(f32[2,48]{1,0:T(2,128)} %copy-done.74) | copy-start | bytes 1156
  890.1 20.2 %copy-start.5 = (f32[2,48,64,128]{3,2,1,0:T(8,128)S(1)}, f32[2,48,64,128]{3,2,1,0:T(8,128)}, u32[]{:S(2)}) copy-start(f32[2,48,64,128]{3,2,1,0:T(8,128)} %get-tuple-element.523) | copy-start | bytes 9437188
  919.8 22.3 %copy-start.59 = (f32[3328]{0:T(1024)S(1)}, f32[3328]{0:T(1024)}, u32[]{:S(2)}) copy-start(f32[3328]{0:T(1024)} %copy-done.58) | copy-start | bytes 39940
  919.8 22.3 %copy-start.61 = (f32[3328]{0:T(1024)S(1)}, f32[3328]{0:T(1024)}, u32[]{:S(2)}) copy-start(f32[3328]{0:T(1024)} %copy-done.60) | copy-start | bytes 39940
  919.8 22.3 %copy-start.63 = (f32[3328]{0:T(1024)S(1)}, f32[3328]{0:T(1024)}, u32[]{:S(2)}) copy-start(f32[3328]{0:T(1024)} %copy-done.62) | copy-start | bytes 39940
  919.8 22.3 %copy-start.64 = (f32[3328]{0:T(1024)S(1)}, f32[3328]{0:T(1024)}, u32[]{:S(2)}) copy-start(f32[3328]{0:T(1024)} %mul.694) | copy-start | bytes 39940
  967.4 106.8 %copy-start.73 = (f32[5,104]{1,0:T(8,128)S(1)}, f32[5,104]{1,0:T(8,128)}, u32[]{:S(2)}) copy-start(f32[5,104]{1,0:T(8,128)} %param.36) | copy-start | bytes 6244
  967.4 106.8 %copy-start.85 = (f32[5,104]{1,0:T(8,128)S(1)}, f32[5,104]{1,0:T(8,128)}, u32[]{:S(2)}) copy-start(f32[5,104]{1,0:T(8,128)} %param.37) | copy-start | bytes 6244
  967.4 106.8 %copy-start.86 = (f32[5,104]{1,0:T(8,128)S(1)}, f32[5,104]{1,0:T(8,128)}, u32[]{:S(2)}) copy-start(f32[5,104]{1,0:T(8,128)} %param.38) | copy-start | bytes 6244
  975.8 99.8 %collective-permute-start.1 = (bf16[2,3,3328]{2,0,1:T(2,128)(2,1)S(1)}, bf16[2,3,3328]{2,0,1:T(2,128)(2,1)}, u32[]{:S(2)}, u32[]{:S(2)}) collective-permute-start(bf16[2,3,3328]{2,0,1:T(2,128)(2,1)S(1)} %copy.277), channel_id=1, source_target_pairs={{1,0},{2,1},{3,2},{5,4},{6,5},{7,6},{9,8},{10,9},{11,10},{13,12},{... | collective-permute-start | bytes 119816 | tf_op jit(solution)/shard_map/ppermute | solution.py:33
  1090.3 22.0 %copy-start.70 = (f32[2,256]{1,0:T(2,128)S(1)}, f32[2,256]{1,0:T(2,128)}, u32[]{:S(2)}) copy-start(f32[2,256]{1,0:T(2,128)} %copy-done.69) | copy-start | bytes 6148
  1090.3 22.0 %copy-start.17 = (bf16[2,256,3328]{2,1,0:T(8,128)(2,1)S(1)}, bf16[2,256,3328]{2,1,0:T(8,128)(2,1)}, u32[]{:S(2)}) copy-start(bf16[2,256,3328]{2,1,0:T(8,128)(2,1)} %copy.288) | copy-start | bytes 10223620
  1255.3 41.4 %copy-start.87 = (f32[3,48]{1,0:T(4,128)S(1)}, f32[3,48]{1,0:T(4,128)}, u32[]{:S(2)}) copy-start(f32[3,48]{1,0:T(4,128)} %param.46) | copy-start | bytes 1732
  1255.3 41.4 %copy-start.88 = (f32[3,48]{1,0:T(4,128)S(1)}, f32[3,48]{1,0:T(4,128)}, u32[]{:S(2)}) copy-start(f32[3,48]{1,0:T(4,128)} %param.47) | copy-start | bytes 1732
  1255.4 42.0 %copy-start.90 = (f32[48]{0:T(128)S(1)}, f32[48]{0:T(128)}, u32[]{:S(2)}) copy-start(f32[48]{0:T(128)} %param.39) | copy-start | bytes 580
  1255.4 42.0 %copy-start.92 = (f32[48]{0:T(128)S(1)}, f32[48]{0:T(128)}, u32[]{:S(2)}) copy-start(f32[48]{0:T(128)} %param.40) | copy-start | bytes 580
  1255.4 42.0 %copy-start.93 = (f32[48]{0:T(128)S(1)}, f32[48]{0:T(128)}, u32[]{:S(2)}) copy-start(f32[48]{0:T(128)} %param.41) | copy-start | bytes 580
  1255.4 42.6 %copy-start.91 = (f32[96]{0:T(128)S(1)}, f32[96]{0:T(128)}, u32[]{:S(2)}) copy-start(f32[96]{0:T(128)} %param.42) | copy-start | bytes 1156
  1255.4 42.6 %copy-start.94 = (f32[96]{0:T(128)S(1)}, f32[96]{0:T(128)}, u32[]{:S(2)}) copy-start(f32[96]{0:T(128)} %param.43) | copy-start | bytes 1156
  1255.4 42.6 %copy-start.95 = (f32[96]{0:T(128)S(1)}, f32[96]{0:T(128)}, u32[]{:S(2)}) copy-start(f32[96]{0:T(128)} %param.44) | copy-start | bytes 1156
  (56 other events, 327.6 us)
Sparse Core Ops, SparseCore 0:
  14.2 124.1 all-reduce.24
  141.8 131.4 all-gather.9
  343.2 216.1 all-gather.13
  562.6 79.6 all-gather.11
  676.7 113.8 all-gather.15
  952.8 121.3 all-reduce.26

commit v2 on v0

--- a/solution.py
+++ b/solution.py
@@ -1,7 +1,15 @@
+import functools
+
 import jax
 import jax.numpy as jnp
 from jax import lax
+from jax.experimental import pallas as pl
+from jax.experimental.pallas import tpu as pltpu
 from jax.sharding import PartitionSpec as P
+
+MESH = pl.DeviceIdType.MESH
+bf = jnp.bfloat16
+f32 = jnp.float32
 
 DI = 3072
 HEADS = 48
@@ -265,6 +273,1013 @@
     )
 
 
+class Place:
+    def __init__(self):
+        self.dp = dp = lax.axis_index("dp")
+        self.z = lax.axis_index("seq")
+        self.c = c = lax.rem(dp, 2)
+        self.x = x = lax.rem(dp // 2, 2)
+        self.y = y = dp // 4
+        self.line = dp * 4 + self.z
+        self.core_peer = {"dp": dp + 1 - 2 * c}
+        self.x_peer = {"dp": dp + 2 - 4 * x}
+        self.y_peer = {"dp": dp + 4 - 8 * y}
+
+    def z_peer(self, k):
+        return {"seq": lax.rem(self.z + k, 4)}
+
+    def any_peer(self, k):
+        at = lax.rem(self.line + k, 32)
+        return {"dp": at // 4, "seq": lax.rem(at, 4)}
+
+    def near(self):
+        return (self.core_peer, self.x_peer, self.y_peer, self.z_peer(1), self.z_peer(2), self.z_peer(3))
+
+
+def greet(peers):
+    bar = pltpu.get_barrier_semaphore()
+    for peer in peers:
+        pl.semaphore_signal(bar, inc=1, device_id=peer, device_id_type=MESH)
+    pl.semaphore_wait(bar, len(peers))
+
+
+def send(src, dst, out_sem, in_sem, peer):
+    return pltpu.make_async_remote_copy(
+        src_ref=src, dst_ref=dst, send_sem=out_sem, recv_sem=in_sem, device_id=peer, device_id_type=MESH
+    )
+
+
+class Gather:
+    def __init__(self, me, n, src, w, sems, skew):
+        self.me, self.n, self.src, self.w, self.sk, self.slots = me, n, src, w, skew, skew + 1
+        self.rows = src.shape[2]
+        self.o1, self.o2, self.o3, self.o4, self.i1, self.i2, self.i3, self.i4 = sems
+
+    @staticmethod
+    def sems(n, skew):
+        D = pltpu.SemaphoreType.DMA
+        return [D((skew + 1, 3)), D((skew + 1, 2)), D((skew + 1, 2)), D((skew + 1,)), D((n, 3)), D((n, 2)), D((n, 2)), D((n,))]
+
+    def c1(self, i, s, k):
+        m, w = self.me, self.w
+        rows = pl.ds(pl.multiple_of(m.z * self.rows, 16), self.rows)
+        return send(self.src.at[i], w.at[i, :, m.y, m.x, m.c, rows], self.o1.at[s, k - 1], self.i1.at[i, k - 1], m.z_peer(k))
+
+    def c2(self, i, s, h):
+        m, w = self.me, self.w
+        part = w.at[i, h, m.y, m.x, m.c]
+        return send(part, part, self.o2.at[s, h], self.i2.at[i, h], (m.y_peer, m.x_peer)[h])
+
+    def c3(self, i, s, h):
+        m, w = self.me, self.w
+        part = w.at[i, 0, :, m.x, m.c] if h == 0 else w.at[i, 1, m.y, :, m.c]
+        return send(part, part, self.o3.at[s, h], self.i3.at[i, h], (m.x_peer, m.y_peer)[h])
+
+    def c4(self, i, s):
+        m, w = self.me, self.w
+        part = w.at[i, :, :, :, m.c]
+        return send(part, part, self.o4.at[s], self.i4.at[i], m.core_peer)
+
+    def step(self, it):
+        n, sk, ns = self.n, self.sk, self.slots
+
+        def stage(lag, body):
+            @pl.when((it >= lag * sk) & (it < n + lag * sk))
+            def _():
+                i = it - lag * sk
+                body(i, lax.rem(i, ns))
+
+        def first(i, s):
+            m = self.me
+            @pl.when(i >= ns)
+            def _():
+                for k in (1, 2, 3): self.c1(i, s, k).wait_send()
+            for k in (2, 1, 3): self.c1(i, s, k).start()
+            rows = pl.ds(pl.multiple_of(m.z * self.rows, 16), self.rows)
+            for h in range(2):
+                self.w[i, h, m.y, m.x, m.c, rows] = self.src[i, h]
+
+        def second(i, s):
+            @pl.when(i >= ns)
+            def _():
+                for h in range(2): self.c2(i, s, h).wait_send()
+            for k in (1, 2, 3): self.c1(i, s, k).wait_recv()
+            for h in range(2): self.c2(i, s, h).start()
+
+        def third(i, s):
+            @pl.when(i >= ns)
+            def _():
+                for h in range(2): self.c3(i, s, h).wait_send()
+            for h in range(2):
+                self.c2(i, s, h).wait_recv()
+                self.c3(i, s, h).start()
+
+        def fourth(i, s):
+            @pl.when(i >= ns)
+            def _(): self.c4(i, s).wait_send()
+            for h in range(2): self.c3(i, s, h).wait_recv()
+            self.c4(i, s).start()
+
+        stage(0, first); stage(1, second); stage(2, third); stage(3, fourth)
+
+    def arrived(self, i):
+        self.c4(i, 0).wait_recv()
+
+    def finish(self):
+        for j in range(self.slots):
+            i = self.n - self.slots + j
+            s = i % self.slots
+            for k in (1, 2, 3): self.c1(i, s, k).wait_send()
+            for h in range(2):
+                self.c2(i, s, h).wait_send()
+                self.c3(i, s, h).wait_send()
+            self.c4(i, s).wait_send()
+
+
+def windows(width, count):
+    return [(o * width // 128) * 128 for o in range(count)]
+
+
+def gather_call(src_in, src_out, small, tokens, edge, cotangent, collective_id, skew=2):
+    NI, NO = src_in.shape[0], src_out.shape[0]
+    T, DM = tokens.shape
+    TE = T + 16
+    DIN = 2 * 16 * 96
+
+    def kernel(src_in, src_out, small_ref, tok_ref, edge_ref, cot_ref,
+               proj_hbm, win_hbm, wout_hbm, low_ref, par_ref, dn_ref,
+               win, wout, sm, low_e, edge_in, pbuf,
+               *sems):
+        gs, os_, (sm_out, sm_in, ed_out, ed_in, pb_sem, wi_sem, wo_sem) = sems[:8], sems[8:16], sems[16:]
+        me = Place()
+        bar = pltpu.get_barrier_semaphore()
+        def sig(k, _):
+            pl.semaphore_signal(bar, inc=1, device_id=me.any_peer(k), device_id_type=MESH)
+            return 0
+        lax.fori_loop(1, 32, sig, 0)
+        pl.semaphore_wait(bar, 31)
+        ga = Gather(me, NI, src_in, win, gs, skew)
+        gb = Gather(me, NO, src_out, wout, os_, skew)
+
+        def small_copy(k):
+            return send(small_ref, sm.at[me.line], sm_out.at[k - 1], sm_in.at[k - 1], me.any_peer(k))
+        def edge_copy():
+            return send(edge_ref, edge_in, ed_out, ed_in, {"seq": lax.rem(me.z + 1, 4)})
+        lax.fori_loop(1, 32, lambda k, _: (small_copy(k).start(), 0)[1], 0)
+        edge_copy().start()
+        sm[me.line] = small_ref[...]
+        ga.step(0); ga.step(1)
+        lax.fori_loop(1, 32, lambda k, _: (small_copy(k).wait(), 0)[1], 0)
+        edge_copy().wait()
+        par_ref[...] = jnp.zeros_like(par_ref)
+        for o in range(32):
+            for base, width, row, lo in ((0, 104, 5, 0), (3328, 48, 1, 5), (4864, 96, 1, 6)):
+                at = base + (o * width // 128) * 128
+                wd = min(256, {0: 3328, 3328: 4864, 4864: 7936}[base] - at)
+                par_ref[:, at:at + wd] += sm[o][:, :wd]
+        gain = par_ref[5:6, 3328:4864]
+        keep = (me.z > 0).astype(f32)
+
+        def norm(v):
+            v = v.astype(f32)
+            return (v * lax.rsqrt(jnp.mean(v * v, axis=-1, keepdims=True) + 1e-5) * gain).astype(bf)
+        def nloop(t, _):
+            r = pl.ds(pl.multiple_of(t * 64, 64), 64)
+            v = norm(tok_ref[r])
+            low_ref[r] = v
+            low_e[r] = v
+            return 0
+        lax.fori_loop(0, T // 64, nloop, 0)
+        low_e[T:] = norm(edge_in[...].astype(f32) * keep)
+
+        def pcopy(i, s): return pltpu.make_async_copy(pbuf.at[s], proj_hbm.at[i], pb_sem.at[s])
+        def wicopy(i): return pltpu.make_async_copy(win.at[i], win_hbm.at[i], wi_sem.at[i])
+        def wocopy(i): return pltpu.make_async_copy(wout.at[i], wout_hbm.at[i], wo_sem.at[i])
+
+        def loop(it, _):
+            @pl.when(it >= 2)
+            def _(): ga.step(it)
+            gb.step(it - NI)
+            @pl.when((it >= 4 * skew) & (it < NI + 4 * skew))
+            def _():
+                i = it - 4 * skew; s = lax.rem(i, 2)
+                ga.arrived(i)
+                wicopy(i).start()
+                @pl.when(i >= 2)
+                def _(): pcopy(i - 2, s).wait()
+                w = jnp.concatenate([win[i, h].reshape(DM, 128) for h in range(2)], axis=1)
+                pbuf[s] = jnp.dot(low_e[...], w, preferred_element_type=f32)
+                pcopy(i, s).start()
+            @pl.when(it >= NI + 4 * skew)
+            def _():
+                i = it - 4 * skew - NI
+                gb.arrived(i)
+                wocopy(i).start()
+                for h in range(2):
+                    a = cot_ref[:, pl.ds(pl.multiple_of(i * 256 + h * 128, 128), 128)]
+                    def cols(q, _):
+                        y = q // 4; x = lax.rem(q // 2, 2); c = lax.rem(q, 2)
+                        r = lax.dot_general(a, wout[i, h, y, x, c], (((1,), (1,)), ((), ())), preferred_element_type=f32)
+                        if h == 0:
+                            @pl.when(i == 0)
+                            def _(): dn_ref[q] = r
+                            @pl.when(i > 0)
+                            def _(): dn_ref[q] += r
+                        else:
+                            dn_ref[q] += r
+                        return 0
+                    lax.fori_loop(0, 8, cols, 0)
+            return 0
+        lax.fori_loop(0, NI + NO + 4 * skew, loop, 0)
+        pcopy(NI - 2, NI % 2).wait()
+        pcopy(NI - 1, (NI - 1) % 2).wait()
+        lax.fori_loop(0, NI, lambda i, _: (wicopy(i).wait(), 0)[1], 0)
+        lax.fori_loop(0, NO, lambda i, _: (wocopy(i).wait(), 0)[1], 0)
+        ga.finish()
+        gb.finish()
+
+    V, D = pltpu.VMEM, pltpu.SemaphoreType.DMA
+    S = jax.ShapeDtypeStruct
+    vm, hb = pl.BlockSpec(memory_space=pltpu.VMEM), pl.BlockSpec(memory_space=pl.ANY)
+    wi, wo = (NI, 2, 2, 2, 2, 192, 128), (NO, 2, 2, 2, 2, 384, 128)
+    return pl.pallas_call(
+        kernel,
+        out_shape=(S((NI, TE, 256), f32), S(wi, bf), S(wo, bf), S((T, DM), bf), S((8, 7936), f32), S((8, T, 384), f32)),
+        in_specs=[vm] * 6,
+        out_specs=(hb, hb, hb, vm, vm, vm),
+        scratch_shapes=[V(wi, bf), V(wo, bf), V((32, 8, 256), f32), V((TE, DM), bf), V((16, DM), bf), V((2, TE, 256), f32)]
+        + Gather.sems(NI, skew) + Gather.sems(NO, skew)
+        + [D((31,)), D((31,)), D, D, D((2,)), D((NI,)), D((NO,))],
+        compiler_params=pltpu.CompilerParams(collective_id=collective_id, has_side_effects=True, vmem_limit_bytes=63 << 20),
+        name="gather",
+    )(src_in, src_out, small, tokens, edge, cotangent)
+
+
+def arrange(in_proj, out_proj, conv_params, norm_gain, gate_gain, line):
+    w = in_proj.astype(bf)
+    w = jnp.concatenate([w[:, 3072:], jnp.zeros((48, 208), bf), w[:, :3072]], axis=1)
+    src_in = w.reshape(48, 26, 2, 128).transpose(1, 2, 0, 3)
+    src_out = out_proj.astype(bf).reshape(96, 6, 2, 128).transpose(1, 2, 0, 3)
+    small = jnp.zeros((8, 256), f32)
+    for rows, row, width in ((conv_params, 0, 104), (norm_gain[None], 5, 48), (gate_gain[None], 6, 96)):
+        small = lax.dynamic_update_slice(small, rows, (row, lax.rem(line * width, 128)))
+    return src_in, src_out, small
+
+
+PAIRS = 24
+NN, NT, TN_ = (((1,), (0,)), ((), ())), (((1,), (1,)), ((), ())), (((0,), (0,)), ((), ()))
+PASSES = 3
+
+
+def one(a, b, dims):
+    return lax.dot_general(a, b, dims, preferred_element_type=f32)
+
+
+def halves(a):
+    hi = a.astype(bf)
+    return hi, (a - hi.astype(f32)).astype(bf)
+
+
+def mul(a, b, dims=NN):
+    if PASSES == 1:
+        return one(a.astype(bf), b.astype(bf), dims)
+    ah, al = halves(a)
+    bh, bl = halves(b)
+    return one(ah, bh, dims) + (one(ah, bl, dims) + one(al, bh, dims))
+
+
+def mul_exact(a, b, dims=NN, left=True):
+    v = b if left else a
+    h = v.astype(bf)
+    r = v - h.astype(f32)
+    m = r.astype(bf)
+    l = (r - m.astype(f32)).astype(bf)
+    if left:
+        a = a.astype(bf)
+        return one(a, h, dims) + (one(a, m, dims) + one(a, l, dims))
+    b = b.astype(bf)
+    return one(h, b, dims) + (one(m, b, dims) + one(l, b, dims))
+
+
+def to_heads(a, spot):
+    h, l = halves(a)
+    return one(h, spot, NN) + one(l, spot, NN)
+
+
+def rolled(a, j):
+    return pltpu.roll(a, lax.rem(128 - 2 * j, 128), 1)
+
+
+def spread(r):
+    lane = lax.broadcasted_iota(jnp.int32, (r.shape[0], 128), 1)
+    return jnp.where(lane < 64, r[:, 0:1], r[:, 1:2])
+
+
+def masks(rows):
+    lane = lax.broadcasted_iota(jnp.int32, (rows, 128), 1)
+    return (lane < 64).astype(f32), (lane >= 64).astype(f32)
+
+
+def spot_of(j):
+    p = lax.broadcasted_iota(jnp.int32, (128, 128), 0)
+    lane = lax.broadcasted_iota(jnp.int32, (128, 128), 1)
+    return (lane == 2 * j + p // 64).astype(bf)
+
+
+def fill_pad(pad, cin, halo):
+    for g in range(2):
+        pad[g, 5:8] = halo[8 * g:8 * g + 3]
+        pad[g, 8:264] = cin[256 * g:256 * g + 256]
+
+
+def conv(pad, taps):
+    out = []
+    for g in range(2):
+        acc = taps[4:5]
+        for k in range(4):
+            acc = acc + taps[k:k + 1] * pad[g, 5 + k:261 + k]
+        out.append(acc)
+    return out
+
+
+def sig(v):
+    return 1.0 / (1.0 + jnp.exp(-v))
+
+
+def causal(flip):
+    r = lax.broadcasted_iota(jnp.int32, (128, 128), 0)
+    c = lax.broadcasted_iota(jnp.int32, (128, 128), 1)
+    return (r <= c) if flip else (c <= r)
+
+
+class Chain:
+    def __init__(self, me, by, got, part, out, out_sem, in_sem, keep):
+        self.me, self.by, self.got, self.part, self.out, self.out_sem, self.in_sem, self.keep = me, by, got, part, out, out_sem, in_sem, keep
+        self.place = me.z if by == 1 else 3 - me.z
+
+    def copy(self, i):
+        s = lax.rem(i, 3)
+        return send(self.out.at[s], self.got.at[i], self.out_sem.at[s], self.in_sem.at[i], self.me.z_peer(1 if self.by == 1 else 3))
+
+    def tile(self, i):
+        @pl.when(self.place > 0)
+        def _(): self.copy(i).wait_recv()
+
+        @pl.when(self.place < 3)
+        def _():
+            @pl.when(i >= 3)
+            def _(): self.copy(i - 3).wait_send()
+            s = lax.rem(i, 3)
+            for g in range(2):
+                self.out[s, g] = (self.keep(i, g) * self.got[i, g].astype(f32) + self.part[i, g]).astype(bf)
+            self.copy(i).start()
+
+    def start(self):
+        @pl.when(self.place == 0)
+        def _(): self.got[...] = jnp.zeros_like(self.got)
+
+    def step(self, j):
+        lag = 2 * self.place
+        @pl.when(j >= lag)
+        def _(): self.tile(j - lag)
+
+        @pl.when(j == PAIRS - 1)
+        def _():
+            lax.fori_loop(PAIRS - lag, PAIRS, lambda i, _: (self.tile(i), 0)[1], 0)
+            @pl.when(self.place < 3)
+            def _():
+                for i in range(PAIRS - 3, PAIRS): self.copy(i).wait_send()
+
+    @staticmethod
+    def scratch():
+        D = pltpu.SemaphoreType.DMA
+        return [V((PAIRS, 2, 128, 128), bf), V((PAIRS, 2, 128, 128), f32), V((3, 2, 128, 128), bf), D((3,)), D((PAIRS,))]
+
+
+def keeper(ds):
+    def keep(i, g):
+        end = 256 * g + 248
+        return jnp.exp(spread(rolled(ds[end:end + 8], i))[7:8])
+    return keep
+
+
+V = pltpu.VMEM
+
+
+def sf1_body(j, cin, halo, bcin, bchalo, raw, taps, bctaps, hp, x_o, yi_o, ent_o, step_o, ds_o, dst_o, b_o, c_o, pad, pad2, s_s, bt_s, got, part, out, out_sem, in_sem):
+    me = Place()
+    line = Chain(me, 1, got, part, out, out_sem, in_sem, keeper(ds_o))
+    @pl.when(j == 0)
+    def _():
+        greet((me.z_peer(1), me.z_peer(3)))
+        line.start()
+        pre = raw[0] + hp[2:3]
+        step = jnp.maximum(pre, 0.0) + jnp.log1p(jnp.exp(-jnp.abs(pre)))
+        rate = step * -jnp.exp(hp[0:1])
+        step_o[...] = step
+        r = lax.broadcasted_iota(jnp.int32, (256, 256), 0)
+        c = lax.broadcasted_iota(jnp.int32, (256, 256), 1)
+        low = (c <= r).astype(bf)
+        for g in range(2):
+            ds_o[256 * g:256 * g + 256] = mul_exact(low, rate[256 * g:256 * g + 256])
+        turned = ds_o[...].T
+        for p in range(PAIRS):
+            dst_o[p, 0:2] = turned[2 * p:2 * p + 2]
+        fill_pad(pad2, bcin[0], bchalo[0])
+        for g, co in enumerate(conv(pad2, bctaps)):
+            act = co * sig(co)
+            b, c = act[:, :128], act[:, 128:]
+            b_o[256 * g:256 * g + 256] = b
+            c_o[256 * g:256 * g + 256] = c
+            bt_s[g] = b.T
+            s_s[g, 0] = mul(c[:128], b[:128], NT)
+            s_s[g, 1] = mul(c[128:], b[128:], NT)
+            s_s[g, 2] = mul(c[128:], b[:128], NT)
+
+    fill_pad(pad, cin[0], halo[0])
+    rds = rolled(ds_o[...], j)
+    dsc = spread(rds)
+    stc = spread(rolled(step_o[...], j))
+    m0, m1 = masks(128)
+    ok = causal(False)
+    for g, co in enumerate(conv(pad, taps)):
+        b0 = 256 * g
+        x = co * sig(co)
+        x_o[b0:b0 + 256] = x
+        xs = x * stc[b0:b0 + 256]
+        d = dsc[b0:b0 + 256]
+        ys = []
+        for q in range(2):
+            b = b0 + 128 * q
+            w = []
+            for h in range(2):
+                gap = rds[b:b + 128, h:h + 1] - dst_o[j, h:h + 1, b:b + 128]
+                w.append(s_s[g, q] * jnp.exp(jnp.where(ok, gap, -1e30)))
+            xq = xs[128 * q:128 * q + 128]
+            ys.append(mul(jnp.concatenate(w, 1), jnp.concatenate([xq * m0, xq * m1], 0)))
+        mid = d[127:128]
+        ys[1] = ys[1] + jnp.exp(d[128:] - mid) * mul(s_s[g, 2], jnp.exp(mid - d[:128]) * xs[:128])
+        yi_o[b0:b0 + 128] = ys[0]
+        yi_o[b0 + 128:b0 + 256] = ys[1]
+        part[j, g] = mul(bt_s[g], jnp.exp(d[255:256] - d) * xs)
+    line.step(j)
+
+    @pl.when(j == PAIRS - 1)
+    def _(): ent_o[...] = got[...]
+
+
+def sf2_body(j, yi, x, ent, z, dn, gain, ds, c_r, hp, mixed_o, rq_o, a1, a2):
+    @pl.when(j == 0)
+    def _():
+        a1[...] = jnp.zeros_like(a1)
+        a2[...] = jnp.zeros_like(a2)
+    dsc = spread(rolled(ds[...], j))
+    skip = spread(rolled(hp[...], j))[1:2]
+    for g in range(2):
+        r = slice(256 * g, 256 * g + 256)
+        car = jnp.exp(dsc[r]) * mul(c_r[r], ent[0, g].astype(f32))
+        mixed = yi[r] + car + skip * x[r]
+        mixed_o[r] = mixed
+        zz = z[0, r]
+        gated = mixed * (zz * sig(zz))
+        a1[r] += gated * gated
+        a2[r] += gain[6:7] * dn[0, r] * gated
+
+    @pl.when(j == PAIRS - 1)
+    def _():
+        r = lax.rsqrt(jnp.sum(a1[...], axis=1, keepdims=True) * (1.0 / 3072) + 1e-5)
+        k = r * r * r * (jnp.sum(a2[...], axis=1, keepdims=True) * (1.0 / 3072))
+        rq_o[0] = jnp.broadcast_to(r, (512, 128))
+        rq_o[1] = jnp.broadcast_to(k, (512, 128))
+
+
+def sb1_body(j, mixed, z, dn, x, ent, gain, ds, step, dst, b_r, c_r, hp, rq,
+             dxa_o, dz_o, ol_o, std_o, rows_o, dst_acc, dc_acc, dds_acc, xu_acc, st_s, ct_s, got, part, out, out_sem, in_sem):
+    me = Place()
+    line = Chain(me, -1, got, part, out, out_sem, in_sem, keeper(ds))
+    @pl.when(j == 0)
+    def _():
+        greet((me.z_peer(1), me.z_peer(3)))
+        line.start()
+        for a in (dst_acc, dc_acc, dds_acc, xu_acc):
+            a[...] = jnp.zeros_like(a)
+        for g in range(2):
+            b, c = b_r[256 * g:256 * g + 256], c_r[256 * g:256 * g + 256]
+            st_s[g, 0] = mul(b[:128], c[:128], NT)
+            st_s[g, 1] = mul(b[128:], c[128:], NT)
+            st_s[g, 2] = mul(b[:128], c[128:], NT)
+            ct_s[g] = c.T
+    rds = rolled(ds[...], j)
+    dsc = spread(rds)
+    stc = spread(rolled(step[...], j))
+    skip = spread(rolled(hp[...], j))[1:2]
+    m0, m1 = masks(128)
+    ok = causal(True)
+    spot = spot_of(j)
+    dgain = jnp.zeros((1, 128), f32)
+    dskip = jnp.zeros((1, 128), f32)
+    for g in range(2):
+        r = slice(256 * g, 256 * g + 256)
+        zz, mx, xx = z[0, r], mixed[r], x[r]
+        s = sig(zz)
+        sil = zz * s
+        gated = mx * sil
+        rr, kk = rq[0, r], rq[1, r]
+        gr = gated * rr
+        ol_o[r] = (gr * gain[6:7]).astype(bf)
+        dgain += jnp.sum(dn[0, r] * gr, axis=0, keepdims=True)
+        dg = rr * (gain[6:7] * dn[0, r]) - gated * kk
+        dy = dg * sil
+        dz_o[0, r] = (dg * mx * (s * (1.0 + zz * (1.0 - s)))).astype(bf)
+        dskip += jnp.sum(dy * xx, axis=0, keepdims=True)
+        d = dsc[r]
+        eu = jnp.exp(d) * dy
+        part[j, g] = mul(ct_s[g], eu)
+        dc_acc[r] += mul(eu, ent[0, g].astype(f32), NT)
+        dds_acc[r] += to_heads(dy * (mx - skip * xx), spot)
+        xs = xx * stc[r]
+        us = []
+        for q in range(2):
+            b = 256 * g + 128 * q
+            e = []
+            for h in range(2):
+                gap = dst[j, h:h + 1, b:b + 128] - rds[b:b + 128, h:h + 1]
+                e.append(jnp.exp(jnp.where(ok, gap, -1e30)))
+            w = jnp.concatenate([st_s[g, q] * e[0], st_s[g, q] * e[1]], 1)
+            lo = slice(128 * q, 128 * q + 128)
+            dq, xq = dy[lo], xs[lo]
+            us.append(mul(w, jnp.concatenate([dq * m0, dq * m1], 0)))
+            gt = mul(jnp.concatenate([xq * m0, xq * m1], 0), dq, NT)
+            dst_acc[g, q] += gt[:128] * e[0] + gt[128:] * e[1]
+        mid = d[127:128]
+        v = jnp.exp(mid - d[:128])
+        ud = jnp.exp(d[128:] - mid) * dy[128:]
+        us[0] = us[0] + v * mul(st_s[g, 2], ud)
+        dst_acc[g, 2] += mul(v * xs[:128], ud, NT)
+        u = jnp.concatenate(us, 0)
+        xu_acc[r] += to_heads(xx * u, spot)
+        dxa_o[r] = skip * dy + stc[r] * u
+    rows_o[0, 0:1] = dgain
+    rows_o[0, 1:2] = dskip
+    rows_o[0, 2:8] = jnp.zeros((6, 128), f32)
+    line.step(j)
+
+    @pl.when(j == PAIRS - 1)
+    def _(): std_o[...] = got[...]
+
+
+def conv_back(pad, dpad, dco, taps):
+    w = taps.shape[1]
+    grads = []
+    for k in range(4):
+        grads.append(sum(jnp.sum(dco[g] * pad[g, 5 + k:261 + k], axis=0, keepdims=True) for g in range(2)))
+    grads.append(sum(jnp.sum(dco[g], axis=0, keepdims=True) for g in range(2)))
+    grads.append(jnp.zeros((3, w), f32))
+    din, prev = [], []
+    for g in range(2):
+        dpad[g, 0:8] = jnp.zeros((8, w), f32)
+        dpad[g, 8:264] = dco[g]
+        dpad[g, 264:272] = jnp.zeros((8, w), f32)
+        din.append(sum(taps[k:k + 1] * dpad[g, 11 - k:267 - k] for k in range(4)))
+        prev.append(sum(taps[k:k + 1] * dpad[g, 3 - k:11 - k] for k in range(4)))
+    return jnp.concatenate(grads, 0), din, prev
+
+
+def sb2_body(j, dxa, x, cin, halo, taps, std, ent, bcin, bchalo, bctaps, raw, ds, step, b_r, c_r, hp, dst_acc, dc_acc, dds_acc, xu_acc,
+             dcp_o, cg_o, hg_o, pad, pad2, dpad, dpad2, db_s, xut_s, de_s, prv, lst, got, out_sem, in_sem):
+    me = Place()
+
+    def edge(i):
+        return send(prv.at[i], got.at[i], out_sem.at[i], in_sem.at[i], me.z_peer(3))
+
+    def pass_edge(i, prev, din):
+        for g in range(2):
+            lst[i, 8 * g:8 * g + 8] = din[g][248:]
+        prv[i] = jnp.concatenate(prev, 0).astype(bf)
+
+        @pl.when(me.z > 0)
+        def _(): edge(i).start()
+
+    @pl.when(j == 0)
+    def _():
+        greet((me.z_peer(1), me.z_peer(3)))
+        for a in (db_s, xut_s, de_s):
+            a[...] = jnp.zeros_like(a)
+    dsc = spread(rolled(ds[...], j))
+    stc = spread(rolled(step[...], j))
+    spot = spot_of(j)
+    fill_pad(pad, cin[0], halo[0])
+    dco = []
+    for g, co in enumerate(conv(pad, taps)):
+        r = slice(256 * g, 256 * g + 256)
+        d, xx, st, e = dsc[r], x[r], std[0, g].astype(f32), ent[0, g].astype(f32)
+        tail = jnp.exp(d[255:256] - d)
+        ut = tail * mul(b_r[r], st)
+        xut_s[r] += to_heads(xx * ut, spot)
+        db_s[r] += mul(tail * stc[r] * xx, st, NT)
+        row = jnp.sum(st * e, axis=0, keepdims=True)
+        de_s[g] += to_heads(jnp.broadcast_to(row, (8, 128)), spot)
+        dx = dxa[r] + stc[r] * ut
+        s = sig(co)
+        dco.append(dx * (s * (1.0 + co * (1.0 - s))))
+    grads, din, prev = conv_back(pad, dpad, dco, taps)
+    cg_o[j] = grads
+    p = j // 2
+    cols = pl.ds(pl.multiple_of(lax.rem(j, 2) * 128, 128), 128)
+    for g in range(2):
+        dcp_o[p, 256 * g:256 * g + 256, cols] = din[g].astype(bf)
+    pass_edge(j, prev, din)
+
+    @pl.when(j == PAIRS - 1)
+    def _():
+        fill_pad(pad2, bcin[0], bchalo[0])
+        dco2 = []
+        for g, co in enumerate(conv(pad2, bctaps)):
+            r0 = 256 * g
+            b, c = b_r[r0:r0 + 256], c_r[r0:r0 + 256]
+            db, dc = db_s[r0:r0 + 256], dc_acc[r0:r0 + 256]
+            db = db + jnp.concatenate([mul(dst_acc[g, 0], c[:128]) + mul(dst_acc[g, 2], c[128:]), mul(dst_acc[g, 1], c[128:])], 0)
+            dc = dc + jnp.concatenate([mul(dst_acc[g, 0].T, b[:128]), mul(dst_acc[g, 1].T, b[128:]) + mul(dst_acc[g, 2].T, b[:128])], 0)
+            s = sig(co)
+            dco2.append(jnp.concatenate([db, dc], 1) * (s * (1.0 + co * (1.0 - s))))
+        grads, din, prev = conv_back(pad2, dpad2, dco2, bctaps)
+        cg_o[24] = grads[:, :128]
+        cg_o[25] = grads[:, 128:]
+        for g in range(2):
+            dcp_o[12, 256 * g:256 * g + 256] = din[g].astype(bf)
+        for h in range(2):
+            lanes = slice(128 * h, 128 * h + 128)
+            pass_edge(PAIRS + h, [a[:, lanes] for a in prev], [a[:, lanes] for a in din])
+        st = step[...]
+        xut = xut_s[...]
+        speed = -jnp.exp(hp[0:1])
+        dds = dds_acc[...] - st * (xu_acc[...] + xut)
+        lane = lax.broadcasted_iota(jnp.int32, (512, 128), 1)
+        tok = lax.broadcasted_iota(jnp.int32, (256, 128), 0)
+        rr = lax.broadcasted_iota(jnp.int32, (256, 256), 0)
+        cc = lax.broadcasted_iota(jnp.int32, (256, 256), 1)
+        up = (cc >= rr).astype(bf)
+        drate = []
+        for g in range(2):
+            r = slice(256 * g, 256 * g + 256)
+            end = jnp.sum(st[r] * xut[r], axis=0, keepdims=True) + de_s[g][0:1] * jnp.exp(ds[256 * g + 255:256 * g + 256])
+            drate.append(mul_exact(up, dds[r] + jnp.where(tok == 255, end, 0.0)))
+        drate = jnp.concatenate(drate, 0)
+        dstep = xu_acc[...] + xut + drate * speed
+        draw = jnp.where(lane < 48, dstep * sig(raw[0] + hp[2:3]), 0.0)
+        dcp_o[13, :, 0:128] = draw.astype(bf)
+        dcp_o[13, :, 128:256] = jnp.zeros((512, 128), bf)
+        hg_o[0:1] = jnp.sum(drate * st * speed, axis=0, keepdims=True)
+        hg_o[1:2] = jnp.zeros((1, 128), f32)
+        hg_o[2:3] = jnp.sum(draw, axis=0, keepdims=True)
+        hg_o[3:8] = jnp.zeros((5, 128), f32)
+
+        @pl.when(me.z < 3)
+        def _():
+            def patch(i, _):
+                edge(i).wait_recv()
+                at = pl.ds(pl.multiple_of(lax.rem(i, 2) * 128, 128), 128)
+                for g in range(2):
+                    rows = lst[i, 8 * g:8 * g + 8] + got[i, 8 * g:8 * g + 8].astype(f32)
+                    dcp_o[i // 2, 256 * g + 248:256 * g + 256, at] = rows.astype(bf)
+                return 0
+            lax.fori_loop(0, PAIRS + 2, patch, 0)
+
+        @pl.when(me.z > 0)
+        def _(): lax.fori_loop(0, PAIRS + 2, lambda i, _: (edge(i).wait_send(), 0)[1], 0)
+
+
+S = jax.ShapeDtypeStruct
+V = pltpu.VMEM
+
+
+def const(*shape):
+    return pl.BlockSpec(shape, lambda j: (0,) * len(shape))
+
+
+TILE = pl.BlockSpec((1, 512, 128), lambda j: (j // 2, 0, lax.rem(j, 2)))
+HALO = pl.BlockSpec((1, 16, 128), lambda j: (j // 2, 32, lax.rem(j, 2)))
+ZT = pl.BlockSpec((1, 512, 128), lambda j: (14 + j // 2, 0, lax.rem(j, 2)))
+BC = pl.BlockSpec((1, 512, 256), lambda j: (12, 0, 0))
+BCH = pl.BlockSpec((1, 16, 256), lambda j: (12, 32, 0))
+RAW = pl.BlockSpec((1, 512, 128), lambda j: (13, 0, 0))
+TAP = pl.BlockSpec((8, 128), lambda j: (0, j))
+BCT = pl.BlockSpec((8, 256), lambda j: (0, 12))
+GAIN = pl.BlockSpec((8, 128), lambda j: (0, 38 + j))
+HP = const(8, 128)
+COL = pl.BlockSpec((512, 128), lambda j: (0, j))
+ST = pl.BlockSpec((1, 2, 128, 128), lambda j: (j, 0, 0, 0))
+DN = pl.BlockSpec((1, 512, 128), lambda j: (j // 3, 0, lax.rem(j, 3)))
+TOK = const(512, 128)
+TOKT = const(24, 8, 512)
+
+
+def call(body, name, in_specs, out_shape, out_specs, scratch, args, cid=None):
+    def kernel(*refs):
+        body(pl.program_id(0), *refs)
+    return pl.pallas_call(
+        kernel, grid=(PAIRS,), in_specs=in_specs, out_specs=out_specs, out_shape=out_shape, scratch_shapes=scratch,
+        compiler_params=pltpu.CompilerParams(vmem_limit_bytes=60 << 20, collective_id=cid, has_side_effects=cid is not None), name=name,
+    )(*args)
+
+
+def sf1(proj, par, hp):
+    return call(sf1_body, "sf1", [TILE, HALO, BC, BCH, RAW, TAP, BCT, HP],
+        (S((512, 3072), f32), S((512, 3072), f32), S((24, 2, 128, 128), bf), S((512, 128), f32), S((512, 128), f32), S((24, 8, 512), f32), S((512, 128), f32), S((512, 128), f32)),
+        (COL, COL, const(24, 2, 128, 128), TOK, TOK, TOKT, TOK, TOK),
+        [V((2, 264, 128), f32), V((2, 264, 256), f32), V((2, 3, 128, 128), f32), V((2, 128, 256), f32)] + Chain.scratch(),
+        (proj, proj, proj, proj, proj, par, par, hp), 4)
+
+
+def sf2(yi, x, ent, proj, dn, par, ds, c, hp):
+    return call(sf2_body, "sf2", [COL, COL, ST, ZT, DN, GAIN, TOK, TOK, HP],
+        (S((512, 3072), f32), S((2, 512, 128), f32)), (COL, const(2, 512, 128)),
+        [V((512, 128), f32), V((512, 128), f32)],
+        (yi, x, ent, proj, dn, par, ds, c, hp))
+
+
+def sb1(mixed, proj, dn, x, ent, par, ds, step, dst, b, c, hp, rq):
+    return call(sb1_body, "sb1", [COL, ZT, DN, COL, ST, GAIN, TOK, TOK, TOKT, TOK, TOK, HP, const(2, 512, 128)],
+        (S((512, 3072), f32), S((12, 512, 256), bf), S((512, 3072), bf), S((24, 2, 128, 128), bf), S((24, 8, 128), f32),
+         S((2, 3, 128, 128), f32), S((512, 128), f32), S((512, 128), f32), S((512, 128), f32)),
+        (COL, pl.BlockSpec((1, 512, 128), lambda j: (j // 2, 0, lax.rem(j, 2))), COL, const(24, 2, 128, 128), pl.BlockSpec((1, 8, 128), lambda j: (j, 0, 0)),
+         const(2, 3, 128, 128), TOK, TOK, TOK),
+        [V((2, 3, 128, 128), f32), V((2, 128, 256), f32)] + Chain.scratch(),
+        (mixed, proj, dn, x, ent, par, ds, step, dst, b, c, hp, rq), 5)
+
+
+def sb2(dxa, x, proj, par, std, ent, ds, step, b, c, hp, acc):
+    return call(sb2_body, "sb2", [COL, COL, TILE, HALO, TAP, ST, ST, BC, BCH, BCT, RAW, TOK, TOK, TOK, TOK, HP, const(2, 3, 128, 128), TOK, TOK, TOK],
+        (S((14, 512, 256), bf), S((26, 8, 128), f32), S((8, 128), f32)),
+        (const(14, 512, 256), const(26, 8, 128), HP),
+        [V((2, 264, 128), f32), V((2, 264, 256), f32), V((2, 272, 128), f32), V((2, 272, 256), f32), V((512, 128), f32), V((512, 128), f32), V((2, 8, 128), f32),
+         V((26, 16, 128), bf), V((26, 16, 128), f32), V((26, 16, 128), bf), pltpu.SemaphoreType.DMA((26,)), pltpu.SemaphoreType.DMA((26,))],
+        (dxa, x, proj, proj, par, std, ent, proj, proj, par, proj, ds, step, b, c, hp) + tuple(acc), 6)
+
+
+class Reduce:
+    def __init__(self, me, n, rows, refs, skew):
+        self.me, self.n, self.rows, self.sk, self.slots = me, n, rows, skew, skew + 1
+        (self.own0, self.own1, self.own2, self.own3, self.s0, self.s1, self.s2, self.s3, self.r0, self.r1, self.r2, self.r3,
+         self.o0, self.o1, self.o2, self.o3, self.i0, self.i1, self.i2, self.i3) = refs
+
+    @staticmethod
+    def scratch(n, rows, skew):
+        V, D, k = pltpu.VMEM, pltpu.SemaphoreType.DMA, skew + 1
+        z = 4 * rows
+        return [V((k, 2, 2, 2, z, 128), f32), V((k, 2, 2, z, 128), f32), V((k, 2, z, 128), f32), V((k, 2, rows, 128), f32),
+                V((k, 2, 2, 2, z, 128), bf), V((k, 2, 2, z, 128), bf), V((k, 2, z, 128), bf), V((k, 3, 2, rows, 128), bf),
+                V((n, 2, 2, 2, z, 128), bf), V((n, 2, 2, z, 128), bf), V((n, 2, z, 128), bf), V((n, 3, 2, rows, 128), bf),
+                D((k,)), D((k, 2)), D((k, 2)), D((k, 3)), D((n,)), D((n, 2)), D((n, 2)), D((n, 3))]
+
+    def c0(self, i, s):
+        return send(self.s0.at[s], self.r0.at[i], self.o0.at[s], self.i0.at[i], self.me.core_peer)
+
+    def c1(self, i, s, h):
+        return send(self.s1.at[s, h], self.r1.at[i, h], self.o1.at[s, h], self.i1.at[i, h], (self.me.x_peer, self.me.y_peer)[h])
+
+    def c2(self, i, s, h):
+        return send(self.s2.at[s, h], self.r2.at[i, h], self.o2.at[s, h], self.i2.at[i, h], (self.me.y_peer, self.me.x_peer)[h])
+
+    def c3(self, i, s, k):
+        return send(self.s3.at[s, k - 1], self.r3.at[i, k - 1], self.o3.at[s, k - 1], self.i3.at[i, k - 1], self.me.z_peer(k))
+
+    def step(self, it, product, out_ref):
+        n, sk, ns, R = self.n, self.sk, self.slots, self.rows
+        me, x, y, z, c = self.me, self.me.x, self.me.y, self.me.z, self.me.c
+
+        def stage(lag, body):
+            @pl.when((it >= lag * sk) & (it < n + lag * sk))
+            def _():
+                i = it - lag * sk
+                body(i, lax.rem(i, ns))
+
+        def zero(i, s):
+            @pl.when(i >= ns)
+            def _(): self.c0(i, s).wait_send()
+            part = product(i, 1 - c).astype(bf)
+            for h in range(2):
+                self.s0[s, h] = part[..., h * 128:(h + 1) * 128]
+            self.c0(i, s).start()
+            part = product(i, c)
+            for h in range(2):
+                self.own0[s, h] = part[..., h * 128:(h + 1) * 128]
+
+        def first(i, s):
+            own0, r0, own1 = self.own0, self.r0, self.own1
+            @pl.when(i >= ns)
+            def _():
+                for h in range(2): self.c1(i, s, h).wait_send()
+            self.c0(i, s).wait_recv()
+            for a in range(2):
+                self.s1[s, 0, a] = (own0[s, 0, a, 1 - x] + r0[i, 0, a, 1 - x].astype(f32)).astype(bf)
+            self.c1(i, s, 0).start()
+            self.s1[s, 1] = (own0[s, 1, 1 - y] + r0[i, 1, 1 - y].astype(f32)).astype(bf)
+            self.c1(i, s, 1).start()
+            for a in range(2):
+                own1[s, 0, a] = own0[s, 0, a, x] + r0[i, 0, a, x].astype(f32)
+            own1[s, 1] = own0[s, 1, y] + r0[i, 1, y].astype(f32)
+
+        def second(i, s):
+            own1, r1 = self.own1, self.r1
+            @pl.when(i >= ns)
+            def _():
+                for h in range(2): self.c2(i, s, h).wait_send()
+            for h, g in ((0, y), (1, x)):
+                self.c1(i, s, h).wait_recv()
+                self.s2[s, h] = (own1[s, h, 1 - g] + r1[i, h, 1 - g].astype(f32)).astype(bf)
+                self.c2(i, s, h).start()
+                self.own2[s, h] = own1[s, h, g] + r1[i, h, g].astype(f32)
+
+        def third(i, s):
+            own2, r2 = self.own2, self.r2
+            @pl.when(i >= ns)
+            def _():
+                for k in (1, 2, 3): self.c3(i, s, k).wait_send()
+            for h in range(2): self.c2(i, s, h).wait_recv()
+            for k in (2, 1, 3):
+                rows = pl.ds(pl.multiple_of(lax.rem(z + k, 4) * R, 16), R)
+                for h in range(2):
+                    self.s3[s, k - 1, h] = (own2[s, h, rows] + r2[i, h, rows].astype(f32)).astype(bf)
+                self.c3(i, s, k).start()
+            rows = pl.ds(pl.multiple_of(z * R, 16), R)
+            for h in range(2):
+                self.own3[s, h] = own2[s, h, rows] + r2[i, h, rows].astype(f32)
+
+        def last(i, s):
+            for k in (1, 2, 3): self.c3(i, s, k).wait_recv()
+            acc = self.own3[s]
+            for k in range(3): acc = acc + self.r3[i, k].astype(f32)
+            out_ref[i] = acc
+
+        stage(0, zero); stage(1, first); stage(2, second); stage(3, third); stage(4, last)
+
+    def finish(self):
+        for j in range(self.slots):
+            i = self.n - self.slots + j
+            s = i % self.slots
+            self.c0(i, s).wait_send()
+            for h in range(2):
+                self.c1(i, s, h).wait_send()
+                self.c2(i, s, h).wait_send()
+            for k in (1, 2, 3): self.c3(i, s, k).wait_send()
+
+
+def prod(lhs_ref, c, rhs, R):
+    lhs = lhs_ref[:, c].reshape(16 * R, 512)
+    return jnp.dot(lhs, rhs, preferred_element_type=f32).reshape(2, 2, 4 * R, 256)
+
+
+def out_call(out_low, out_low_t, cot, tokens, wout, collective_id, skew=2):
+    n, R = 6, 96
+
+    def kernel(ol, lhs, cot_ref, tok, w_hbm, sums, blk, wbuf, wsem, *refs):
+        me = Place()
+        greet(me.near())
+        red = Reduce(me, n, R, refs, skew)
+        def wcopy(i): return pltpu.make_async_copy(w_hbm.at[i], wbuf.at[lax.rem(i, 2)], wsem.at[lax.rem(i, 2)])
+        wcopy(0).start()
+
+        def cols(i): return pl.ds(pl.multiple_of(i * 256, 256), 256)
+        def loop(it, _):
+            red.step(it, lambda i, c: prod(lhs, c, cot_ref[:, cols(i)], R), sums)
+            @pl.when(it < n)
+            def _():
+                wcopy(it).wait()
+                @pl.when(it + 1 < n)
+                def _(): wcopy(it + 1).start()
+                s = lax.rem(it, 2)
+                w = jnp.concatenate([wbuf[s, h].reshape(3072, 128) for h in range(2)], axis=1)
+                branch = jnp.dot(ol[...], w, preferred_element_type=f32)
+                blk[:, cols(it)] = (tok[:, cols(it)].astype(f32) + branch).astype(bf)
+            return 0
+        lax.fori_loop(0, n + 4 * skew, loop, 0)
+        red.finish()
+
+    V, D, Sd = pltpu.VMEM, pltpu.SemaphoreType.DMA, jax.ShapeDtypeStruct
+    vm = pl.BlockSpec(memory_space=pltpu.VMEM)
+    return pl.pallas_call(
+        kernel, out_shape=(Sd((n, 2, R, 128), f32), Sd((512, 1536), bf)),
+        in_specs=[vm] * 4 + [pl.BlockSpec(memory_space=pl.ANY)], out_specs=(vm, vm),
+        scratch_shapes=[V((2, 2, 2, 2, 2, 384, 128), bf), D((2,))] + Reduce.scratch(n, R, skew),
+        compiler_params=pltpu.CompilerParams(collective_id=collective_id, has_side_effects=True, vmem_limit_bytes=63 << 20), name="outgrad",
+    )(out_low, out_low_t.reshape(4, 2, 384, 512), cot, tokens, wout)
+
+
+def in_call(low_t, dcp, dz, win, tok, cot, par, cg, rows, hg, collective_id, skew=2):
+    n, R = 26, 48
+
+    def kernel(lhs, dcp_ref, dz_ref, w_hbm, tok, cot, par_ref, cg_ref, rows_ref, hg_ref, sums, tg, small_o,
+               wbuf, wsem, dp, dn, flat, mail, box, m_out, m_in, *refs):
+        me = Place()
+        bar = pltpu.get_barrier_semaphore()
+        def sig(k, _):
+            pl.semaphore_signal(bar, inc=1, device_id=me.any_peer(k), device_id_type=MESH)
+            return 0
+        lax.fori_loop(1, 32, sig, 0)
+        pl.semaphore_wait(bar, 31)
+        red = Reduce(me, n, R, refs, skew)
+        def wcopy(i): return pltpu.make_async_copy(w_hbm.at[i], wbuf.at[lax.rem(i, 2)], wsem.at[lax.rem(i, 2)])
+        wcopy(0).start()
+        def post(k):
+            to = lax.rem(me.line + k, 32)
+            return send(mail.at[to], box.at[k - 1], m_out.at[k - 1], m_in.at[k - 1], me.any_peer(k))
+
+        def tail():
+            gain = par_ref[5:6, 3328:4864]
+            def block(t, acc):
+                r = pl.ds(pl.multiple_of(t * 64, 64), 64)
+                xf = tok[r].astype(f32)
+                h = lax.rsqrt(jnp.mean(xf * xf, axis=-1, keepdims=True) + 1e-5)
+                d = dn[r]
+                gd = d * gain
+                tg[r] = cot[r].astype(f32) + (h * gd - xf * (h * h * h * jnp.mean(gd * xf, axis=-1, keepdims=True)))
+                return acc + jnp.sum(d * xf * h, axis=0, keepdims=True)
+            norm = lax.fori_loop(0, 8, block, jnp.zeros((1, 1536), f32))
+            flat[...] = jnp.zeros_like(flat)
+            for j in range(26):
+                flat[0:5, 128 * j:128 * j + 128] = cg_ref[j, 0:5]
+            flat[5:6, 0:1536] = norm
+            for j in range(24):
+                flat[6:7, 128 * j:128 * j + 128] = rows_ref[j, 0:1]
+            for o in range(32):
+                b = [(o * w // 128) * 128 for w in (104, 48, 96)]
+                mail[o, 0:5] = flat[0:5, b[0]:b[0] + 256]
+                mail[o, 5:6] = flat[5:6, b[1]:b[1] + 256]
+                mail[o, 6:7] = flat[6:7, b[2]:b[2] + 256]
+                mail[o, 7:8] = hg_ref[0:1]
+            lax.fori_loop(1, 32, lambda k, _: (post(k).start(), 0)[1], 0)
+
+        def loop(it, _):
+            @pl.when(it < 14)
+            def _(): dp[...] = dcp_ref[lax.rem(it, 14)]
+            @pl.when((it >= 14) & (it < n))
+            def _(): dp[...] = dz_ref[lax.rem(it + 12 - 14, 12)]
+            red.step(it, lambda i, c: prod(lhs, c, dp[...], R), sums)
+            @pl.when(it < n)
+            def _():
+                wcopy(it).wait()
+                @pl.when(it + 1 < n)
+                def _(): wcopy(it + 1).start()
+                s = lax.rem(it, 2)
+                w = jnp.concatenate([wbuf[s, h].reshape(1536, 128) for h in range(2)], axis=1)
+                r = lax.dot_general(dp[...], w, (((1,), (1,)), ((), ())), preferred_element_type=f32)
+                @pl.when(it == 0)
+                def _(): dn[...] = r
+                @pl.when(it > 0)
+                def _(): dn[...] += r
+            @pl.when(it == n)
+            def _(): tail()
+            return 0
+        lax.fori_loop(0, n + 4 * skew, loop, 0)
+        small_o[...] = mail[me.line]
+        def take(k, _):
+            post(k).wait()
+            small_o[...] += box[k - 1]
+            return 0
+        lax.fori_loop(1, 32, take, 0)
+        red.finish()
+
+    V, D, Sd = pltpu.VMEM, pltpu.SemaphoreType.DMA, jax.ShapeDtypeStruct
+    vm = pl.BlockSpec(memory_space=pltpu.VMEM)
+    return pl.pallas_call(
+        kernel, out_shape=(Sd((n, 2, R, 128), f32), Sd((512, 1536), f32), Sd((8, 256), f32)),
+        in_specs=[vm] * 3 + [pl.BlockSpec(memory_space=pl.ANY)] + [vm] * 6, out_specs=(vm, vm, vm),
+        scratch_shapes=[V((2, 2, 2, 2, 2, 192, 128), bf), D((2,)), V((512, 256), bf), V((512, 1536), f32), V((8, 3584), f32), V((32, 8, 256), f32), V((31, 8, 256), f32), D((31,)), D((31,))]
+        + Reduce.scratch(n, R, skew),
+        compiler_params=pltpu.CompilerParams(collective_id=collective_id, has_side_effects=True, vmem_limit_bytes=63 << 20), name="ingrad",
+    )(low_t.reshape(4, 2, 192, 512), dcp, dz, win, tok, cot, par, cg, rows, hg)
+
+
+def fast(adamw, tokens, cotangent, in_proj, in_mom, in_var, out_proj, out_mom, out_var, conv_params, conv_mom, conv_var,
+         norm_gain, norm_mom, norm_var, gate_gain, gate_mom, gate_var, head_params, head_mom, head_var):
+    line = lax.axis_index("dp") * 4 + lax.axis_index("seq")
+    src_in, src_out, small = arrange(in_proj, out_proj, conv_params, norm_gain, gate_gain, line)
+    edge = jnp.pad(tokens[:, 253:], ((0, 0), (0, 5), (0, 0))).reshape(16, 1536)
+    tok, cot = tokens.reshape(512, 1536), cotangent.reshape(512, 1536)
+    proj, win, wout, low, par, dn = gather_call(src_in, src_out, small, tok, edge, cot, 1)
+    hp = jnp.pad(head_params, ((0, 5), (0, 80)))
+    x, yi, ent, step, ds, dst, b, c = sf1(proj, par, hp)
+    mixed, rq = sf2(yi, x, ent, proj, dn, par, ds, c, hp)
+    dxa, dz, ol, std, rows, *acc = sb1(mixed, proj, dn, x, ent, par, ds, step, dst, b, c, hp, rq)
+    dcp, cg, hg = sb2(dxa, x, proj, par, std, ent, ds, step, b, c, hp, acc)
+    out_sums, block = out_call(ol, ol.T, cot, tok, wout, 2)
+    skip = jnp.sum(rows[:, 1].reshape(48, 64), axis=1)
+    heads = jnp.pad(jnp.concatenate([hg[0, :48], skip, hg[2, :48]])[None], ((0, 7), (0, 112)))
+    in_sums, tokens_grad, small_sum = in_call(low.T, dcp, dz, win, tok, cot, par, cg, rows, heads, 3)
+    out_grad = out_sums.transpose(2, 0, 1, 3).reshape(96, 1536)
+    in_sums = in_sums.transpose(2, 0, 1, 3).reshape(48, 6656)
+    in_grad = jnp.concatenate([in_sums[:, 3584:], in_sums[:, :3376]], axis=1)
+    tokens_grad = tokens_grad.reshape(2, 256, 1536)
+    mine = lambda row, n, w: lax.dynamic_slice(small_sum, (row, lax.rem(line * w, 128)), (n, w))
+    conv_grad, norm_grad, gate_grad = mine(0, 5, 104), mine(5, 1, 48)[0], mine(6, 1, 96)[0]
+    head_grad = small_sum[7, :144].reshape(3, 48)
+    res = [(in_proj, in_mom, in_var, in_grad, 0.1), (out_proj, out_mom, out_var, out_grad, 0.1), (conv_params, conv_mom, conv_var, conv_grad, 0.1),
+           (norm_gain, norm_mom, norm_var, norm_grad, 0.0), (gate_gain, gate_mom, gate_var, gate_grad, 0.0), (head_params, head_mom, head_var, head_grad, 0.0)]
+    new = [v for a in res for v in adamw(*a)]
+    return (block.reshape(2, 256, 1536), tokens_grad, in_grad, out_grad, conv_grad, norm_grad, gate_grad, head_grad, *new)
+
+
 def solution(mesh):
     in_specs = (
         P("dp", "seq", None),
@@ -316,4 +1331,6 @@
         P(),
         P(),
     )
-    return jax.shard_map(body, mesh=mesh, in_specs=in_specs, out_specs=out_specs, check_vma=False)
+    own = tuple(mesh.shape[a] for a in ("dp", "seq")) == (8, 4)
+    step = functools.partial(fast, adamw) if own else body
+    return jax.shard_map(step, mesh=mesh, in_specs=in_specs, out_specs=out_specs, check_vma=False)

time: 1530 us -> 562 us (0.37)
  waiting for transfers between devices: 655 us -> 0 us
  Pallas kernels: 0 us -> 521 us
  matrix products: 264 us -> 0 us
  other arithmetic: 220 us -> 9.4 us
  blocking collectives: 183 us -> 0 us
  local copies, waits for them, and re-layouts: 179 us -> 28.6 us
    pallas_call x0 -> x7, Pallas kernels: none -> 521 us  [the longest x1 174 us: gather_call(): pl.pallas_call(kernel, out_shape=(S((NI, TE, 256), f32), S(wi, bf), S(wo,...]
    reduce_scatter x2 -> x0, waiting for transfers between devices: 500 us -> none  [the longest x1 367 us: body(): lax.psum_scatter(in_grad_local, ('dp', 'seq'), scatter_dimension=0, tiled...]
    dot_general x26 -> x0, matrix products: 264 us -> none  [the longest x6 98.9 us: intra_item(): return jnp.einsum('hts,shp->thp', weights, head_x, precision=highest)]
    all_gather x4 -> x0, waiting for transfers between devices: 153 us -> none  [the longest x1 141 us: entering(): gathered = jax.tree.map(lambda a: lax.all_gather(a, axis), part)]
    reduce_sum x9 -> x1, other arithmetic: 101 us -> 0.11 us  [fast(): skip = jnp.sum(rows[:, 1].reshape(48, 64), axis=1)]
    all_gather x3 -> x0, blocking collectives: 99.7 us -> none  [the longest x1 74.2 us: body(): lax.all_gather(conv_params, ('dp', 'seq'), axis=1, tiled=True)]
    unnamed x2 -> x0, blocking collectives: 83.1 us -> none
    slice x12 -> x9, local copies, waits for them, and re-layouts: 41.1 us -> 1.82 us  [the longest x1 0.93 us: fast(): skip = jnp.sum(rows[:, 1].reshape(48, 64), axis=1)]
  transfers between devices with their start and end apart: 9 -> 0, of which waited for: 5 -> 0; matrix products, arithmetic and copies ran while one was open for 30% -> 0% of each run, Pallas kernels for 0% -> 0%
where the time goes in v2:
time: 562 us; the launch traced here: 560 us
  Pallas kernels  521 us (93%)
  local copies, waits for them, and re-layouts  28.6 us (5%)
  other arithmetic  9.4 us (2%)
    pallas_call x1, Pallas kernels, gather_call(): pl.pallas_call(kernel, out_shape=(S((NI, TE, 256), f32), S(wi, bf), S(wo,...  174 us
    pallas_call x4, Pallas kernels, call(): pl.pallas_call(kernel, grid=(PAIRS,), in_specs=in_specs, out_specs=out_sp...  172 us
    pallas_call x1, Pallas kernels, in_call(): pl.pallas_call(kernel, out_shape=(Sd((n, 2, R, 128), f32), Sd((512, 1536)...  111 us
    pallas_call x1, Pallas kernels, out_call(): pl.pallas_call(kernel, out_shape=(Sd((n, 2, R, 128), f32), Sd((512, 1536)...  63.6 us

profile of v2, /device:TPU:0, one launch (start us, length us, event | category | flops | bytes accessed | tf_op | source)
XLA Modules:
  0.0 560.1 jit_solution(6314470191228768152)
XLA Ops:
  0.7 0.0 copy-start.1
  0.7 1.4 pad.13.refs_7_.refs_8_.refs_11_.refs_15_
  2.1 1.5 dynamic_update_slice.9
  3.6 0.8 dynamic_update_slice.10
  4.4 0.8 dynamic_update_slice.11.small_ref
  5.2 0.0 copy-start.9
  5.2 0.8 slice.29
  6.0 0.6 pad_bitcast_fusion.edge_ref
  6.6 1.1 convert_element_type.13
  7.7 0.1 reshape.86
  7.8 0.8 copy.57
  8.6 0.0 copy-done.1
  8.6 0.1 convert_element_type.12
  8.7 0.2 concatenate.9
  8.9 0.1 reshape.85
  9.1 0.9 copy.56
  10.0 174.1 %gather.1 = (f32[26,528,256]{2,1,0:T(8,128)}, bf16[26,2,2,2,2,192,128]{6,5,4,3,2,1,0:T(8,128)(2,1)}, bf16[6,2,2,2,2,384,128]{6,5,4,3,2,1,0:T(8,128)(2,1)}, bf16[...) custom-call(bf16[26,2,48,128]{3,2,1,0:T(8,128)(2,1)} %bitcast.41, ...), custom_call_target="tpu_custom_call" | custom-call | tf_op jit(solution)/shard_map/gather/pallas_call | solution.py:505
  184.1 2.6 copy.51
  186.7 40.7 %sf1.1 = (f32[512,3072]{1,0:T(8,128)}, f32[512,3072]{1,0:T(8,128)}, bf16[24,2,128,128]{3,2,1,0:T(8,128)(2,1)}, f32[512,128]{1,0:T(8,128)}, f32[512,128]{1,0:T(8,...) custom-call(f32[26,528,256]{2,1,0:T(8,128)} %get-tuple-element.59.refs_0_.refs_1_.refs_2_.refs_3_.refs_4_.refs_7, ...), custom_call_target="tpu_custom_call" | custom-call | tf_op jit(solution)/shard_map/sf1/pallas_call | solution.py:980
  227.4 24.7 %sf2.1 = (f32[512,3072]{1,0:T(8,128)}, f32[2,512,128]{2,1,0:T(8,128)}) custom-call(f32[512,3072]{1,0:T(8,128)} %get-tuple-element.61.refs_0_, f32[512,3072]{1,0:T(8,128)} %get-tuple-element.62.refs_1_.refs_3_, bf16[24,2,128,128]{3,2,1,0:T(8,128)(2,1)} %get-tuple-element.63.refs_2_.refs_4_.refs_6_, ...), custom_call_target="tpu_custom_call" | custom-call | tf_op jit(solution)/shard_map/sf2/pallas_call | solution.py:980
  252.1 69.5 %sb1.1 = (f32[512,3072]{1,0:T(8,128)}, bf16[12,512,256]{2,1,0:T(8,128)(2,1)}, bf16[512,3072]{1,0:T(8,128)(2,1)}, bf16[24,2,128,128]{3,2,1,0:T(8,128)(2,1)}, f32[...) custom-call(f32[512,3072]{1,0:T(8,128)} %get-tuple-element.67.refs_0, ...), custom_call_target="tpu_custom_call" | custom-call | tf_op jit(solution)/shard_map/sb1/pallas_call | solution.py:980
  321.5 37.5 %sb2.1 = (bf16[14,512,256]{2,1,0:T(8,128)(2,1)}, f32[26,8,128]{2,1,0:T(8,128)}, f32[8,128]{1,0:T(8,128)}) custom-call(f32[512,3072]{1,0:T(8,128)} %get-tuple-element.76.refs_0_, f32[512,3072]{1,0:T(8,128)} %get-tuple-element.62.refs_1_.refs_3_, f32[26,528,256]{2,1,0:T(8,128)} %get-tuple-element.59.refs_0_.refs_1_.refs_2_.refs_3_.refs_4_.refs_7_.refs_8_.refs_10_, ...), custom_call_target="tpu_custom_call" | custom-call | tf_op jit(solution)/shard_map/sb2/pallas_call | solution.py:980
  359.0 0.8 slice_bitcast_fusion.1
  359.8 0.9 slice_reduce_fusion
  360.7 0.1 reshape_squeeze.6
  360.8 0.1 reduce_sum.9
  360.9 0.1 pad_maximum_fusion.1
  361.0 0.6 pad.14.hg_ref
  361.6 0.0 copy-start.22
  361.6 0.0 copy-start.23
  361.7 0.0 copy-start.11
  361.7 0.0 copy-start.16
  361.7 0.0 copy-start.17
  361.7 0.0 copy-start.10
  361.7 0.0 copy-start.14
  361.7 0.0 copy-start.15
  361.7 111.0 %ingrad.1 = (f32[26,2,48,128]{3,2,1,0:T(8,128)}, f32[512,1536]{1,0:T(8,128)}, f32[8,256]{1,0:T(8,128)}) custom-call(bf16[4,2,192,512]{3,2,1,0:T(8,128)(2,1)} %bitcast.39, bf16[14,512,256]{2,1,0:T(8,128)(2,1)} %get-tuple-element.82.dcp_ref, bf16[12,512,256]{2,1,0:T(8,128)(2,1)} %get-tuple-element.83.dz_ref, ...), custom_call_target="tpu_custom_call" | custom-call | tf_op jit(solution)/shard_map/ingrad/pallas_call | solution.py:1245
  472.7 3.0 copy.52
  475.7 3.3 reshape.94
  479.1 0.1 reshape_squeeze.7
  479.2 0.0 copy-done.20
  479.2 0.0 copy-start.12
  479.2 0.6 multiply_subtract_fusion.4
  479.8 0.6 multiply_subtract_fusion.5
  480.4 0.0 copy-done.11
  480.4 0.0 copy-done.17
  480.5 0.6 multiply_subtract_fusion.3
  481.1 0.7 multiply_subtract_fusion.2
  481.8 2.8 copy.50
  484.5 63.6 %outgrad.1 = (f32[6,2,96,128]{3,2,1,0:T(8,128)}, bf16[512,1536]{1,0:T(8,128)(2,1)}) custom-call(bf16[512,3072]{1,0:T(8,128)(2,1)} %get-tuple-element.72.ol, bf16[4,2,384,512]{3,2,1,0:T(8,128)(2,1)} %bitcast.38, bf16[512,1536]{1,0:T(8,128)(2,1)} %bitcast.36, bf16[512,1536]{1,0:T(8,128)(2,1)} %bitcast.33, ...), custom_call_target="tpu_custom_call" | custom-call | tf_op jit(solution)/shard_map/outgrad/pallas_call | solution.py:1161
  548.2 0.0 copy-start.4
  548.2 1.6 copy.53
  549.8 0.0 copy-start.8
  549.8 0.5 reshape.95
  550.3 0.0 copy-start.5
  550.3 0.0 slice-start
  550.3 0.0 slice-start.1
  550.3 0.0 copy-start.2
  550.4 0.0 copy-start.7
  550.4 3.0 multiply_subtract_fusion.1
  553.4 2.5 multiply_subtract_fusion
  555.9 1.1 copy.63
  557.1 1.3 copy-done.3
  558.4 1.7 copy.64
  (34 shorter events, 0.1 us)
Async XLA Ops:
  0.7 7.9 %copy-start.1 = (f32[48,6448]{1,0:T(8,128)S(1)}, f32[48,6448]{1,0:T(8,128)}, u32[]{:S(2)}) copy-start(f32[48,6448]{1,0:T(8,128)} %param.22) | copy-start | bytes 3714052
  5.2 3.5 copy-start.9
  361.6 117.6 %copy-start.18 = (f32[96]{0:T(128)S(1)}, f32[96]{0:T(128)}, u32[]{:S(2)}) copy-start(f32[96]{0:T(128)} %param.34) | copy-start | bytes 1156
  361.6 117.6 %copy-start.20 = (f32[96]{0:T(128)S(1)}, f32[96]{0:T(128)}, u32[]{:S(2)}) copy-start(f32[96]{0:T(128)} %param.35) | copy-start | bytes 1156
  361.6 117.6 %copy-start.21 = (f32[96]{0:T(128)S(1)}, f32[96]{0:T(128)}, u32[]{:S(2)}) copy-start(f32[96]{0:T(128)} %param.36) | copy-start | bytes 1156
  361.6 118.2 %copy-start.19 = (f32[48]{0:T(128)S(1)}, f32[48]{0:T(128)}, u32[]{:S(2)}) copy-start(f32[48]{0:T(128)} %param.31) | copy-start | bytes 580
  361.6 118.2 %copy-start.22 = (f32[48]{0:T(128)S(1)}, f32[48]{0:T(128)}, u32[]{:S(2)}) copy-start(f32[48]{0:T(128)} %param.32) | copy-start | bytes 580
  361.6 118.2 %copy-start.23 = (f32[48]{0:T(128)S(1)}, f32[48]{0:T(128)}, u32[]{:S(2)}) copy-start(f32[48]{0:T(128)} %param.33) | copy-start | bytes 580
  361.7 118.8 %copy-start.11 = (f32[3,48]{1,0:T(4,128)S(1)}, f32[3,48]{1,0:T(4,128)}, u32[]{:S(2)}) copy-start(f32[3,48]{1,0:T(4,128)} %param.37) | copy-start | bytes 1732
  361.7 118.8 %copy-start.16 = (f32[3,48]{1,0:T(4,128)S(1)}, f32[3,48]{1,0:T(4,128)}, u32[]{:S(2)}) copy-start(f32[3,48]{1,0:T(4,128)} %param.38) | copy-start | bytes 1732
  361.7 118.8 %copy-start.17 = (f32[3,48]{1,0:T(4,128)S(1)}, f32[3,48]{1,0:T(4,128)}, u32[]{:S(2)}) copy-start(f32[3,48]{1,0:T(4,128)} %param.39) | copy-start | bytes 1732
  361.7 119.4 %copy-start.10 = (f32[5,104]{1,0:T(8,128)S(1)}, f32[5,104]{1,0:T(8,128)}, u32[]{:S(2)}) copy-start(f32[5,104]{1,0:T(8,128)} %param.28) | copy-start | bytes 6244
  361.7 119.4 %copy-start.14 = (f32[5,104]{1,0:T(8,128)S(1)}, f32[5,104]{1,0:T(8,128)}, u32[]{:S(2)}) copy-start(f32[5,104]{1,0:T(8,128)} %param.29) | copy-start | bytes 6244
  361.7 119.4 %copy-start.15 = (f32[5,104]{1,0:T(8,128)S(1)}, f32[5,104]{1,0:T(8,128)}, u32[]{:S(2)}) copy-start(f32[5,104]{1,0:T(8,128)} %param.30) | copy-start | bytes 6244
  472.7 6.4 %copy-start.13 = (f32[8,256]{1,0:T(8,128)S(1)}, f32[8,256]{1,0:T(8,128)}, u32[]{:S(2)}) copy-start(f32[8,256]{1,0:T(8,128)} %get-tuple-element.91) | copy-start | bytes 24580
  475.7 6.0 %copy-start = (bf16[512,3072]{1,0:T(8,128)(2,1)S(1)}, bf16[512,3072]{1,0:T(8,128)(2,1)}, u32[]{:S(2)}) copy-start(bf16[512,3072]{1,0:T(8,128)(2,1)} %get-tuple-element.72.ol) | copy-start | bytes 9437188
  479.2 2.6 copy-start.12
  548.2 2.1 copy-start.4
  549.8 3.5 copy-start.8
  550.3 3.0 copy-start.5
  550.3 3.0 slice-start
  550.3 3.0 slice-start.1
  550.3 3.0 copy-start.2
  550.4 3.0 copy-start.7
  553.4 2.5 copy-start.6
  555.9 2.5 copy-start.3

commit v3 on v2

--- a/solution.py
+++ b/solution.py
@@ -480,13 +480,15 @@
                     def cols(q, _):
                         y = q // 4; x = lax.rem(q // 2, 2); c = lax.rem(q, 2)
                         r = lax.dot_general(a, wout[i, h, y, x, c], (((1,), (1,)), ((), ())), preferred_element_type=f32)
-                        if h == 0:
-                            @pl.when(i == 0)
-                            def _(): dn_ref[q] = r
-                            @pl.when(i > 0)
-                            def _(): dn_ref[q] += r
-                        else:
-                            dn_ref[q] += r
+                        for t in range(3):
+                            rt = r[:, 128 * t:128 * t + 128]
+                            if h == 0:
+                                @pl.when(i == 0)
+                                def _(): dn_ref[3 * q + t] = rt
+                                @pl.when(i > 0)
+                                def _(): dn_ref[3 * q + t] += rt
+                            else:
+                                dn_ref[3 * q + t] += rt
                         return 0
                     lax.fori_loop(0, 8, cols, 0)
             return 0
@@ -504,7 +506,7 @@
     wi, wo = (NI, 2, 2, 2, 2, 192, 128), (NO, 2, 2, 2, 2, 384, 128)
     return pl.pallas_call(
         kernel,
-        out_shape=(S((NI, TE, 256), f32), S(wi, bf), S(wo, bf), S((T, DM), bf), S((8, 7936), f32), S((8, T, 384), f32)),
+        out_shape=(S((NI, TE, 256), f32), S(wi, bf), S(wo, bf), S((T, DM), bf), S((8, 7936), f32), S((24, T, 128), f32)),
         in_specs=[vm] * 6,
         out_specs=(hb, hb, hb, vm, vm, vm),
         scratch_shapes=[V(wi, bf), V(wo, bf), V((32, 8, 256), f32), V((TE, DM), bf), V((16, DM), bf), V((2, TE, 256), f32)]
@@ -526,9 +528,8 @@
     return src_in, src_out, small
 
 
-PAIRS = 24
+TILES = 12
 NN, NT, TN_ = (((1,), (0,)), ((), ())), (((1,), (1,)), ((), ())), (((0,), (0,)), ((), ()))
-PASSES = 3
 
 
 def one(a, b, dims):
@@ -540,12 +541,18 @@
     return hi, (a - hi.astype(f32)).astype(bf)
 
 
+def cross(a, b, dims=NN):
+    (ah, al), (bh, bl) = (v if isinstance(v, tuple) else (v, None) for v in (a, b))
+    out = one(ah, bh, dims)
+    if bl is not None:
+        out = out + one(ah, bl, dims)
+    if al is not None:
+        out = out + one(al, bh, dims)
+    return out
+
+
 def mul(a, b, dims=NN):
-    if PASSES == 1:
-        return one(a.astype(bf), b.astype(bf), dims)
-    ah, al = halves(a)
-    bh, bl = halves(b)
-    return one(ah, bh, dims) + (one(ah, bl, dims) + one(al, bh, dims))
+    return cross(*(v if isinstance(v, tuple) or v.dtype == bf else halves(v) for v in (a, b)), dims)
 
 
 def mul_exact(a, b, dims=NN, left=True):
@@ -562,28 +569,36 @@
 
 
 def to_heads(a, spot):
-    h, l = halves(a)
-    return one(h, spot, NN) + one(l, spot, NN)
+    return cross(halves(a), spot)
 
 
 def rolled(a, j):
-    return pltpu.roll(a, lax.rem(128 - 2 * j, 128), 1)
+    return pltpu.roll(a, lax.rem(128 - 4 * j, 128), 1)
 
 
 def spread(r):
     lane = lax.broadcasted_iota(jnp.int32, (r.shape[0], 128), 1)
-    return jnp.where(lane < 64, r[:, 0:1], r[:, 1:2])
-
-
-def masks(rows):
-    lane = lax.broadcasted_iota(jnp.int32, (rows, 128), 1)
-    return (lane < 64).astype(f32), (lane >= 64).astype(f32)
+    return jnp.concatenate([jnp.where(lane < 64, r[:, h:h + 1], r[:, h + 1:h + 2]) for h in (0, 2)], 1)
+
+
+def by_head(v):
+    lane = lax.broadcasted_iota(jnp.int32, v.shape, 1)
+    zero = jnp.zeros_like(v)
+    return jnp.concatenate([jnp.where(lane < 64, v, zero), jnp.where(lane >= 64, v, zero)], 0)
+
+
+def heads_apart(pair):
+    return tuple(by_head(v.astype(f32)).astype(bf) for v in pair)
+
+
+def part_of(pair, *index):
+    return tuple(v[index] for v in pair)
 
 
 def spot_of(j):
-    p = lax.broadcasted_iota(jnp.int32, (128, 128), 0)
-    lane = lax.broadcasted_iota(jnp.int32, (128, 128), 1)
-    return (lane == 2 * j + p // 64).astype(bf)
+    p = lax.broadcasted_iota(jnp.int32, (256, 128), 0)
+    lane = lax.broadcasted_iota(jnp.int32, (256, 128), 1)
+    return (lane == 4 * j + p // 64).astype(bf)
 
 
 def fill_pad(pad, cin, halo):
@@ -613,7 +628,8 @@
 
 
 class Chain:
-    def __init__(self, me, by, got, part, out, out_sem, in_sem, keep):
+    def __init__(self, me, by, got, part, out, out_sem, in_sem, keep, lag):
+        self.lag = lag
         self.me, self.by, self.got, self.part, self.out, self.out_sem, self.in_sem, self.keep = me, by, got, part, out, out_sem, in_sem, keep
         self.place = me.z if by == 1 else 3 - me.z
 
@@ -638,22 +654,25 @@
         @pl.when(self.place == 0)
         def _(): self.got[...] = jnp.zeros_like(self.got)
 
-    def step(self, j):
-        lag = 2 * self.place
-        @pl.when(j >= lag)
+    def step(self, j, drain):
+        lag = self.lag * self.place
+        @pl.when((j >= lag) & (j < TILES + lag))
         def _(): self.tile(j - lag)
 
-        @pl.when(j == PAIRS - 1)
+        if drain:
+            @pl.when(j == TILES - 1)
+            def _():
+                lax.fori_loop(TILES - lag, TILES, lambda i, _: (self.tile(i), 0)[1], 0)
+
+    def finish(self):
+        @pl.when(self.place < 3)
         def _():
-            lax.fori_loop(PAIRS - lag, PAIRS, lambda i, _: (self.tile(i), 0)[1], 0)
-            @pl.when(self.place < 3)
-            def _():
-                for i in range(PAIRS - 3, PAIRS): self.copy(i).wait_send()
+            for i in range(TILES - 3, TILES): self.copy(i).wait_send()
 
     @staticmethod
     def scratch():
         D = pltpu.SemaphoreType.DMA
-        return [V((PAIRS, 2, 128, 128), bf), V((PAIRS, 2, 128, 128), f32), V((3, 2, 128, 128), bf), D((3,)), D((PAIRS,))]
+        return [V((TILES, 2, 128, 256), bf), V((TILES, 2, 128, 256), f32), V((3, 2, 128, 256), bf), D((3,)), D((TILES,))]
 
 
 def keeper(ds):
@@ -668,7 +687,7 @@
 
 def sf1_body(j, cin, halo, bcin, bchalo, raw, taps, bctaps, hp, x_o, yi_o, ent_o, step_o, ds_o, dst_o, b_o, c_o, pad, pad2, s_s, bt_s, got, part, out, out_sem, in_sem):
     me = Place()
-    line = Chain(me, 1, got, part, out, out_sem, in_sem, keeper(ds_o))
+    line = Chain(me, 1, got, part, out, out_sem, in_sem, keeper(ds_o), 1)
     @pl.when(j == 0)
     def _():
         greet((me.z_peer(1), me.z_peer(3)))
@@ -683,8 +702,8 @@
         for g in range(2):
             ds_o[256 * g:256 * g + 256] = mul_exact(low, rate[256 * g:256 * g + 256])
         turned = ds_o[...].T
-        for p in range(PAIRS):
-            dst_o[p, 0:2] = turned[2 * p:2 * p + 2]
+        for p in range(TILES):
+            dst_o[p, 0:4] = turned[4 * p:4 * p + 4]
         fill_pad(pad2, bcin[0], bchalo[0])
         for g, co in enumerate(conv(pad2, bctaps)):
             act = co * sig(co)
@@ -700,32 +719,36 @@
     rds = rolled(ds_o[...], j)
     dsc = spread(rds)
     stc = spread(rolled(step_o[...], j))
-    m0, m1 = masks(128)
     ok = causal(False)
     for g, co in enumerate(conv(pad, taps)):
         b0 = 256 * g
         x = co * sig(co)
         x_o[b0:b0 + 256] = x
         xs = x * stc[b0:b0 + 256]
+        xp = halves(xs)
         d = dsc[b0:b0 + 256]
         ys = []
         for q in range(2):
             b = b0 + 128 * q
-            w = []
-            for h in range(2):
-                gap = rds[b:b + 128, h:h + 1] - dst_o[j, h:h + 1, b:b + 128]
-                w.append(s_s[g, q] * jnp.exp(jnp.where(ok, gap, -1e30)))
-            xq = xs[128 * q:128 * q + 128]
-            ys.append(mul(jnp.concatenate(w, 1), jnp.concatenate([xq * m0, xq * m1], 0)))
+            y = []
+            for m in range(2):
+                w = []
+                for h in (2 * m, 2 * m + 1):
+                    gap = rds[b:b + 128, h:h + 1] - dst_o[j, h:h + 1, b:b + 128]
+                    w.append(s_s[g, q] * jnp.exp(jnp.where(ok, gap, -1e30)))
+                y.append(mul(jnp.concatenate(w, 1), heads_apart(part_of(xp, slice(128 * q, 128 * q + 128), slice(128 * m, 128 * m + 128)))))
+            ys.append(jnp.concatenate(y, 1))
         mid = d[127:128]
         ys[1] = ys[1] + jnp.exp(d[128:] - mid) * mul(s_s[g, 2], jnp.exp(mid - d[:128]) * xs[:128])
         yi_o[b0:b0 + 128] = ys[0]
         yi_o[b0 + 128:b0 + 256] = ys[1]
         part[j, g] = mul(bt_s[g], jnp.exp(d[255:256] - d) * xs)
-    line.step(j)
-
-    @pl.when(j == PAIRS - 1)
-    def _(): ent_o[...] = got[...]
+    line.step(j, True)
+
+    @pl.when(j == TILES - 1)
+    def _():
+        line.finish()
+        ent_o[...] = got[...]
 
 
 def sf2_body(j, yi, x, ent, z, dn, gain, ds, c_r, hp, mixed_o, rq_o, a1, a2):
@@ -737,15 +760,15 @@
     skip = spread(rolled(hp[...], j))[1:2]
     for g in range(2):
         r = slice(256 * g, 256 * g + 256)
-        car = jnp.exp(dsc[r]) * mul(c_r[r], ent[0, g].astype(f32))
+        car = jnp.exp(dsc[r]) * mul(c_r[r], ent[0, g])
         mixed = yi[r] + car + skip * x[r]
         mixed_o[r] = mixed
         zz = z[0, r]
         gated = mixed * (zz * sig(zz))
         a1[r] += gated * gated
-        a2[r] += gain[6:7] * dn[0, r] * gated
-
-    @pl.when(j == PAIRS - 1)
+        a2[r] += gain[6:7] * jnp.concatenate([dn[0, r], dn[1, r]], 1) * gated
+
+    @pl.when(j == TILES - 1)
     def _():
         r = lax.rsqrt(jnp.sum(a1[...], axis=1, keepdims=True) * (1.0 / 3072) + 1e-5)
         k = r * r * r * (jnp.sum(a2[...], axis=1, keepdims=True) * (1.0 / 3072))
@@ -753,79 +776,90 @@
         rq_o[1] = jnp.broadcast_to(k, (512, 128))
 
 
-def sb1_body(j, mixed, z, dn, x, ent, gain, ds, step, dst, b_r, c_r, hp, rq,
-             dxa_o, dz_o, ol_o, std_o, rows_o, dst_acc, dc_acc, dds_acc, xu_acc, st_s, ct_s, got, part, out, out_sem, in_sem):
-    me = Place()
-    line = Chain(me, -1, got, part, out, out_sem, in_sem, keeper(ds))
-    @pl.when(j == 0)
-    def _():
-        greet((me.z_peer(1), me.z_peer(3)))
-        line.start()
-        for a in (dst_acc, dc_acc, dds_acc, xu_acc):
-            a[...] = jnp.zeros_like(a)
-        for g in range(2):
-            b, c = b_r[256 * g:256 * g + 256], c_r[256 * g:256 * g + 256]
-            st_s[g, 0] = mul(b[:128], c[:128], NT)
-            st_s[g, 1] = mul(b[128:], c[128:], NT)
-            st_s[g, 2] = mul(b[:128], c[128:], NT)
-            ct_s[g] = c.T
+def sb1_start(b_r, c_r, dst_acc, dc_acc, dds_acc, xu_acc, st_s, ct_s):
+    for a in (dst_acc, dc_acc, dds_acc, xu_acc):
+        a[...] = jnp.zeros_like(a)
+    for g in range(2):
+        b, c = b_r[256 * g:256 * g + 256], c_r[256 * g:256 * g + 256]
+        st_s[g, 0] = mul(b[:128], c[:128], NT)
+        st_s[g, 1] = mul(b[128:], c[128:], NT)
+        st_s[g, 2] = mul(b[:128], c[128:], NT)
+        ct_s[g] = c.T
+
+
+def sb1_tile(j, mixed, z, dn, x, ent, gain, ds, step, dst, hp, rq, dxa_s, dz_o, dz_s, ol_o, lhs_s, rows_o,
+             dst_acc, dc_acc, dds_acc, xu_acc, st_s, ct_s, part):
     rds = rolled(ds[...], j)
     dsc = spread(rds)
     stc = spread(rolled(step[...], j))
     skip = spread(rolled(hp[...], j))[1:2]
-    m0, m1 = masks(128)
     ok = causal(True)
     spot = spot_of(j)
-    dgain = jnp.zeros((1, 128), f32)
-    dskip = jnp.zeros((1, 128), f32)
+    dgain = jnp.zeros((1, 256), f32)
+    turned = []
+    dskip = jnp.zeros((1, 256), f32)
     for g in range(2):
         r = slice(256 * g, 256 * g + 256)
         zz, mx, xx = z[0, r], mixed[r], x[r]
+        dnr = jnp.concatenate([dn[0, r], dn[1, r]], 1)
         s = sig(zz)
         sil = zz * s
         gated = mx * sil
-        rr, kk = rq[0, r], rq[1, r]
+        rr, kk = (jnp.concatenate([rq[k, r]] * 2, 1) for k in (0, 1))
         gr = gated * rr
-        ol_o[r] = (gr * gain[6:7]).astype(bf)
-        dgain += jnp.sum(dn[0, r] * gr, axis=0, keepdims=True)
-        dg = rr * (gain[6:7] * dn[0, r]) - gated * kk
+        ol = gr * gain[6:7]
+        ol_o[r] = ol.astype(bf)
+        turned.append(ol.T.astype(bf))
+        dgain += jnp.sum(dnr * gr, axis=0, keepdims=True)
+        dg = rr * (gain[6:7] * dnr) - gated * kk
         dy = dg * sil
-        dz_o[0, r] = (dg * mx * (s * (1.0 + zz * (1.0 - s)))).astype(bf)
+        dz = (dg * mx * (s * (1.0 + zz * (1.0 - s)))).astype(bf)
+        dz_o[0, r] = dz
+        dz_s[r] = dz
         dskip += jnp.sum(dy * xx, axis=0, keepdims=True)
         d = dsc[r]
-        eu = jnp.exp(d) * dy
+        eu = halves(jnp.exp(d) * dy)
         part[j, g] = mul(ct_s[g], eu)
-        dc_acc[r] += mul(eu, ent[0, g].astype(f32), NT)
+        dc_acc[r] += mul(eu, ent[j, g], NT)
         dds_acc[r] += to_heads(dy * (mx - skip * xx), spot)
         xs = xx * stc[r]
+        dp, xp = halves(dy), halves(xs)
         us = []
         for q in range(2):
             b = 256 * g + 128 * q
-            e = []
-            for h in range(2):
-                gap = dst[j, h:h + 1, b:b + 128] - rds[b:b + 128, h:h + 1]
-                e.append(jnp.exp(jnp.where(ok, gap, -1e30)))
-            w = jnp.concatenate([st_s[g, q] * e[0], st_s[g, q] * e[1]], 1)
             lo = slice(128 * q, 128 * q + 128)
-            dq, xq = dy[lo], xs[lo]
-            us.append(mul(w, jnp.concatenate([dq * m0, dq * m1], 0)))
-            gt = mul(jnp.concatenate([xq * m0, xq * m1], 0), dq, NT)
-            dst_acc[g, q] += gt[:128] * e[0] + gt[128:] * e[1]
+            u, acc = [], 0.0
+            for m in range(2):
+                e = []
+                for h in (2 * m, 2 * m + 1):
+                    gap = dst[j, h:h + 1, b:b + 128] - rds[b:b + 128, h:h + 1]
+                    e.append(jnp.exp(jnp.where(ok, gap, -1e30)))
+                w = jnp.concatenate([st_s[g, q] * e[0], st_s[g, q] * e[1]], 1)
+                cols = slice(128 * m, 128 * m + 128)
+                dh = heads_apart(part_of(dp, lo, cols))
+                u.append(mul(w, dh))
+                gt = mul(part_of(xp, lo, cols), dh, NT)
+                acc = acc + (gt[:, :128] * e[0] + gt[:, 128:] * e[1])
+            dst_acc[g, q] += acc
+            us.append(jnp.concatenate(u, 1))
         mid = d[127:128]
         v = jnp.exp(mid - d[:128])
-        ud = jnp.exp(d[128:] - mid) * dy[128:]
+        ud = halves(jnp.exp(d[128:] - mid) * dy[128:])
         us[0] = us[0] + v * mul(st_s[g, 2], ud)
         dst_acc[g, 2] += mul(v * xs[:128], ud, NT)
         u = jnp.concatenate(us, 0)
         xu_acc[r] += to_heads(xx * u, spot)
-        dxa_o[r] = skip * dy + stc[r] * u
-    rows_o[0, 0:1] = dgain
-    rows_o[0, 1:2] = dskip
-    rows_o[0, 2:8] = jnp.zeros((6, 128), f32)
-    line.step(j)
-
-    @pl.when(j == PAIRS - 1)
-    def _(): std_o[...] = got[...]
+        dxa_s[j, r] = skip * dy + stc[r] * u
+    rows_o[j, 0:1] = dgain
+    rows_o[j, 1:2] = dskip
+    rows_o[j, 2:8] = jnp.zeros((6, 256), f32)
+    turned = jnp.concatenate(turned, 1)
+    for k in range(16):
+        at = 16 * j + k
+        q = at // 3
+        owner, sub = q // 2, lax.rem(q, 2)
+        rows = pl.ds(pl.multiple_of(lax.rem(at, 3) * 16, 16), 16)
+        lhs_s[1 + sub, owner // 8, lax.rem(owner // 4, 2), lax.rem(owner, 4), rows] = turned[16 * k:16 * k + 16]
 
 
 def conv_back(pad, dpad, dco, taps):
@@ -845,12 +879,9 @@
     return jnp.concatenate(grads, 0), din, prev
 
 
-def sb2_body(j, dxa, x, cin, halo, taps, std, ent, bcin, bchalo, bctaps, raw, ds, step, b_r, c_r, hp, dst_acc, dc_acc, dds_acc, xu_acc,
-             dcp_o, cg_o, hg_o, pad, pad2, dpad, dpad2, db_s, xut_s, de_s, prv, lst, got, out_sem, in_sem):
-    me = Place()
-
+def sb2_make(me, dcp_o, cg_o, hg_o, pad, pad2, dpad, dpad2, db_s, xut_s, de_s, prv, lst, edge_in, e_out, e_in):
     def edge(i):
-        return send(prv.at[i], got.at[i], out_sem.at[i], in_sem.at[i], me.z_peer(3))
+        return send(prv.at[i], edge_in.at[i], e_out.at[i], e_in.at[i], me.z_peer(3))
 
     def pass_edge(i, prev, din):
         for g in range(2):
@@ -860,38 +891,35 @@
         @pl.when(me.z > 0)
         def _(): edge(i).start()
 
-    @pl.when(j == 0)
-    def _():
-        greet((me.z_peer(1), me.z_peer(3)))
+    def start():
         for a in (db_s, xut_s, de_s):
             a[...] = jnp.zeros_like(a)
-    dsc = spread(rolled(ds[...], j))
-    stc = spread(rolled(step[...], j))
-    spot = spot_of(j)
-    fill_pad(pad, cin[0], halo[0])
-    dco = []
-    for g, co in enumerate(conv(pad, taps)):
-        r = slice(256 * g, 256 * g + 256)
-        d, xx, st, e = dsc[r], x[r], std[0, g].astype(f32), ent[0, g].astype(f32)
-        tail = jnp.exp(d[255:256] - d)
-        ut = tail * mul(b_r[r], st)
-        xut_s[r] += to_heads(xx * ut, spot)
-        db_s[r] += mul(tail * stc[r] * xx, st, NT)
-        row = jnp.sum(st * e, axis=0, keepdims=True)
-        de_s[g] += to_heads(jnp.broadcast_to(row, (8, 128)), spot)
-        dx = dxa[r] + stc[r] * ut
-        s = sig(co)
-        dco.append(dx * (s * (1.0 + co * (1.0 - s))))
-    grads, din, prev = conv_back(pad, dpad, dco, taps)
-    cg_o[j] = grads
-    p = j // 2
-    cols = pl.ds(pl.multiple_of(lax.rem(j, 2) * 128, 128), 128)
-    for g in range(2):
-        dcp_o[p, 256 * g:256 * g + 256, cols] = din[g].astype(bf)
-    pass_edge(j, prev, din)
-
-    @pl.when(j == PAIRS - 1)
-    def _():
+
+    def tile(j, dxa_s, x, cin, halo, taps, got, ent, ds, step, b_r):
+        dsc = spread(rolled(ds[...], j))
+        stc = spread(rolled(step[...], j))
+        spot = spot_of(j)
+        fill_pad(pad, cin[0], halo[0])
+        dco = []
+        for g, co in enumerate(conv(pad, taps)):
+            r = slice(256 * g, 256 * g + 256)
+            d, xx, st, e = dsc[r], x[r], got[j, g], ent[j, g]
+            tail = jnp.exp(d[255:256] - d)
+            ut = tail * mul(b_r[r], st)
+            xut_s[r] += to_heads(xx * ut, spot)
+            db_s[r] += mul(tail * stc[r] * xx, st, NT)
+            row = jnp.sum(st.astype(f32) * e.astype(f32), axis=0, keepdims=True)
+            de_s[g] += to_heads(jnp.broadcast_to(row, (8, 256)), spot)
+            dx = dxa_s[j, r] + stc[r] * ut
+            s = sig(co)
+            dco.append(dx * (s * (1.0 + co * (1.0 - s))))
+        grads, din, prev = conv_back(pad, dpad, dco, taps)
+        cg_o[j] = grads
+        for g in range(2):
+            dcp_o[j, 256 * g:256 * g + 256] = din[g].astype(bf)
+        pass_edge(j, prev, din)
+
+    def final(bcin, bchalo, bctaps, raw, ds, step, b_r, c_r, hp, dst_acc, dc_acc, dds_acc, xu_acc):
         fill_pad(pad2, bcin[0], bchalo[0])
         dco2 = []
         for g, co in enumerate(conv(pad2, bctaps)):
@@ -903,13 +931,10 @@
             s = sig(co)
             dco2.append(jnp.concatenate([db, dc], 1) * (s * (1.0 + co * (1.0 - s))))
         grads, din, prev = conv_back(pad2, dpad2, dco2, bctaps)
-        cg_o[24] = grads[:, :128]
-        cg_o[25] = grads[:, 128:]
+        cg_o[12] = grads
         for g in range(2):
             dcp_o[12, 256 * g:256 * g + 256] = din[g].astype(bf)
-        for h in range(2):
-            lanes = slice(128 * h, 128 * h + 128)
-            pass_edge(PAIRS + h, [a[:, lanes] for a in prev], [a[:, lanes] for a in din])
+        pass_edge(TILES, prev, din)
         st = step[...]
         xut = xut_s[...]
         speed = -jnp.exp(hp[0:1])
@@ -938,15 +963,16 @@
         def _():
             def patch(i, _):
                 edge(i).wait_recv()
-                at = pl.ds(pl.multiple_of(lax.rem(i, 2) * 128, 128), 128)
                 for g in range(2):
-                    rows = lst[i, 8 * g:8 * g + 8] + got[i, 8 * g:8 * g + 8].astype(f32)
-                    dcp_o[i // 2, 256 * g + 248:256 * g + 256, at] = rows.astype(bf)
+                    rows = lst[i, 8 * g:8 * g + 8] + edge_in[i, 8 * g:8 * g + 8].astype(f32)
+                    dcp_o[i, 256 * g + 248:256 * g + 256] = rows.astype(bf)
                 return 0
-            lax.fori_loop(0, PAIRS + 2, patch, 0)
+            lax.fori_loop(0, TILES + 1, patch, 0)
 
         @pl.when(me.z > 0)
-        def _(): lax.fori_loop(0, PAIRS + 2, lambda i, _: (edge(i).wait_send(), 0)[1], 0)
+        def _(): lax.fori_loop(0, TILES + 1, lambda i, _: (edge(i).wait_send(), 0)[1], 0)
+
+    return start, tile, final
 
 
 S = jax.ShapeDtypeStruct
@@ -954,86 +980,67 @@
 
 
 def const(*shape):
-    return pl.BlockSpec(shape, lambda j: (0,) * len(shape))
-
-
-TILE = pl.BlockSpec((1, 512, 128), lambda j: (j // 2, 0, lax.rem(j, 2)))
-HALO = pl.BlockSpec((1, 16, 128), lambda j: (j // 2, 32, lax.rem(j, 2)))
-ZT = pl.BlockSpec((1, 512, 128), lambda j: (14 + j // 2, 0, lax.rem(j, 2)))
-BC = pl.BlockSpec((1, 512, 256), lambda j: (12, 0, 0))
-BCH = pl.BlockSpec((1, 16, 256), lambda j: (12, 32, 0))
-RAW = pl.BlockSpec((1, 512, 128), lambda j: (13, 0, 0))
-TAP = pl.BlockSpec((8, 128), lambda j: (0, j))
-BCT = pl.BlockSpec((8, 256), lambda j: (0, 12))
-GAIN = pl.BlockSpec((8, 128), lambda j: (0, 38 + j))
+    return pl.BlockSpec(shape, lambda j: (0,) * len(shape), pipeline_mode=pl.Buffered(1))
+
+
+TILE = pl.BlockSpec((1, 512, 256), lambda j: (j, 0, 0))
+HALO = pl.BlockSpec((1, 16, 256), lambda j: (j, 32, 0))
+ZT = pl.BlockSpec((1, 512, 256), lambda j: (14 + j, 0, 0))
+BC = pl.BlockSpec((1, 512, 256), lambda j: (12, 0, 0), pipeline_mode=pl.Buffered(1))
+BCH = pl.BlockSpec((1, 16, 256), lambda j: (12, 32, 0), pipeline_mode=pl.Buffered(1))
+RAW = pl.BlockSpec((1, 512, 128), lambda j: (13, 0, 0), pipeline_mode=pl.Buffered(1))
+TAP = pl.BlockSpec((8, 256), lambda j: (0, j))
+BCT = pl.BlockSpec((8, 256), lambda j: (0, 12), pipeline_mode=pl.Buffered(1))
+GAIN = pl.BlockSpec((8, 256), lambda j: (0, 19 + j))
 HP = const(8, 128)
-COL = pl.BlockSpec((512, 128), lambda j: (0, j))
-ST = pl.BlockSpec((1, 2, 128, 128), lambda j: (j, 0, 0, 0))
-DN = pl.BlockSpec((1, 512, 128), lambda j: (j // 3, 0, lax.rem(j, 3)))
+COL = pl.BlockSpec((512, 256), lambda j: (0, j))
+ST = pl.BlockSpec((1, 2, 128, 256), lambda j: (j, 0, 0, 0))
+DN = pl.BlockSpec((2, 512, 128), lambda j: (j, 0, 0))
 TOK = const(512, 128)
-TOKT = const(24, 8, 512)
+TOKT = const(12, 8, 512)
 
 
 def call(body, name, in_specs, out_shape, out_specs, scratch, args, cid=None):
     def kernel(*refs):
         body(pl.program_id(0), *refs)
     return pl.pallas_call(
-        kernel, grid=(PAIRS,), in_specs=in_specs, out_specs=out_specs, out_shape=out_shape, scratch_shapes=scratch,
+        kernel, grid=(TILES,), in_specs=in_specs, out_specs=out_specs, out_shape=out_shape, scratch_shapes=scratch,
         compiler_params=pltpu.CompilerParams(vmem_limit_bytes=60 << 20, collective_id=cid, has_side_effects=cid is not None), name=name,
     )(*args)
 
 
 def sf1(proj, par, hp):
     return call(sf1_body, "sf1", [TILE, HALO, BC, BCH, RAW, TAP, BCT, HP],
-        (S((512, 3072), f32), S((512, 3072), f32), S((24, 2, 128, 128), bf), S((512, 128), f32), S((512, 128), f32), S((24, 8, 512), f32), S((512, 128), f32), S((512, 128), f32)),
-        (COL, COL, const(24, 2, 128, 128), TOK, TOK, TOKT, TOK, TOK),
-        [V((2, 264, 128), f32), V((2, 264, 256), f32), V((2, 3, 128, 128), f32), V((2, 128, 256), f32)] + Chain.scratch(),
+        (S((512, 3072), f32), S((512, 3072), f32), S((12, 2, 128, 256), bf), S((512, 128), f32), S((512, 128), f32), S((12, 8, 512), f32), S((512, 128), f32), S((512, 128), f32)),
+        (COL, COL, const(12, 2, 128, 256), TOK, TOK, TOKT, TOK, TOK),
+        [V((2, 264, 256), f32), V((2, 264, 256), f32), V((2, 3, 128, 128), f32), V((2, 128, 256), f32)] + Chain.scratch(),
         (proj, proj, proj, proj, proj, par, par, hp), 4)
 
 
 def sf2(yi, x, ent, proj, dn, par, ds, c, hp):
     return call(sf2_body, "sf2", [COL, COL, ST, ZT, DN, GAIN, TOK, TOK, HP],
         (S((512, 3072), f32), S((2, 512, 128), f32)), (COL, const(2, 512, 128)),
-        [V((512, 128), f32), V((512, 128), f32)],
+        [V((512, 256), f32), V((512, 256), f32)],
         (yi, x, ent, proj, dn, par, ds, c, hp))
-
-
-def sb1(mixed, proj, dn, x, ent, par, ds, step, dst, b, c, hp, rq):
-    return call(sb1_body, "sb1", [COL, ZT, DN, COL, ST, GAIN, TOK, TOK, TOKT, TOK, TOK, HP, const(2, 512, 128)],
-        (S((512, 3072), f32), S((12, 512, 256), bf), S((512, 3072), bf), S((24, 2, 128, 128), bf), S((24, 8, 128), f32),
-         S((2, 3, 128, 128), f32), S((512, 128), f32), S((512, 128), f32), S((512, 128), f32)),
-        (COL, pl.BlockSpec((1, 512, 128), lambda j: (j // 2, 0, lax.rem(j, 2))), COL, const(24, 2, 128, 128), pl.BlockSpec((1, 8, 128), lambda j: (j, 0, 0)),
-         const(2, 3, 128, 128), TOK, TOK, TOK),
-        [V((2, 3, 128, 128), f32), V((2, 128, 256), f32)] + Chain.scratch(),
-        (mixed, proj, dn, x, ent, par, ds, step, dst, b, c, hp, rq), 5)
-
-
-def sb2(dxa, x, proj, par, std, ent, ds, step, b, c, hp, acc):
-    return call(sb2_body, "sb2", [COL, COL, TILE, HALO, TAP, ST, ST, BC, BCH, BCT, RAW, TOK, TOK, TOK, TOK, HP, const(2, 3, 128, 128), TOK, TOK, TOK],
-        (S((14, 512, 256), bf), S((26, 8, 128), f32), S((8, 128), f32)),
-        (const(14, 512, 256), const(26, 8, 128), HP),
-        [V((2, 264, 128), f32), V((2, 264, 256), f32), V((2, 272, 128), f32), V((2, 272, 256), f32), V((512, 128), f32), V((512, 128), f32), V((2, 8, 128), f32),
-         V((26, 16, 128), bf), V((26, 16, 128), f32), V((26, 16, 128), bf), pltpu.SemaphoreType.DMA((26,)), pltpu.SemaphoreType.DMA((26,))],
-        (dxa, x, proj, proj, par, std, ent, proj, proj, par, proj, ds, step, b, c, hp) + tuple(acc), 6)
 
 
 class Reduce:
     def __init__(self, me, n, rows, refs, skew):
-        self.me, self.n, self.rows, self.sk, self.slots = me, n, rows, skew, skew + 1
+        self.me, self.n, self.rows, self.sk, self.slots, self.ring = me, n, rows, skew, skew + 1, skew + 2
         (self.own0, self.own1, self.own2, self.own3, self.s0, self.s1, self.s2, self.s3, self.r0, self.r1, self.r2, self.r3,
-         self.o0, self.o1, self.o2, self.o3, self.i0, self.i1, self.i2, self.i3) = refs
+         self.o0, self.o1, self.o2, self.o3, self.i0, self.i1, self.i2, self.i3, self.free) = refs
 
     @staticmethod
     def scratch(n, rows, skew):
         V, D, k = pltpu.VMEM, pltpu.SemaphoreType.DMA, skew + 1
         z = 4 * rows
         return [V((k, 2, 2, 2, z, 128), f32), V((k, 2, 2, z, 128), f32), V((k, 2, z, 128), f32), V((k, 2, rows, 128), f32),
-                V((k, 2, 2, 2, z, 128), bf), V((k, 2, 2, z, 128), bf), V((k, 2, z, 128), bf), V((k, 3, 2, rows, 128), bf),
-                V((n, 2, 2, 2, z, 128), bf), V((n, 2, 2, z, 128), bf), V((n, 2, z, 128), bf), V((n, 3, 2, rows, 128), bf),
-                D((k,)), D((k, 2)), D((k, 2)), D((k, 3)), D((n,)), D((n, 2)), D((n, 2)), D((n, 3))]
+                V((k, 2, 2, 2, z, 128), f32), V((k, 2, 2, z, 128), bf), V((k, 2, z, 128), bf), V((k, 3, 2, rows, 128), bf),
+                V((skew + 2, 2, 2, 2, z, 128), f32), V((n, 2, 2, z, 128), bf), V((n, 2, z, 128), bf), V((n, 3, 2, rows, 128), bf),
+                D((k,)), D((k, 2)), D((k, 2)), D((k, 3)), D((n,)), D((n, 2)), D((n, 2)), D((n, 3)), pltpu.SemaphoreType.REGULAR]
 
     def c0(self, i, s):
-        return send(self.s0.at[s], self.r0.at[i], self.o0.at[s], self.i0.at[i], self.me.core_peer)
+        return send(self.s0.at[s], self.r0.at[lax.rem(i, self.ring)], self.o0.at[s], self.i0.at[i], self.me.core_peer)
 
     def c1(self, i, s, h):
         return send(self.s1.at[s, h], self.r1.at[i, h], self.o1.at[s, h], self.i1.at[i, h], (self.me.x_peer, self.me.y_peer)[h])
@@ -1057,9 +1064,11 @@
         def zero(i, s):
             @pl.when(i >= ns)
             def _(): self.c0(i, s).wait_send()
-            part = product(i, 1 - c).astype(bf)
+            part = product(i, 1 - c)
             for h in range(2):
                 self.s0[s, h] = part[..., h * 128:(h + 1) * 128]
+            @pl.when(i >= self.ring)
+            def _(): pl.semaphore_wait(self.free, 1)
             self.c0(i, s).start()
             part = product(i, c)
             for h in range(2):
@@ -1067,18 +1076,20 @@
 
         def first(i, s):
             own0, r0, own1 = self.own0, self.r0, self.own1
+            q = lax.rem(i, self.ring)
             @pl.when(i >= ns)
             def _():
                 for h in range(2): self.c1(i, s, h).wait_send()
             self.c0(i, s).wait_recv()
             for a in range(2):
-                self.s1[s, 0, a] = (own0[s, 0, a, 1 - x] + r0[i, 0, a, 1 - x].astype(f32)).astype(bf)
+                self.s1[s, 0, a] = (own0[s, 0, a, 1 - x] + r0[q, 0, a, 1 - x]).astype(bf)
             self.c1(i, s, 0).start()
-            self.s1[s, 1] = (own0[s, 1, 1 - y] + r0[i, 1, 1 - y].astype(f32)).astype(bf)
+            self.s1[s, 1] = (own0[s, 1, 1 - y] + r0[q, 1, 1 - y]).astype(bf)
             self.c1(i, s, 1).start()
             for a in range(2):
-                own1[s, 0, a] = own0[s, 0, a, x] + r0[i, 0, a, x].astype(f32)
-            own1[s, 1] = own0[s, 1, y] + r0[i, 1, y].astype(f32)
+                own1[s, 0, a] = own0[s, 0, a, x] + r0[q, 0, a, x]
+            own1[s, 1] = own0[s, 1, y] + r0[q, 1, y]
+            pl.semaphore_signal(self.free, inc=1, device_id=me.core_peer, device_id_type=MESH)
 
         def second(i, s):
             own1, r1 = self.own1, self.r1
@@ -1112,7 +1123,9 @@
             for k in range(3): acc = acc + self.r3[i, k].astype(f32)
             out_ref[i] = acc
 
-        stage(0, zero); stage(1, first); stage(2, second); stage(3, third); stage(4, last)
+        if product is not None:
+            stage(0, zero)
+        stage(1, first); stage(2, second); stage(3, third); stage(4, last)
 
     def finish(self):
         for j in range(self.slots):
@@ -1123,64 +1136,134 @@
                 self.c1(i, s, h).wait_send()
                 self.c2(i, s, h).wait_send()
             for k in (1, 2, 3): self.c3(i, s, k).wait_send()
-
-
-def prod(lhs_ref, c, rhs, R):
-    lhs = lhs_ref[:, c].reshape(16 * R, 512)
-    return jnp.dot(lhs, rhs, preferred_element_type=f32).reshape(2, 2, 4 * R, 256)
-
-
-def out_call(out_low, out_low_t, cot, tokens, wout, collective_id, skew=2):
-    n, R = 6, 96
-
-    def kernel(ol, lhs, cot_ref, tok, w_hbm, sums, blk, wbuf, wsem, *refs):
+        pl.semaphore_wait(self.free, self.ring)
+
+
+def one_time(*shape):
+    return pl.BlockSpec(shape, lambda j: (0,) * len(shape), pipeline_mode=pl.Buffered(1))
+
+
+def phase_one(j):
+    return jnp.minimum(j, TILES - 1)
+
+
+def phase_two(j):
+    return jnp.maximum(j - TILES, 0)
+
+
+def back_call(mixed, proj, dn, x, par, ent, ds, step, dst, b, c, hp, rq, low_t, cot, collective_id):
+    n, R, sk = 24, 48, 1
+
+    def kernel(mixed, z, dn, x, gain, cin, halo, taps, ent, ds, step, dst, b_r, c_r, hp, rq, bcin, bchalo, bctaps, raw, low_t, cot,
+               dz_o, ol_o, dcp_o, cg_o, hg_o, rows_o, sums,
+               dst_acc, dc_acc, dds_acc, xu_acc, st_s, ct_s, got, part, out, out_sem, in_sem,
+               pad, pad2, dpad, dpad2, db_s, xut_s, de_s, prv, lst, edge_in, e_out, e_in,
+               dxa_s, dz_s, rhs, lhs_s, *refs):
+        j = pl.program_id(0)
         me = Place()
-        greet(me.near())
-        red = Reduce(me, n, R, refs, skew)
-        def wcopy(i): return pltpu.make_async_copy(w_hbm.at[i], wbuf.at[lax.rem(i, 2)], wsem.at[lax.rem(i, 2)])
-        wcopy(0).start()
-
-        def cols(i): return pl.ds(pl.multiple_of(i * 256, 256), 256)
-        def loop(it, _):
-            red.step(it, lambda i, c: prod(lhs, c, cot_ref[:, cols(i)], R), sums)
-            @pl.when(it < n)
-            def _():
-                wcopy(it).wait()
-                @pl.when(it + 1 < n)
-                def _(): wcopy(it + 1).start()
-                s = lax.rem(it, 2)
-                w = jnp.concatenate([wbuf[s, h].reshape(3072, 128) for h in range(2)], axis=1)
-                branch = jnp.dot(ol[...], w, preferred_element_type=f32)
-                blk[:, cols(it)] = (tok[:, cols(it)].astype(f32) + branch).astype(bf)
-            return 0
-        lax.fori_loop(0, n + 4 * skew, loop, 0)
-        red.finish()
-
-    V, D, Sd = pltpu.VMEM, pltpu.SemaphoreType.DMA, jax.ShapeDtypeStruct
-    vm = pl.BlockSpec(memory_space=pltpu.VMEM)
+        line = Chain(me, -1, got, part, out, out_sem, in_sem, keeper(ds), 1)
+        red = Reduce(me, n, R, refs, sk)
+        two_start, two_tile, two_final = sb2_make(me, dcp_o, cg_o, hg_o, pad, pad2, dpad, dpad2, db_s, xut_s, de_s, prv, lst, edge_in, e_out, e_in)
+
+        def rs(it):
+            outer = it // 12
+            li = outer * (1 + lax.rem(it, 2))
+            @pl.when(it < 12)
+            def _(): rhs[...] = dz_s[...]
+            @pl.when((it >= 12) & (it < n))
+            def _(): rhs[...] = cot[:, pl.ds(pl.multiple_of((it - 12) // 2 * 256, 256), 256)]
+            red.step(it, lambda i, c: jnp.dot(lhs_s[li, :, c].reshape(16 * R, 512), rhs[...], preferred_element_type=f32).reshape(2, 2, 4 * R, 256), sums)
+
+        @pl.when(j == 0)
+        def _():
+            greet(me.near())
+            line.start()
+            sb1_start(b_r, c_r, dst_acc, dc_acc, dds_acc, xu_acc, st_s, ct_s)
+            lhs_s[0] = low_t[...]
+
+        @pl.when(j < TILES)
+        def _():
+            sb1_tile(j, mixed, z, dn, x, ent, gain, ds, step, dst, hp, rq, dxa_s, dz_o, dz_s, ol_o, lhs_s, rows_o,
+                     dst_acc, dc_acc, dds_acc, xu_acc, st_s, ct_s, part)
+        line.step(j, False)
+
+        @pl.when(j == TILES)
+        def _(): two_start()
+
+        @pl.when(j >= TILES)
+        def _(): two_tile(j - TILES, dxa_s, x, cin, halo, taps, got, ent, ds, step, b_r)
+
+        rs(j)
+
+        @pl.when(j == 2 * TILES - 1)
+        def _():
+            two_final(bcin, bchalo, bctaps, raw, ds, step, b_r, c_r, hp, dst_acc, dc_acc, dds_acc, xu_acc)
+            line.finish()
+            lax.fori_loop(n, n + 4 * sk, lambda it, _: (rs_drain(red, it, sums), 0)[1], 0)
+            red.finish()
+
+    D = pltpu.SemaphoreType.DMA
+    p1, p2 = phase_one, phase_two
+    xt = lambda j: jnp.where(j < TILES, j, j - TILES)
+    tok = one_time(512, 128)
+    in_specs = [
+        pl.BlockSpec((512, 256), lambda j: (0, p1(j))),
+        pl.BlockSpec((1, 512, 256), lambda j: (14 + p1(j), 0, 0)),
+        pl.BlockSpec((2, 512, 128), lambda j: (p1(j), 0, 0)),
+        pl.BlockSpec((512, 256), lambda j: (0, xt(j))),
+        pl.BlockSpec((8, 256), lambda j: (0, 19 + p1(j))),
+        pl.BlockSpec((1, 512, 256), lambda j: (p2(j), 0, 0)),
+        pl.BlockSpec((1, 16, 256), lambda j: (p2(j), 32, 0)),
+        pl.BlockSpec((8, 256), lambda j: (0, p2(j))),
+        one_time(12, 2, 128, 256), tok, tok, one_time(12, 8, 512), tok, tok, one_time(8, 128), one_time(2, 512, 128),
+        BC, BCH, BCT, RAW, one_time(4, 2, 4, 48, 512), one_time(512, 1536),
+    ]
+    out_specs = (
+        pl.BlockSpec((1, 512, 256), lambda j: (p1(j), 0, 0)),
+        pl.BlockSpec((512, 256), lambda j: (0, p1(j))),
+        one_time(14, 512, 256), one_time(13, 8, 256), one_time(8, 128), one_time(12, 8, 256), one_time(24, 2, 48, 128),
+    )
+    out_shape = (S((12, 512, 256), bf), S((512, 3072), bf), S((14, 512, 256), bf), S((13, 8, 256), f32), S((8, 128), f32), S((12, 8, 256), f32), S((24, 2, 48, 128), f32))
+    scratch = (
+        [V((2, 3, 128, 128), f32), V((512, 128), f32), V((512, 128), f32), V((512, 128), f32), V((2, 3, 128, 128), f32), V((2, 128, 256), f32)]
+        + Chain.scratch()
+        + [V((2, 264, 256), f32), V((2, 264, 256), f32), V((2, 272, 256), f32), V((2, 272, 256), f32), V((512, 128), f32), V((512, 128), f32), V((2, 8, 128), f32),
+           V((13, 16, 256), bf), V((13, 16, 256), f32), V((13, 16, 256), bf), D((13,)), D((13,))]
+        + [V((12, 512, 256), f32), V((512, 256), bf), V((512, 256), bf), V((3, 4, 2, 4, 48, 512), bf)]
+        + Reduce.scratch(n, R, sk)
+    )
     return pl.pallas_call(
-        kernel, out_shape=(Sd((n, 2, R, 128), f32), Sd((512, 1536), bf)),
-        in_specs=[vm] * 4 + [pl.BlockSpec(memory_space=pl.ANY)], out_specs=(vm, vm),
-        scratch_shapes=[V((2, 2, 2, 2, 2, 384, 128), bf), D((2,))] + Reduce.scratch(n, R, skew),
-        compiler_params=pltpu.CompilerParams(collective_id=collective_id, has_side_effects=True, vmem_limit_bytes=63 << 20), name="outgrad",
-    )(out_low, out_low_t.reshape(4, 2, 384, 512), cot, tokens, wout)
-
-
-def in_call(low_t, dcp, dz, win, tok, cot, par, cg, rows, hg, collective_id, skew=2):
-    n, R = 26, 48
-
-    def kernel(lhs, dcp_ref, dz_ref, w_hbm, tok, cot, par_ref, cg_ref, rows_ref, hg_ref, sums, tg, small_o,
-               wbuf, wsem, dp, dn, flat, mail, box, m_out, m_in, *refs):
+        kernel, grid=(2 * TILES,), in_specs=in_specs, out_specs=out_specs, out_shape=out_shape, scratch_shapes=scratch,
+        compiler_params=pltpu.CompilerParams(vmem_limit_bytes=63 << 20, collective_id=collective_id, has_side_effects=True), name="back",
+    )(mixed, proj, dn, x, par, proj, proj, par, ent, ds, step, dst, b, c, hp, rq, proj, proj, par, proj, low_t.reshape(4, 2, 4, 48, 512), cot)
+
+
+def rs_drain(red, it, sums):
+    red.step(it, None, sums)
+
+
+def end_call(low_t, dcp, dz, ol, win, wout, tok, cot, par, cg, rows, hg, collective_id, skew=2):
+    n, R = 14, 48
+
+    def kernel(lhs, dcp_ref, dz_ref, ol_ref, win_hbm, wout_hbm, tok, cot, par_ref, cg_ref, rows_ref, hg_ref, sums, blk, tg, small_o,
+               wbuf, wsem, obuf, osem, dn, flat, mail, box, m_out, m_in, *refs):
         me = Place()
+        def wcopy(t, p): return pltpu.make_async_copy(win_hbm.at[p], wbuf.at[lax.rem(t, 2), 0 if p is t else 1], wsem.at[lax.rem(t, 2), 0 if p is t else 1])
+        def ocopy(i): return pltpu.make_async_copy(wout_hbm.at[i], obuf.at[lax.rem(i, 2)], osem.at[lax.rem(i, 2)])
+        def fetch(t):
+            wcopy(t, t).start()
+            @pl.when(t < 12)
+            def _(): wcopy(t, t + 14).start()
+        fetch(jnp.int32(0))
+        ocopy(jnp.int32(0)).start()
+        ocopy(jnp.int32(1)).start()
         bar = pltpu.get_barrier_semaphore()
-        def sig(k, _):
+        def sg(k, _):
             pl.semaphore_signal(bar, inc=1, device_id=me.any_peer(k), device_id_type=MESH)
             return 0
-        lax.fori_loop(1, 32, sig, 0)
+        lax.fori_loop(1, 32, sg, 0)
         pl.semaphore_wait(bar, 31)
         red = Reduce(me, n, R, refs, skew)
-        def wcopy(i): return pltpu.make_async_copy(w_hbm.at[i], wbuf.at[lax.rem(i, 2)], wsem.at[lax.rem(i, 2)])
-        wcopy(0).start()
         def post(k):
             to = lax.rem(me.line + k, 32)
             return send(mail.at[to], box.at[k - 1], m_out.at[k - 1], m_in.at[k - 1], me.any_peer(k))
@@ -1197,11 +1280,11 @@
                 return acc + jnp.sum(d * xf * h, axis=0, keepdims=True)
             norm = lax.fori_loop(0, 8, block, jnp.zeros((1, 1536), f32))
             flat[...] = jnp.zeros_like(flat)
-            for j in range(26):
-                flat[0:5, 128 * j:128 * j + 128] = cg_ref[j, 0:5]
+            for j in range(13):
+                flat[0:5, 256 * j:256 * j + 256] = cg_ref[j, 0:5]
             flat[5:6, 0:1536] = norm
-            for j in range(24):
-                flat[6:7, 128 * j:128 * j + 128] = rows_ref[j, 0:1]
+            for j in range(12):
+                flat[6:7, 256 * j:256 * j + 256] = rows_ref[j, 0:1]
             for o in range(32):
                 b = [(o * w // 128) * 128 for w in (104, 48, 96)]
                 mail[o, 0:5] = flat[0:5, b[0]:b[0] + 256]
@@ -1210,26 +1293,39 @@
                 mail[o, 7:8] = hg_ref[0:1]
             lax.fori_loop(1, 32, lambda k, _: (post(k).start(), 0)[1], 0)
 
+        def dgrad(t, q, dp):
+            s = lax.rem(t, 2)
+            w = jnp.concatenate([wbuf[s, q, h].reshape(1536, 128) for h in range(2)], axis=1)
+            return lax.dot_general(dp, w, (((1,), (1,)), ((), ())), preferred_element_type=f32)
+
         def loop(it, _):
-            @pl.when(it < 14)
-            def _(): dp[...] = dcp_ref[lax.rem(it, 14)]
-            @pl.when((it >= 14) & (it < n))
-            def _(): dp[...] = dz_ref[lax.rem(it + 12 - 14, 12)]
-            red.step(it, lambda i, c: prod(lhs, c, dp[...], R), sums)
+            red.step(it, lambda i, c: jnp.dot(lhs[:, c].reshape(16 * R, 512), dcp_ref[i], preferred_element_type=f32).reshape(2, 2, 4 * R, 256), sums)
             @pl.when(it < n)
             def _():
-                wcopy(it).wait()
                 @pl.when(it + 1 < n)
-                def _(): wcopy(it + 1).start()
-                s = lax.rem(it, 2)
-                w = jnp.concatenate([wbuf[s, h].reshape(1536, 128) for h in range(2)], axis=1)
-                r = lax.dot_general(dp[...], w, (((1,), (1,)), ((), ())), preferred_element_type=f32)
+                def _(): fetch(it + 1)
+                wcopy(it, it).wait()
+                r = dgrad(it, 0, dcp_ref[it])
                 @pl.when(it == 0)
                 def _(): dn[...] = r
                 @pl.when(it > 0)
                 def _(): dn[...] += r
+            @pl.when(it < 12)
+            def _():
+                wcopy(it, it + 14).wait()
+                dn[...] += dgrad(it, 1, dz_ref[it])
             @pl.when(it == n)
             def _(): tail()
+            @pl.when((it >= n) & (it < n + 6))
+            def _():
+                i = it - n
+                ocopy(i).wait()
+                s = lax.rem(i, 2)
+                w = jnp.concatenate([obuf[s, h].reshape(3072, 128) for h in range(2)], axis=1)
+                at = pl.ds(pl.multiple_of(i * 256, 256), 256)
+                blk[:, at] = (tok[:, at].astype(f32) + jnp.dot(ol_ref[...], w, preferred_element_type=f32)).astype(bf)
+                @pl.when(i + 2 < 6)
+                def _(): ocopy(i + 2).start()
             return 0
         lax.fori_loop(0, n + 4 * skew, loop, 0)
         small_o[...] = mail[me.line]
@@ -1240,15 +1336,16 @@
         lax.fori_loop(1, 32, take, 0)
         red.finish()
 
-    V, D, Sd = pltpu.VMEM, pltpu.SemaphoreType.DMA, jax.ShapeDtypeStruct
-    vm = pl.BlockSpec(memory_space=pltpu.VMEM)
+    D, Sd = pltpu.SemaphoreType.DMA, jax.ShapeDtypeStruct
+    vm, hb = pl.BlockSpec(memory_space=pltpu.VMEM), pl.BlockSpec(memory_space=pl.ANY)
     return pl.pallas_call(
-        kernel, out_shape=(Sd((n, 2, R, 128), f32), Sd((512, 1536), f32), Sd((8, 256), f32)),
-        in_specs=[vm] * 3 + [pl.BlockSpec(memory_space=pl.ANY)] + [vm] * 6, out_specs=(vm, vm, vm),
-        scratch_shapes=[V((2, 2, 2, 2, 2, 192, 128), bf), D((2,)), V((512, 256), bf), V((512, 1536), f32), V((8, 3584), f32), V((32, 8, 256), f32), V((31, 8, 256), f32), D((31,)), D((31,))]
+        kernel, out_shape=(Sd((n, 2, R, 128), f32), Sd((512, 1536), bf), Sd((512, 1536), f32), Sd((8, 256), f32)),
+        in_specs=[vm] * 4 + [hb] * 2 + [vm] * 6, out_specs=(vm, vm, vm, vm),
+        scratch_shapes=[V((2, 2, 2, 2, 2, 2, 192, 128), bf), D((2, 2)), V((2, 2, 2, 2, 2, 384, 128), bf), D((2,)),
+                        V((512, 1536), f32), V((8, 3584), f32), V((32, 8, 256), f32), V((31, 8, 256), f32), D((31,)), D((31,))]
         + Reduce.scratch(n, R, skew),
-        compiler_params=pltpu.CompilerParams(collective_id=collective_id, has_side_effects=True, vmem_limit_bytes=63 << 20), name="ingrad",
-    )(low_t.reshape(4, 2, 192, 512), dcp, dz, win, tok, cot, par, cg, rows, hg)
+        compiler_params=pltpu.CompilerParams(collective_id=collective_id, has_side_effects=True, vmem_limit_bytes=63 << 20), name="end",
+    )(low_t.reshape(4, 2, 192, 512), dcp, dz, ol, win, wout, tok, cot, par, cg, rows, hg)
 
 
 def fast(adamw, tokens, cotangent, in_proj, in_mom, in_var, out_proj, out_mom, out_var, conv_params, conv_mom, conv_var,
@@ -1261,15 +1358,13 @@
     hp = jnp.pad(head_params, ((0, 5), (0, 80)))
     x, yi, ent, step, ds, dst, b, c = sf1(proj, par, hp)
     mixed, rq = sf2(yi, x, ent, proj, dn, par, ds, c, hp)
-    dxa, dz, ol, std, rows, *acc = sb1(mixed, proj, dn, x, ent, par, ds, step, dst, b, c, hp, rq)
-    dcp, cg, hg = sb2(dxa, x, proj, par, std, ent, ds, step, b, c, hp, acc)
-    out_sums, block = out_call(ol, ol.T, cot, tok, wout, 2)
+    low_t = low.T
+    dz, ol, dcp, cg, hg, rows, sums = back_call(mixed, proj, dn, x, par, ent, ds, step, dst, b, c, hp, rq, low_t, cot, 5)
     skip = jnp.sum(rows[:, 1].reshape(48, 64), axis=1)
     heads = jnp.pad(jnp.concatenate([hg[0, :48], skip, hg[2, :48]])[None], ((0, 7), (0, 112)))
-    in_sums, tokens_grad, small_sum = in_call(low.T, dcp, dz, win, tok, cot, par, cg, rows, heads, 3)
-    out_grad = out_sums.transpose(2, 0, 1, 3).reshape(96, 1536)
-    in_sums = in_sums.transpose(2, 0, 1, 3).reshape(48, 6656)
-    in_grad = jnp.concatenate([in_sums[:, 3584:], in_sums[:, :3376]], axis=1)
+    last, block, tokens_grad, small_sum = end_call(low_t, dcp, dz, ol, win, wout, tok, cot, par, cg, rows, heads, 3)
+    out_grad = sums[12:].reshape(6, 2, 2, 48, 128).transpose(1, 3, 0, 2, 4).reshape(96, 1536)
+    in_grad = jnp.concatenate([sums[:12].transpose(2, 0, 1, 3).reshape(48, 3072), last.transpose(2, 0, 1, 3).reshape(48, 3584)[:, :304 + 3072]], axis=1)
     tokens_grad = tokens_grad.reshape(2, 256, 1536)
     mine = lambda row, n, w: lax.dynamic_slice(small_sum, (row, lax.rem(line * w, 128)), (n, w))
     conv_grad, norm_grad, gate_grad = mine(0, 5, 104), mine(5, 1, 48)[0], mine(6, 1, 96)[0]

time: 562 us -> 500 us (0.89)
  Pallas kernels: 521 us -> 461 us
    pallas_call x6 -> x4, Pallas kernels: 347 us -> 287 us  [the longest x1 153 us: back_call(): pl.pallas_call(kernel, grid=(2 * TILES,), in_specs=in_specs, out_specs=ou...]
where the time goes in v3:
time: 500 us; the launch traced here: 499 us
  Pallas kernels  461 us (92%)
  local copies, waits for them, and re-layouts  25.1 us (5%)
  other arithmetic  11.5 us (2%)
    pallas_call x1, Pallas kernels, gather_call(): pl.pallas_call(kernel, out_shape=(S((NI, TE, 256), f32), S(wi, bf), S(wo,...  174 us
    pallas_call x1, Pallas kernels, back_call(): pl.pallas_call(kernel, grid=(2 * TILES,), in_specs=in_specs, out_specs=ou...  153 us
    pallas_call x1, Pallas kernels, end_call(): pl.pallas_call(kernel, out_shape=(Sd((n, 2, R, 128), f32), Sd((512, 1536)...  75.7 us
    pallas_call x2, Pallas kernels, call(): pl.pallas_call(kernel, grid=(TILES,), in_specs=in_specs, out_specs=out_sp...  57.9 us
    sub x6, other arithmetic, adamw(): weight - learn_rate * (mean_hat / (jnp.sqrt(var_hat) + adam_eps) + decay_...  10.1 us

profile of v3, /device:TPU:0, one launch (start us, length us, event | category | flops | bytes accessed | tf_op | source)
XLA Modules:
  0.0 499.0 jit_solution(11758303325449161483)
XLA Ops:
  0.7 0.0 copy-start
  0.7 1.4 pad.13.refs_7_.refs_8_.hp
  2.1 1.5 dynamic_update_slice.9
  3.6 0.8 dynamic_update_slice.10
  4.4 0.8 dynamic_update_slice.11.small_ref
  5.2 0.0 copy-start.11
  5.2 0.8 slice.32
  6.0 0.6 pad_bitcast_fusion.edge_ref
  6.6 1.1 convert_element_type.13
  7.7 0.1 reshape.92
  7.8 0.8 copy.59
  8.6 0.1 convert_element_type.12
  8.7 0.2 concatenate.9
  8.9 0.1 reshape.91
  9.1 0.9 copy.58
  10.0 174.4 %gather.1 = (f32[26,528,256]{2,1,0:T(8,128)}, bf16[26,2,2,2,2,192,128]{6,5,4,3,2,1,0:T(8,128)(2,1)}, bf16[6,2,2,2,2,384,128]{6,5,4,3,2,1,0:T(8,128)(2,1)}, bf16[...) custom-call(bf16[26,2,48,128]{3,2,1,0:T(8,128)(2,1)} %bitcast.42, ...), custom_call_target="tpu_custom_call" | custom-call | tf_op jit(solution)/shard_map/gather/pallas_call | solution.py:507
  184.4 2.6 copy.51
  187.0 39.2 %sf1.1 = (f32[512,3072]{1,0:T(8,128)}, f32[512,3072]{1,0:T(8,128)}, bf16[12,2,128,256]{3,2,1,0:T(8,128)(2,1)}, f32[512,128]{1,0:T(8,128)}, f32[512,128]{1,0:T(8,...) custom-call(f32[26,528,256]{2,1,0:T(8,128)} %get-tuple-element.54.refs_0_.refs_1_.refs_2_.refs_3_.refs_4_.z.cin., ...), custom_call_target="tpu_custom_call" | custom-call | tf_op jit(solution)/shard_map/sf1/pallas_call | solution.py:1006
  226.2 18.8 %sf2.1 = (f32[512,3072]{1,0:T(8,128)}, f32[2,512,128]{2,1,0:T(8,128)}) custom-call(f32[512,3072]{1,0:T(8,128)} %get-tuple-element.56.refs_0_, f32[512,3072]{1,0:T(8,128)} %get-tuple-element.57.refs_1_.x, bf16[12,2,128,256]{3,2,1,0:T(8,128)(2,1)} %get-tuple-element.58.refs_2_.ent, ...), custom_call_target="tpu_custom_call" | custom-call | tf_op jit(solution)/shard_map/sf2/pallas_call | solution.py:1006
  245.0 153.4 %back.1 = (bf16[12,512,256]{2,1,0:T(8,128)(2,1)}, bf16[512,3072]{1,0:T(8,128)(2,1)}, bf16[14,512,256]{2,1,0:T(8,128)(2,1)}, f32[13,8,256]{2,1,0:T(8,128)}, f32[8...) custom-call(f32[512,3072]{1,0:T(8,128)} %get-tuple-element.62.mixed, ...), custom_call_target="tpu_custom_call" | custom-call | tf_op jit(solution)/shard_map/back/pallas_call | solution.py:1235
  398.4 0.7 slice_bitcast_fusion.2
  399.2 0.9 slice_reduce_fusion
  400.1 0.1 reshape_squeeze.6
  400.2 0.1 reduce_sum.9
  400.3 0.1 pad_maximum_fusion.1
  400.4 0.6 pad.14.hg_ref
  401.0 0.0 copy-start.23
  401.0 0.0 copy-start.24
  401.0 0.0 copy-start.13
  401.0 0.0 copy-start.17
  401.1 0.0 copy-start.18
  401.1 0.0 copy-start.12
  401.1 0.0 copy-start.15
  401.1 0.0 copy-start.16
  401.1 75.7 %end.1 = (f32[14,2,48,128]{3,2,1,0:T(8,128)}, bf16[512,1536]{1,0:T(8,128)(2,1)}, f32[512,1536]{1,0:T(8,128)}, f32[8,256]{1,0:T(8,128)}) custom-call(bf16[4,2,192,512]{3,2,1,0:T(8,128)(2,1)} %bitcast.35, bf16[14,512,256]{2,1,0:T(8,128)(2,1)} %get-tuple-element.67.dcp_ref, bf16[12,512,256]{2,1,0:T(8,128)(2,1)} %get-tuple-element.68.dz_ref, ...), custom_call_target="tpu_custom_call" | custom-call | tf_op jit(solution)/shard_map/end/pallas_call | solution.py:1341
  476.8 0.7 slice_reduce_fusion.1
  477.5 0.1 reshape_squeeze.7
  477.6 0.0 copy-start.14
  477.6 1.3 multiply_subtract_fusion.4
  478.9 1.3 multiply_subtract_fusion.5
  480.3 0.6 multiply_subtract_fusion.3
  480.9 1.4 multiply_subtract_fusion.2
  482.3 1.5 copy.54
  483.7 0.6 reshape.101
  484.3 1.5 copy-done.8
  485.8 0.1 fusion.12
  485.9 0.3 copy.55
  486.2 0.5 reshape.103
  486.7 0.0 copy-start.5
  486.8 0.0 copy-start.9
  486.8 0.3 copy.53
  487.1 0.0 copy-start.10
  487.1 0.5 reshape.100
  487.6 0.5 copy-done.4
  488.0 0.2 copy-done.9
  488.2 0.2 copy-done.10
  488.4 1.5 multiply_subtract_fusion.1
  489.9 0.2 copy-done.1
  490.1 0.4 slice-done
  490.5 0.4 copy-done.7
  490.9 4.0 multiply_subtract_fusion
  494.9 1.1 copy.65
  496.0 1.3 copy-done.2
  497.4 1.7 copy.66
  (34 shorter events, 0.1 us)
Async XLA Ops:
  0.7 7.9 %copy-start = (f32[48,6448]{1,0:T(8,128)S(1)}, f32[48,6448]{1,0:T(8,128)}, u32[]{:S(2)}) copy-start(f32[48,6448]{1,0:T(8,128)} %param.22) | copy-start | bytes 3714052
  5.2 3.5 copy-start.11
  401.0 76.6 %copy-start.19 = (f32[96]{0:T(128)S(1)}, f32[96]{0:T(128)}, u32[]{:S(2)}) copy-start(f32[96]{0:T(128)} %param.34) | copy-start | bytes 1156
  401.0 76.6 %copy-start.21 = (f32[96]{0:T(128)S(1)}, f32[96]{0:T(128)}, u32[]{:S(2)}) copy-start(f32[96]{0:T(128)} %param.35) | copy-start | bytes 1156
  401.0 76.6 %copy-start.22 = (f32[96]{0:T(128)S(1)}, f32[96]{0:T(128)}, u32[]{:S(2)}) copy-start(f32[96]{0:T(128)} %param.36) | copy-start | bytes 1156
  401.0 77.9 %copy-start.20 = (f32[48]{0:T(128)S(1)}, f32[48]{0:T(128)}, u32[]{:S(2)}) copy-start(f32[48]{0:T(128)} %param.31) | copy-start | bytes 580
  401.0 77.9 %copy-start.23 = (f32[48]{0:T(128)S(1)}, f32[48]{0:T(128)}, u32[]{:S(2)}) copy-start(f32[48]{0:T(128)} %param.32) | copy-start | bytes 580
  401.0 77.9 %copy-start.24 = (f32[48]{0:T(128)S(1)}, f32[48]{0:T(128)}, u32[]{:S(2)}) copy-start(f32[48]{0:T(128)} %param.33) | copy-start | bytes 580
  401.0 79.2 %copy-start.13 = (f32[3,48]{1,0:T(4,128)S(1)}, f32[3,48]{1,0:T(4,128)}, u32[]{:S(2)}) copy-start(f32[3,48]{1,0:T(4,128)} %param.37) | copy-start | bytes 1732
  401.0 79.2 %copy-start.17 = (f32[3,48]{1,0:T(4,128)S(1)}, f32[3,48]{1,0:T(4,128)}, u32[]{:S(2)}) copy-start(f32[3,48]{1,0:T(4,128)} %param.38) | copy-start | bytes 1732
  401.1 79.2 %copy-start.18 = (f32[3,48]{1,0:T(4,128)S(1)}, f32[3,48]{1,0:T(4,128)}, u32[]{:S(2)}) copy-start(f32[3,48]{1,0:T(4,128)} %param.39) | copy-start | bytes 1732
  401.1 79.8 %copy-start.12 = (f32[5,104]{1,0:T(8,128)S(1)}, f32[5,104]{1,0:T(8,128)}, u32[]{:S(2)}) copy-start(f32[5,104]{1,0:T(8,128)} %param.28) | copy-start | bytes 6244
  401.1 79.8 %copy-start.15 = (f32[5,104]{1,0:T(8,128)S(1)}, f32[5,104]{1,0:T(8,128)}, u32[]{:S(2)}) copy-start(f32[5,104]{1,0:T(8,128)} %param.29) | copy-start | bytes 6244
  401.1 79.8 %copy-start.16 = (f32[5,104]{1,0:T(8,128)S(1)}, f32[5,104]{1,0:T(8,128)}, u32[]{:S(2)}) copy-start(f32[5,104]{1,0:T(8,128)} %param.30) | copy-start | bytes 6244
  477.6 6.7 %copy-start.14 = (f32[3,48]{1,0:T(4,128)}, f32[3,48]{1,0:T(4,128)S(1)}, u32[]{:S(2)}) copy-start(f32[3,48]{1,0:T(4,128)S(1)} %reshape_squeeze.7) | copy-start | bytes 1732
  484.3 1.6 copy-start.3
  484.3 1.5 copy-start.8
  486.7 3.2 copy-start.5
  486.7 1.3 copy-start.4
  486.8 1.4 copy-start.9
  487.1 1.3 copy-start.10
  488.4 1.7 copy-start.1
  488.4 2.1 slice-start
  488.4 2.5 copy-start.7
  490.9 4.0 copy-start.6
  494.9 2.5 copy-start.2

commit v4 on v3

--- a/solution.py
+++ b/solution.py
@@ -310,34 +310,40 @@
 
 
 class Gather:
-    def __init__(self, me, n, src, w, sems, skew):
+    def __init__(self, me, n, src, w, sems, skew, base=0):
+        self.base = base
         self.me, self.n, self.src, self.w, self.sk, self.slots = me, n, src, w, skew, skew + 1
         self.rows = src.shape[2]
-        self.o1, self.o2, self.o3, self.o4, self.i1, self.i2, self.i3, self.i4 = sems
+        self.o1, self.o2, self.o3, self.o4, self.i1, self.i2, self.i3, self.i4, self.own = sems
 
     @staticmethod
     def sems(n, skew):
         D = pltpu.SemaphoreType.DMA
-        return [D((skew + 1, 3)), D((skew + 1, 2)), D((skew + 1, 2)), D((skew + 1,)), D((n, 3)), D((n, 2)), D((n, 2)), D((n,))]
+        return [D((skew + 1, 3)), D((skew + 1, 2)), D((skew + 1, 2)), D((skew + 1,)), D((n, 3)), D((n, 2)), D((n, 2)), D((n,)), D((skew + 1,))]
+
+    def mine(self, i, s):
+        m = self.me
+        rows = pl.ds(pl.multiple_of(m.z * self.rows, 16), self.rows)
+        return pltpu.make_async_copy(self.src.at[self.base + i], self.w.at[self.base + i, :, m.y, m.x, m.c, rows], self.own.at[s])
 
     def c1(self, i, s, k):
         m, w = self.me, self.w
         rows = pl.ds(pl.multiple_of(m.z * self.rows, 16), self.rows)
-        return send(self.src.at[i], w.at[i, :, m.y, m.x, m.c, rows], self.o1.at[s, k - 1], self.i1.at[i, k - 1], m.z_peer(k))
+        return send(self.src.at[self.base + i], w.at[self.base + i, :, m.y, m.x, m.c, rows], self.o1.at[s, k - 1], self.i1.at[i, k - 1], m.z_peer(k))
 
     def c2(self, i, s, h):
         m, w = self.me, self.w
-        part = w.at[i, h, m.y, m.x, m.c]
+        part = w.at[self.base + i, h, m.y, m.x, m.c]
         return send(part, part, self.o2.at[s, h], self.i2.at[i, h], (m.y_peer, m.x_peer)[h])
 
     def c3(self, i, s, h):
         m, w = self.me, self.w
-        part = w.at[i, 0, :, m.x, m.c] if h == 0 else w.at[i, 1, m.y, :, m.c]
+        part = w.at[self.base + i, 0, :, m.x, m.c] if h == 0 else w.at[self.base + i, 1, m.y, :, m.c]
         return send(part, part, self.o3.at[s, h], self.i3.at[i, h], (m.x_peer, m.y_peer)[h])
 
     def c4(self, i, s):
         m, w = self.me, self.w
-        part = w.at[i, :, :, :, m.c]
+        part = w.at[self.base + i, :, :, :, m.c]
         return send(part, part, self.o4.at[s], self.i4.at[i], m.core_peer)
 
     def step(self, it):
@@ -354,15 +360,14 @@
             @pl.when(i >= ns)
             def _():
                 for k in (1, 2, 3): self.c1(i, s, k).wait_send()
+            self.mine(i, s).start()
             for k in (2, 1, 3): self.c1(i, s, k).start()
-            rows = pl.ds(pl.multiple_of(m.z * self.rows, 16), self.rows)
-            for h in range(2):
-                self.w[i, h, m.y, m.x, m.c, rows] = self.src[i, h]
 
         def second(i, s):
             @pl.when(i >= ns)
             def _():
                 for h in range(2): self.c2(i, s, h).wait_send()
+            self.mine(i, s).wait()
             for k in (1, 2, 3): self.c1(i, s, k).wait_recv()
             for h in range(2): self.c2(i, s, h).start()
 
@@ -396,130 +401,9 @@
             self.c4(i, s).wait_send()
 
 
-def windows(width, count):
-    return [(o * width // 128) * 128 for o in range(count)]
-
-
-def gather_call(src_in, src_out, small, tokens, edge, cotangent, collective_id, skew=2):
-    NI, NO = src_in.shape[0], src_out.shape[0]
-    T, DM = tokens.shape
-    TE = T + 16
-    DIN = 2 * 16 * 96
-
-    def kernel(src_in, src_out, small_ref, tok_ref, edge_ref, cot_ref,
-               proj_hbm, win_hbm, wout_hbm, low_ref, par_ref, dn_ref,
-               win, wout, sm, low_e, edge_in, pbuf,
-               *sems):
-        gs, os_, (sm_out, sm_in, ed_out, ed_in, pb_sem, wi_sem, wo_sem) = sems[:8], sems[8:16], sems[16:]
-        me = Place()
-        bar = pltpu.get_barrier_semaphore()
-        def sig(k, _):
-            pl.semaphore_signal(bar, inc=1, device_id=me.any_peer(k), device_id_type=MESH)
-            return 0
-        lax.fori_loop(1, 32, sig, 0)
-        pl.semaphore_wait(bar, 31)
-        ga = Gather(me, NI, src_in, win, gs, skew)
-        gb = Gather(me, NO, src_out, wout, os_, skew)
-
-        def small_copy(k):
-            return send(small_ref, sm.at[me.line], sm_out.at[k - 1], sm_in.at[k - 1], me.any_peer(k))
-        def edge_copy():
-            return send(edge_ref, edge_in, ed_out, ed_in, {"seq": lax.rem(me.z + 1, 4)})
-        lax.fori_loop(1, 32, lambda k, _: (small_copy(k).start(), 0)[1], 0)
-        edge_copy().start()
-        sm[me.line] = small_ref[...]
-        ga.step(0); ga.step(1)
-        lax.fori_loop(1, 32, lambda k, _: (small_copy(k).wait(), 0)[1], 0)
-        edge_copy().wait()
-        par_ref[...] = jnp.zeros_like(par_ref)
-        for o in range(32):
-            for base, width, row, lo in ((0, 104, 5, 0), (3328, 48, 1, 5), (4864, 96, 1, 6)):
-                at = base + (o * width // 128) * 128
-                wd = min(256, {0: 3328, 3328: 4864, 4864: 7936}[base] - at)
-                par_ref[:, at:at + wd] += sm[o][:, :wd]
-        gain = par_ref[5:6, 3328:4864]
-        keep = (me.z > 0).astype(f32)
-
-        def norm(v):
-            v = v.astype(f32)
-            return (v * lax.rsqrt(jnp.mean(v * v, axis=-1, keepdims=True) + 1e-5) * gain).astype(bf)
-        def nloop(t, _):
-            r = pl.ds(pl.multiple_of(t * 64, 64), 64)
-            v = norm(tok_ref[r])
-            low_ref[r] = v
-            low_e[r] = v
-            return 0
-        lax.fori_loop(0, T // 64, nloop, 0)
-        low_e[T:] = norm(edge_in[...].astype(f32) * keep)
-
-        def pcopy(i, s): return pltpu.make_async_copy(pbuf.at[s], proj_hbm.at[i], pb_sem.at[s])
-        def wicopy(i): return pltpu.make_async_copy(win.at[i], win_hbm.at[i], wi_sem.at[i])
-        def wocopy(i): return pltpu.make_async_copy(wout.at[i], wout_hbm.at[i], wo_sem.at[i])
-
-        def loop(it, _):
-            @pl.when(it >= 2)
-            def _(): ga.step(it)
-            gb.step(it - NI)
-            @pl.when((it >= 4 * skew) & (it < NI + 4 * skew))
-            def _():
-                i = it - 4 * skew; s = lax.rem(i, 2)
-                ga.arrived(i)
-                wicopy(i).start()
-                @pl.when(i >= 2)
-                def _(): pcopy(i - 2, s).wait()
-                w = jnp.concatenate([win[i, h].reshape(DM, 128) for h in range(2)], axis=1)
-                pbuf[s] = jnp.dot(low_e[...], w, preferred_element_type=f32)
-                pcopy(i, s).start()
-            @pl.when(it >= NI + 4 * skew)
-            def _():
-                i = it - 4 * skew - NI
-                gb.arrived(i)
-                wocopy(i).start()
-                for h in range(2):
-                    a = cot_ref[:, pl.ds(pl.multiple_of(i * 256 + h * 128, 128), 128)]
-                    def cols(q, _):
-                        y = q // 4; x = lax.rem(q // 2, 2); c = lax.rem(q, 2)
-                        r = lax.dot_general(a, wout[i, h, y, x, c], (((1,), (1,)), ((), ())), preferred_element_type=f32)
-                        for t in range(3):
-                            rt = r[:, 128 * t:128 * t + 128]
-                            if h == 0:
-                                @pl.when(i == 0)
-                                def _(): dn_ref[3 * q + t] = rt
-                                @pl.when(i > 0)
-                                def _(): dn_ref[3 * q + t] += rt
-                            else:
-                                dn_ref[3 * q + t] += rt
-                        return 0
-                    lax.fori_loop(0, 8, cols, 0)
-            return 0
-        lax.fori_loop(0, NI + NO + 4 * skew, loop, 0)
-        pcopy(NI - 2, NI % 2).wait()
-        pcopy(NI - 1, (NI - 1) % 2).wait()
-        lax.fori_loop(0, NI, lambda i, _: (wicopy(i).wait(), 0)[1], 0)
-        lax.fori_loop(0, NO, lambda i, _: (wocopy(i).wait(), 0)[1], 0)
-        ga.finish()
-        gb.finish()
-
-    V, D = pltpu.VMEM, pltpu.SemaphoreType.DMA
-    S = jax.ShapeDtypeStruct
-    vm, hb = pl.BlockSpec(memory_space=pltpu.VMEM), pl.BlockSpec(memory_space=pl.ANY)
-    wi, wo = (NI, 2, 2, 2, 2, 192, 128), (NO, 2, 2, 2, 2, 384, 128)
-    return pl.pallas_call(
-        kernel,
-        out_shape=(S((NI, TE, 256), f32), S(wi, bf), S(wo, bf), S((T, DM), bf), S((8, 7936), f32), S((24, T, 128), f32)),
-        in_specs=[vm] * 6,
-        out_specs=(hb, hb, hb, vm, vm, vm),
-        scratch_shapes=[V(wi, bf), V(wo, bf), V((32, 8, 256), f32), V((TE, DM), bf), V((16, DM), bf), V((2, TE, 256), f32)]
-        + Gather.sems(NI, skew) + Gather.sems(NO, skew)
-        + [D((31,)), D((31,)), D, D, D((2,)), D((NI,)), D((NO,))],
-        compiler_params=pltpu.CompilerParams(collective_id=collective_id, has_side_effects=True, vmem_limit_bytes=63 << 20),
-        name="gather",
-    )(src_in, src_out, small, tokens, edge, cotangent)
-
-
 def arrange(in_proj, out_proj, conv_params, norm_gain, gate_gain, line):
     w = in_proj.astype(bf)
-    w = jnp.concatenate([w[:, 3072:], jnp.zeros((48, 208), bf), w[:, :3072]], axis=1)
+    w = jnp.concatenate([w[:, 6400:], jnp.zeros((48, 208), bf), w[:, 6144:6400], w[:, 3072:6144], w[:, :3072]], axis=1)
     src_in = w.reshape(48, 26, 2, 128).transpose(1, 2, 0, 3)
     src_out = out_proj.astype(bf).reshape(96, 6, 2, 128).transpose(1, 2, 0, 3)
     small = jnp.zeros((8, 256), f32)
@@ -628,8 +512,7 @@
 
 
 class Chain:
-    def __init__(self, me, by, got, part, out, out_sem, in_sem, keep, lag):
-        self.lag = lag
+    def __init__(self, me, by, got, part, out, out_sem, in_sem, keep):
         self.me, self.by, self.got, self.part, self.out, self.out_sem, self.in_sem, self.keep = me, by, got, part, out, out_sem, in_sem, keep
         self.place = me.z if by == 1 else 3 - me.z
 
@@ -654,15 +537,17 @@
         @pl.when(self.place == 0)
         def _(): self.got[...] = jnp.zeros_like(self.got)
 
-    def step(self, j, drain):
-        lag = self.lag * self.place
-        @pl.when((j >= lag) & (j < TILES + lag))
-        def _(): self.tile(j - lag)
-
-        if drain:
-            @pl.when(j == TILES - 1)
-            def _():
-                lax.fori_loop(TILES - lag, TILES, lambda i, _: (self.tile(i), 0)[1], 0)
+    def every_other(self, i):
+        u = i - self.place
+        @pl.when((u >= 0) & (u < 2 * TILES) & (lax.rem(u, 2) == 0))
+        def _(): self.tile(u // 2)
+
+    def four_of_seven(self, i):
+        u = i - self.place
+        m = lax.rem(u, 7)
+        t = 4 * (u // 7) + (m + 1) // 2
+        @pl.when((u >= 0) & (t < TILES) & ((m == 0) | (lax.rem(m, 2) == 1)))
+        def _(): self.tile(t)
 
     def finish(self):
         @pl.when(self.place < 3)
@@ -683,97 +568,6 @@
 
 
 V = pltpu.VMEM
-
-
-def sf1_body(j, cin, halo, bcin, bchalo, raw, taps, bctaps, hp, x_o, yi_o, ent_o, step_o, ds_o, dst_o, b_o, c_o, pad, pad2, s_s, bt_s, got, part, out, out_sem, in_sem):
-    me = Place()
-    line = Chain(me, 1, got, part, out, out_sem, in_sem, keeper(ds_o), 1)
-    @pl.when(j == 0)
-    def _():
-        greet((me.z_peer(1), me.z_peer(3)))
-        line.start()
-        pre = raw[0] + hp[2:3]
-        step = jnp.maximum(pre, 0.0) + jnp.log1p(jnp.exp(-jnp.abs(pre)))
-        rate = step * -jnp.exp(hp[0:1])
-        step_o[...] = step
-        r = lax.broadcasted_iota(jnp.int32, (256, 256), 0)
-        c = lax.broadcasted_iota(jnp.int32, (256, 256), 1)
-        low = (c <= r).astype(bf)
-        for g in range(2):
-            ds_o[256 * g:256 * g + 256] = mul_exact(low, rate[256 * g:256 * g + 256])
-        turned = ds_o[...].T
-        for p in range(TILES):
-            dst_o[p, 0:4] = turned[4 * p:4 * p + 4]
-        fill_pad(pad2, bcin[0], bchalo[0])
-        for g, co in enumerate(conv(pad2, bctaps)):
-            act = co * sig(co)
-            b, c = act[:, :128], act[:, 128:]
-            b_o[256 * g:256 * g + 256] = b
-            c_o[256 * g:256 * g + 256] = c
-            bt_s[g] = b.T
-            s_s[g, 0] = mul(c[:128], b[:128], NT)
-            s_s[g, 1] = mul(c[128:], b[128:], NT)
-            s_s[g, 2] = mul(c[128:], b[:128], NT)
-
-    fill_pad(pad, cin[0], halo[0])
-    rds = rolled(ds_o[...], j)
-    dsc = spread(rds)
-    stc = spread(rolled(step_o[...], j))
-    ok = causal(False)
-    for g, co in enumerate(conv(pad, taps)):
-        b0 = 256 * g
-        x = co * sig(co)
-        x_o[b0:b0 + 256] = x
-        xs = x * stc[b0:b0 + 256]
-        xp = halves(xs)
-        d = dsc[b0:b0 + 256]
-        ys = []
-        for q in range(2):
-            b = b0 + 128 * q
-            y = []
-            for m in range(2):
-                w = []
-                for h in (2 * m, 2 * m + 1):
-                    gap = rds[b:b + 128, h:h + 1] - dst_o[j, h:h + 1, b:b + 128]
-                    w.append(s_s[g, q] * jnp.exp(jnp.where(ok, gap, -1e30)))
-                y.append(mul(jnp.concatenate(w, 1), heads_apart(part_of(xp, slice(128 * q, 128 * q + 128), slice(128 * m, 128 * m + 128)))))
-            ys.append(jnp.concatenate(y, 1))
-        mid = d[127:128]
-        ys[1] = ys[1] + jnp.exp(d[128:] - mid) * mul(s_s[g, 2], jnp.exp(mid - d[:128]) * xs[:128])
-        yi_o[b0:b0 + 128] = ys[0]
-        yi_o[b0 + 128:b0 + 256] = ys[1]
-        part[j, g] = mul(bt_s[g], jnp.exp(d[255:256] - d) * xs)
-    line.step(j, True)
-
-    @pl.when(j == TILES - 1)
-    def _():
-        line.finish()
-        ent_o[...] = got[...]
-
-
-def sf2_body(j, yi, x, ent, z, dn, gain, ds, c_r, hp, mixed_o, rq_o, a1, a2):
-    @pl.when(j == 0)
-    def _():
-        a1[...] = jnp.zeros_like(a1)
-        a2[...] = jnp.zeros_like(a2)
-    dsc = spread(rolled(ds[...], j))
-    skip = spread(rolled(hp[...], j))[1:2]
-    for g in range(2):
-        r = slice(256 * g, 256 * g + 256)
-        car = jnp.exp(dsc[r]) * mul(c_r[r], ent[0, g])
-        mixed = yi[r] + car + skip * x[r]
-        mixed_o[r] = mixed
-        zz = z[0, r]
-        gated = mixed * (zz * sig(zz))
-        a1[r] += gated * gated
-        a2[r] += gain[6:7] * jnp.concatenate([dn[0, r], dn[1, r]], 1) * gated
-
-    @pl.when(j == TILES - 1)
-    def _():
-        r = lax.rsqrt(jnp.sum(a1[...], axis=1, keepdims=True) * (1.0 / 3072) + 1e-5)
-        k = r * r * r * (jnp.sum(a2[...], axis=1, keepdims=True) * (1.0 / 3072))
-        rq_o[0] = jnp.broadcast_to(r, (512, 128))
-        rq_o[1] = jnp.broadcast_to(k, (512, 128))
 
 
 def sb1_start(b_r, c_r, dst_acc, dc_acc, dds_acc, xu_acc, st_s, ct_s):
@@ -800,7 +594,7 @@
     dskip = jnp.zeros((1, 256), f32)
     for g in range(2):
         r = slice(256 * g, 256 * g + 256)
-        zz, mx, xx = z[0, r], mixed[r], x[r]
+        zz, mx, xx = z[0, r], mixed[0, r], x[0, r]
         dnr = jnp.concatenate([dn[0, r], dn[1, r]], 1)
         s = sig(zz)
         sil = zz * s
@@ -903,7 +697,7 @@
         dco = []
         for g, co in enumerate(conv(pad, taps)):
             r = slice(256 * g, 256 * g + 256)
-            d, xx, st, e = dsc[r], x[r], got[j, g], ent[j, g]
+            d, xx, st, e = dsc[r], x[0, r], got[j, g], ent[j, g]
             tail = jnp.exp(d[255:256] - d)
             ut = tail * mul(b_r[r], st)
             xut_s[r] += to_heads(xx * ut, spot)
@@ -916,7 +710,7 @@
         grads, din, prev = conv_back(pad, dpad, dco, taps)
         cg_o[j] = grads
         for g in range(2):
-            dcp_o[j, 256 * g:256 * g + 256] = din[g].astype(bf)
+            dcp_o[j + 2, 256 * g:256 * g + 256] = din[g].astype(bf)
         pass_edge(j, prev, din)
 
     def final(bcin, bchalo, bctaps, raw, ds, step, b_r, c_r, hp, dst_acc, dc_acc, dds_acc, xu_acc):
@@ -933,7 +727,7 @@
         grads, din, prev = conv_back(pad2, dpad2, dco2, bctaps)
         cg_o[12] = grads
         for g in range(2):
-            dcp_o[12, 256 * g:256 * g + 256] = din[g].astype(bf)
+            dcp_o[1, 256 * g:256 * g + 256] = din[g].astype(bf)
         pass_edge(TILES, prev, din)
         st = step[...]
         xut = xut_s[...]
@@ -952,8 +746,8 @@
         drate = jnp.concatenate(drate, 0)
         dstep = xu_acc[...] + xut + drate * speed
         draw = jnp.where(lane < 48, dstep * sig(raw[0] + hp[2:3]), 0.0)
-        dcp_o[13, :, 0:128] = draw.astype(bf)
-        dcp_o[13, :, 128:256] = jnp.zeros((512, 128), bf)
+        dcp_o[0, :, 0:128] = draw.astype(bf)
+        dcp_o[0, :, 128:256] = jnp.zeros((512, 128), bf)
         hg_o[0:1] = jnp.sum(drate * st * speed, axis=0, keepdims=True)
         hg_o[1:2] = jnp.zeros((1, 128), f32)
         hg_o[2:3] = jnp.sum(draw, axis=0, keepdims=True)
@@ -965,7 +759,7 @@
                 edge(i).wait_recv()
                 for g in range(2):
                     rows = lst[i, 8 * g:8 * g + 8] + edge_in[i, 8 * g:8 * g + 8].astype(f32)
-                    dcp_o[i, 256 * g + 248:256 * g + 256] = rows.astype(bf)
+                    dcp_o[jnp.where(i < TILES, i + 2, 1), 256 * g + 248:256 * g + 256] = rows.astype(bf)
                 return 0
             lax.fori_loop(0, TILES + 1, patch, 0)
 
@@ -983,45 +777,10 @@
     return pl.BlockSpec(shape, lambda j: (0,) * len(shape), pipeline_mode=pl.Buffered(1))
 
 
-TILE = pl.BlockSpec((1, 512, 256), lambda j: (j, 0, 0))
-HALO = pl.BlockSpec((1, 16, 256), lambda j: (j, 32, 0))
-ZT = pl.BlockSpec((1, 512, 256), lambda j: (14 + j, 0, 0))
-BC = pl.BlockSpec((1, 512, 256), lambda j: (12, 0, 0), pipeline_mode=pl.Buffered(1))
-BCH = pl.BlockSpec((1, 16, 256), lambda j: (12, 32, 0), pipeline_mode=pl.Buffered(1))
-RAW = pl.BlockSpec((1, 512, 128), lambda j: (13, 0, 0), pipeline_mode=pl.Buffered(1))
-TAP = pl.BlockSpec((8, 256), lambda j: (0, j))
+BC = pl.BlockSpec((1, 512, 256), lambda j: (1, 0, 0), pipeline_mode=pl.Buffered(1))
+BCH = pl.BlockSpec((1, 16, 256), lambda j: (1, 32, 0), pipeline_mode=pl.Buffered(1))
+RAW = pl.BlockSpec((1, 512, 128), lambda j: (0, 0, 0), pipeline_mode=pl.Buffered(1))
 BCT = pl.BlockSpec((8, 256), lambda j: (0, 12), pipeline_mode=pl.Buffered(1))
-GAIN = pl.BlockSpec((8, 256), lambda j: (0, 19 + j))
-HP = const(8, 128)
-COL = pl.BlockSpec((512, 256), lambda j: (0, j))
-ST = pl.BlockSpec((1, 2, 128, 256), lambda j: (j, 0, 0, 0))
-DN = pl.BlockSpec((2, 512, 128), lambda j: (j, 0, 0))
-TOK = const(512, 128)
-TOKT = const(12, 8, 512)
-
-
-def call(body, name, in_specs, out_shape, out_specs, scratch, args, cid=None):
-    def kernel(*refs):
-        body(pl.program_id(0), *refs)
-    return pl.pallas_call(
-        kernel, grid=(TILES,), in_specs=in_specs, out_specs=out_specs, out_shape=out_shape, scratch_shapes=scratch,
-        compiler_params=pltpu.CompilerParams(vmem_limit_bytes=60 << 20, collective_id=cid, has_side_effects=cid is not None), name=name,
-    )(*args)
-
-
-def sf1(proj, par, hp):
-    return call(sf1_body, "sf1", [TILE, HALO, BC, BCH, RAW, TAP, BCT, HP],
-        (S((512, 3072), f32), S((512, 3072), f32), S((12, 2, 128, 256), bf), S((512, 128), f32), S((512, 128), f32), S((12, 8, 512), f32), S((512, 128), f32), S((512, 128), f32)),
-        (COL, COL, const(12, 2, 128, 256), TOK, TOK, TOKT, TOK, TOK),
-        [V((2, 264, 256), f32), V((2, 264, 256), f32), V((2, 3, 128, 128), f32), V((2, 128, 256), f32)] + Chain.scratch(),
-        (proj, proj, proj, proj, proj, par, par, hp), 4)
-
-
-def sf2(yi, x, ent, proj, dn, par, ds, c, hp):
-    return call(sf2_body, "sf2", [COL, COL, ST, ZT, DN, GAIN, TOK, TOK, HP],
-        (S((512, 3072), f32), S((2, 512, 128), f32)), (COL, const(2, 512, 128)),
-        [V((512, 256), f32), V((512, 256), f32)],
-        (yi, x, ent, proj, dn, par, ds, c, hp))
 
 
 class Reduce:
@@ -1161,7 +920,7 @@
                dxa_s, dz_s, rhs, lhs_s, *refs):
         j = pl.program_id(0)
         me = Place()
-        line = Chain(me, -1, got, part, out, out_sem, in_sem, keeper(ds), 1)
+        line = Chain(me, -1, got, part, out, out_sem, in_sem, keeper(ds))
         red = Reduce(me, n, R, refs, sk)
         two_start, two_tile, two_final = sb2_make(me, dcp_o, cg_o, hg_o, pad, pad2, dpad, dpad2, db_s, xut_s, de_s, prv, lst, edge_in, e_out, e_in)
 
@@ -1185,7 +944,7 @@
         def _():
             sb1_tile(j, mixed, z, dn, x, ent, gain, ds, step, dst, hp, rq, dxa_s, dz_o, dz_s, ol_o, lhs_s, rows_o,
                      dst_acc, dc_acc, dds_acc, xu_acc, st_s, ct_s, part)
-        line.step(j, False)
+        line.four_of_seven(j)
 
         @pl.when(j == TILES)
         def _(): two_start()
@@ -1207,13 +966,13 @@
     xt = lambda j: jnp.where(j < TILES, j, j - TILES)
     tok = one_time(512, 128)
     in_specs = [
-        pl.BlockSpec((512, 256), lambda j: (0, p1(j))),
+        pl.BlockSpec((1, 512, 256), lambda j: (p1(j), 0, 0)),
         pl.BlockSpec((1, 512, 256), lambda j: (14 + p1(j), 0, 0)),
         pl.BlockSpec((2, 512, 128), lambda j: (p1(j), 0, 0)),
-        pl.BlockSpec((512, 256), lambda j: (0, xt(j))),
+        pl.BlockSpec((1, 512, 256), lambda j: (xt(j), 0, 0)),
         pl.BlockSpec((8, 256), lambda j: (0, 19 + p1(j))),
-        pl.BlockSpec((1, 512, 256), lambda j: (p2(j), 0, 0)),
-        pl.BlockSpec((1, 16, 256), lambda j: (p2(j), 32, 0)),
+        pl.BlockSpec((1, 512, 256), lambda j: (2 + p2(j), 0, 0)),
+        pl.BlockSpec((1, 16, 256), lambda j: (2 + p2(j), 32, 0)),
         pl.BlockSpec((8, 256), lambda j: (0, p2(j))),
         one_time(12, 2, 128, 256), tok, tok, one_time(12, 8, 512), tok, tok, one_time(8, 128), one_time(2, 512, 128),
         BC, BCH, BCT, RAW, one_time(4, 2, 4, 48, 512), one_time(512, 1536),
@@ -1348,23 +1107,270 @@
     )(low_t.reshape(4, 2, 192, 512), dcp, dz, ol, win, wout, tok, cot, par, cg, rows, hg)
 
 
+def dt_part(raw, hp, step_o, ds_o, dst_o):
+    pre = raw + hp[2:3]
+    step = jnp.maximum(pre, 0.0) + jnp.log1p(jnp.exp(-jnp.abs(pre)))
+    rate = step * -jnp.exp(hp[0:1])
+    step_o[...] = step
+    r = lax.broadcasted_iota(jnp.int32, (256, 256), 0)
+    c = lax.broadcasted_iota(jnp.int32, (256, 256), 1)
+    low = (c <= r).astype(bf)
+    for g in range(2):
+        ds_o[256 * g:256 * g + 256] = mul_exact(low, rate[256 * g:256 * g + 256])
+    turned = ds_o[...].T
+    for p in range(TILES):
+        dst_o[p, 0:4] = turned[4 * p:4 * p + 4]
+
+
+def bc_part(block, taps, b_o, c_o, pad, s_s, bt_s):
+    fill_pad(pad, block, block[512:528])
+    for g, co in enumerate(conv(pad, taps)):
+        act = co * sig(co)
+        b, c = act[:, :128], act[:, 128:]
+        b_o[256 * g:256 * g + 256] = b
+        c_o[256 * g:256 * g + 256] = c
+        bt_s[g] = b.T
+        s_s[g, 0] = mul(c[:128], b[:128], NT)
+        s_s[g, 1] = mul(c[128:], b[128:], NT)
+        s_s[g, 2] = mul(c[128:], b[:128], NT)
+
+
+def sf1_tile(j, block, taps, step, ds, dst, x_s, yi_s, part, pad, s_s, bt_s):
+    fill_pad(pad, block, block[512:528])
+    rds = rolled(ds[...], j)
+    dsc = spread(rds)
+    stc = spread(rolled(step[...], j))
+    ok = causal(False)
+    for g, co in enumerate(conv(pad, taps)):
+        b0 = 256 * g
+        x = co * sig(co)
+        x_s[j, b0:b0 + 256] = x
+        xs = x * stc[b0:b0 + 256]
+        xp = halves(xs)
+        d = dsc[b0:b0 + 256]
+        ys = []
+        for q in range(2):
+            b = b0 + 128 * q
+            y = []
+            for m in range(2):
+                w = []
+                for h in (2 * m, 2 * m + 1):
+                    gap = rds[b:b + 128, h:h + 1] - dst[j, h:h + 1, b:b + 128]
+                    w.append(s_s[g, q] * jnp.exp(jnp.where(ok, gap, -1e30)))
+                y.append(mul(jnp.concatenate(w, 1), heads_apart(part_of(xp, slice(128 * q, 128 * q + 128), slice(128 * m, 128 * m + 128)))))
+            ys.append(jnp.concatenate(y, 1))
+        mid = d[127:128]
+        ys[1] = ys[1] + jnp.exp(d[128:] - mid) * mul(s_s[g, 2], jnp.exp(mid - d[:128]) * xs[:128])
+        yi_s[j, b0:b0 + 128] = ys[0]
+        yi_s[j, b0 + 128:b0 + 256] = ys[1]
+        part[j, g] = mul(bt_s[g], jnp.exp(d[255:256] - d) * xs)
+
+
+def sf2_tile(j, z, gain, ds, c_r, hp, x_s, yi_s, got, dn, a1, a2):
+    dsc = spread(rolled(ds[...], j))
+    skip = spread(rolled(hp[...], j))[1:2]
+    for g in range(2):
+        r = slice(256 * g, 256 * g + 256)
+        mixed = yi_s[j, r] + jnp.exp(dsc[r]) * mul(c_r[r], got[j, g]) + skip * x_s[j, r]
+        yi_s[j, r] = mixed
+        gated = mixed * (z[r] * sig(z[r]))
+        a1[r] += gated * gated
+        a2[r] += gain * jnp.concatenate([dn[2 * j, r], dn[2 * j + 1, r]], 1) * gated
+
+
+def front_call(src_in, src_out, small, tokens, edge, cotangent, hp, collective_id, skew=2):
+    NI, NO = src_in.shape[0], src_out.shape[0]
+    T, DM = tokens.shape
+    TE = T + 16
+    FIRST = NI - TILES
+    Z0 = FIRST + NO
+
+    def kernel(src_in, src_out, small_ref, tok_ref, edge_ref, cot_ref, hp,
+               proj_hbm, win, wout, x_hbm, mixed_hbm, low_hbm, dn_hbm, par_ref, ent_o, step_o, ds_o, dst_o, b_o, c_o, rq_o,
+               sm, low_e, edge_in, pbuf, wbuf, obuf, x_s, yi_s, dn_ref, a1, a2, pad, s_s, bt_s, got, part, out, out_sem, in_sem, *sems):
+        gs, os_, zs, (sm_out, sm_in, ed_out, ed_in, pb_sem, wl_sem, ol_sem, x_sem, mx_sem, dn_sem, low_sem) = sems[:9], sems[9:18], sems[18:27], sems[27:]
+        me = Place()
+        bar = pltpu.get_barrier_semaphore()
+        def sg(k, _):
+            pl.semaphore_signal(bar, inc=1, device_id=me.any_peer(k), device_id_type=MESH)
+            return 0
+        lax.fori_loop(1, 32, sg, 0)
+        pl.semaphore_wait(bar, 31)
+        ga = Gather(me, FIRST, src_in, win, gs, skew)
+        gb = Gather(me, NO, src_out, wout, os_, skew)
+        gz = Gather(me, NI - FIRST, src_in, win, zs, skew, FIRST)
+        line = Chain(me, 1, got, part, out, out_sem, in_sem, keeper(ds_o))
+
+        def small_copy(k):
+            return send(small_ref, sm.at[me.line], sm_out.at[k - 1], sm_in.at[k - 1], me.any_peer(k))
+        def edge_copy():
+            return send(edge_ref, edge_in, ed_out, ed_in, {"seq": lax.rem(me.z + 1, 4)})
+        lax.fori_loop(1, 32, lambda k, _: (small_copy(k).start(), 0)[1], 0)
+        edge_copy().start()
+        sm[me.line] = small_ref[...]
+        ga.step(0)
+        ga.step(1)
+        line.start()
+        a1[...] = jnp.zeros_like(a1)
+        a2[...] = jnp.zeros_like(a2)
+        par_ref[...] = jnp.zeros_like(par_ref)
+        lax.fori_loop(1, 32, lambda k, _: (small_copy(k).wait(), 0)[1], 0)
+        edge_copy().wait()
+        for o in range(32):
+            for base, width, stop in ((0, 104, 3328), (3328, 48, 4864), (4864, 96, 7936)):
+                at = base + (o * width // 128) * 128
+                wd = min(256, stop - at)
+                par_ref[:, at:at + wd] += sm[o][:, :wd]
+        gain = par_ref[5:6, 3328:4864]
+        keep = (me.z > 0).astype(f32)
+
+        def norm(v):
+            v = v.astype(f32)
+            return (v * lax.rsqrt(jnp.mean(v * v, axis=-1, keepdims=True) + 1e-5) * gain).astype(bf)
+        def nloop(t, _):
+            r = pl.ds(pl.multiple_of(t * 64, 64), 64)
+            low_e[r] = norm(tok_ref[r])
+            return 0
+        lax.fori_loop(0, T // 64, nloop, 0)
+        low_e[T:] = norm(edge_in[...].astype(f32) * keep)
+        low_copy = pltpu.make_async_copy(low_e.at[0:T], low_hbm, low_sem)
+        dn_copy = pltpu.make_async_copy(dn_ref, dn_hbm, dn_sem)
+        low_copy.start()
+
+        def two(i): return lax.rem(i, 2)
+        def pcopy(i): return pltpu.make_async_copy(pbuf.at[two(i)], proj_hbm.at[i], pb_sem.at[two(i)])
+        def wload(i): return pltpu.make_async_copy(win.at[i], wbuf.at[two(i)], wl_sem.at[two(i)])
+        def oload(i): return pltpu.make_async_copy(wout.at[i], obuf.at[two(i)], ol_sem.at[two(i)])
+        def xcopy(j): return pltpu.make_async_copy(x_s.at[j], x_hbm.at[j], x_sem.at[j])
+        def mcopy(j): return pltpu.make_async_copy(yi_s.at[j], mixed_hbm.at[j], mx_sem.at[j])
+        def cols(base, j): return pl.ds(pl.multiple_of(base + j * 256, 128), 256)
+
+        LAG = 4 * skew
+        def chunk(i):
+            s = two(i)
+            wload(i).wait()
+            @pl.when(i >= 2)
+            def _(): pcopy(i - 2).wait()
+            w = jnp.concatenate([wbuf[s, h].reshape(DM, 128) for h in range(2)], axis=1)
+            pbuf[s] = jnp.dot(low_e[...], w, preferred_element_type=f32)
+            pcopy(i).start()
+            return pbuf.at[s]
+
+        def loop(it, _):
+            @pl.when(it >= 2)
+            def _(): ga.step(it)
+            gb.step(it - FIRST)
+            gz.step(it - Z0)
+            a = it - LAG
+            @pl.when((a >= 0) & (a < FIRST))
+            def _():
+                ga.arrived(a)
+                wload(a).start()
+            @pl.when((a >= FIRST) & (a < Z0))
+            def _():
+                gb.arrived(a - FIRST)
+                oload(a - FIRST).start()
+            @pl.when((a >= Z0) & (a < Z0 + TILES))
+            def _():
+                gz.arrived(a - Z0)
+                wload(a - NO).start()
+            i = a - 1
+            @pl.when((i >= 0) & (i < FIRST))
+            def _():
+                block = chunk(i)
+
+                @pl.when(i == 0)
+                def _(): dt_part(block[0:512, 0:128], hp, step_o, ds_o, dst_o)
+                @pl.when(i == 1)
+                def _(): bc_part(block, par_ref[:, 3072:3328], b_o, c_o, pad, s_s, bt_s)
+                @pl.when(i >= 2)
+                def _():
+                    j = i - 2
+                    sf1_tile(j, block, par_ref[:, cols(0, j)], step_o, ds_o, dst_o, x_s, yi_s, part, pad, s_s, bt_s)
+                    xcopy(j).start()
+            line.every_other(i - 2)
+            @pl.when((i >= FIRST) & (i < Z0))
+            def _():
+                i2 = i - FIRST
+                s = two(i2)
+                oload(i2).wait()
+                a_ = cot_ref[:, cols(0, i2)]
+                def rows(q, _):
+                    y = q // 4
+                    x = lax.rem(q // 2, 2)
+                    c = lax.rem(q, 2)
+                    w = jnp.concatenate([obuf[s, h, y, x, c] for h in range(2)], axis=1)
+                    r = lax.dot_general(a_, w, NT, preferred_element_type=f32)
+                    for t in range(3):
+                        rt = r[:, 128 * t:128 * t + 128]
+                        @pl.when(i2 == 0)
+                        def _(): dn_ref[3 * q + t] = rt
+                        @pl.when(i2 > 0)
+                        def _(): dn_ref[3 * q + t] += rt
+                    return 0
+                lax.fori_loop(0, 8, rows, 0)
+                @pl.when(i2 == NO - 1)
+                def _(): dn_copy.start()
+            @pl.when(i >= Z0)
+            def _():
+                j = i - Z0
+                block = chunk(i - NO)
+                sf2_tile(j, block, par_ref[6:7, cols(4864, j)], ds_o, c_o, hp, x_s, yi_s, got, dn_ref, a1, a2)
+                mcopy(j).start()
+            return 0
+        lax.fori_loop(0, NI + NO + LAG + 1, loop, 0)
+
+        q = jnp.sum(a2[...], axis=1, keepdims=True) * (1.0 / 3072)
+        r = lax.rsqrt(jnp.sum(a1[...], axis=1, keepdims=True) * (1.0 / 3072) + 1e-5)
+        rq_o[0] = jnp.broadcast_to(r, (512, 128))
+        rq_o[1] = jnp.broadcast_to(r * r * r * q, (512, 128))
+        ent_o[...] = got[...]
+        pcopy(NI - 2).wait()
+        pcopy(NI - 1).wait()
+        lax.fori_loop(0, TILES, lambda j, _: (mcopy(j).wait(), 0)[1], 0)
+        lax.fori_loop(0, TILES, lambda j, _: (xcopy(j).wait(), 0)[1], 0)
+        dn_copy.wait()
+        low_copy.wait()
+        line.finish()
+        ga.finish()
+        gb.finish()
+        gz.finish()
+
+    D = pltpu.SemaphoreType.DMA
+    vm, hb = pl.BlockSpec(memory_space=pltpu.VMEM), pl.BlockSpec(memory_space=pl.ANY)
+    wi, wo = (NI, 2, 2, 2, 2, 192, 128), (NO, 2, 2, 2, 2, 384, 128)
+    tile = S((TILES, T, 256), f32)
+    col = S((T, 128), f32)
+    return pl.pallas_call(
+        kernel,
+        out_shape=(S((NI, TE, 256), f32), S(wi, bf), S(wo, bf), tile, tile, S((T, DM), bf), S((24, T, 128), f32), S((8, 7936), f32),
+                   S((TILES, 2, 128, 256), bf), col, col, S((TILES, 8, T), f32), col, col, S((2, T, 128), f32)),
+        in_specs=[vm] * 7,
+        out_specs=(hb,) * 7 + (vm,) * 8,
+        scratch_shapes=[V((32, 8, 256), f32), V((TE, DM), bf), V((16, DM), bf), V((2, TE, 256), f32), V((2,) + wi[1:], bf), V((2,) + wo[1:], bf),
+                        V((TILES, T, 256), f32), V((TILES, T, 256), f32), V((24, T, 128), f32), V((T, 256), f32), V((T, 256), f32), V((2, 264, 256), f32), V((2, 3, 128, 128), f32), V((2, 128, 256), f32)]
+        + Chain.scratch() + Gather.sems(FIRST, skew) + Gather.sems(NO, skew) + Gather.sems(TILES, skew)
+        + [D((31,)), D((31,)), D, D, D((2,)), D((2,)), D((2,)), D((TILES,)), D((TILES,)), D, D],
+        compiler_params=pltpu.CompilerParams(collective_id=collective_id, has_side_effects=True, vmem_limit_bytes=63 << 20),
+        name="front",
+    )(src_in, src_out, small, tokens, edge, cotangent, hp)
+
+
 def fast(adamw, tokens, cotangent, in_proj, in_mom, in_var, out_proj, out_mom, out_var, conv_params, conv_mom, conv_var,
          norm_gain, norm_mom, norm_var, gate_gain, gate_mom, gate_var, head_params, head_mom, head_var):
     line = lax.axis_index("dp") * 4 + lax.axis_index("seq")
     src_in, src_out, small = arrange(in_proj, out_proj, conv_params, norm_gain, gate_gain, line)
     edge = jnp.pad(tokens[:, 253:], ((0, 0), (0, 5), (0, 0))).reshape(16, 1536)
     tok, cot = tokens.reshape(512, 1536), cotangent.reshape(512, 1536)
-    proj, win, wout, low, par, dn = gather_call(src_in, src_out, small, tok, edge, cot, 1)
     hp = jnp.pad(head_params, ((0, 5), (0, 80)))
-    x, yi, ent, step, ds, dst, b, c = sf1(proj, par, hp)
-    mixed, rq = sf2(yi, x, ent, proj, dn, par, ds, c, hp)
+    proj, win, wout, x, mixed, low, dn, par, ent, step, ds, dst, b, c, rq = front_call(src_in, src_out, small, tok, edge, cot, hp, 1)
     low_t = low.T
     dz, ol, dcp, cg, hg, rows, sums = back_call(mixed, proj, dn, x, par, ent, ds, step, dst, b, c, hp, rq, low_t, cot, 5)
     skip = jnp.sum(rows[:, 1].reshape(48, 64), axis=1)
     heads = jnp.pad(jnp.concatenate([hg[0, :48], skip, hg[2, :48]])[None], ((0, 7), (0, 112)))
     last, block, tokens_grad, small_sum = end_call(low_t, dcp, dz, ol, win, wout, tok, cot, par, cg, rows, heads, 3)
     out_grad = sums[12:].reshape(6, 2, 2, 48, 128).transpose(1, 3, 0, 2, 4).reshape(96, 1536)
-    in_grad = jnp.concatenate([sums[:12].transpose(2, 0, 1, 3).reshape(48, 3072), last.transpose(2, 0, 1, 3).reshape(48, 3584)[:, :304 + 3072]], axis=1)
+    in_grad = jnp.concatenate([sums[:12].transpose(2, 0, 1, 3).reshape(48, 3072), jnp.concatenate([last[2:], last[1:2], last[:1]]).transpose(2, 0, 1, 3).reshape(48, 3584)[:, :3376]], axis=1)
     tokens_grad = tokens_grad.reshape(2, 256, 1536)
     mine = lambda row, n, w: lax.dynamic_slice(small_sum, (row, lax.rem(line * w, 128)), (n, w))
     conv_grad, norm_grad, gate_grad = mine(0, 5, 104), mine(5, 1, 48)[0], mine(6, 1, 96)[0]

time: 500 us -> 430 us (0.86)
  Pallas kernels: 461 us -> 391 us
    pallas_call x3 -> x1, Pallas kernels: 232 us -> 169 us  [front_call(): pl.pallas_call(kernel, out_shape=(S((NI, TE, 256), f32), S(wi, bf), S(wo,...]
    pallas_call x1, Pallas kernels: 153 us -> 146 us  [back_call(): pl.pallas_call(kernel, grid=(2 * TILES,), in_specs=in_specs, out_specs=ou...]
where the time goes in v4:
time: 430 us; the launch traced here: 429 us
  Pallas kernels  391 us (91%)
  local copies, waits for them, and re-layouts  25.9 us (6%)
  other arithmetic  11.5 us (3%)
    pallas_call x1, Pallas kernels, front_call(): pl.pallas_call(kernel, out_shape=(S((NI, TE, 256), f32), S(wi, bf), S(wo,...  169 us
    pallas_call x1, Pallas kernels, back_call(): pl.pallas_call(kernel, grid=(2 * TILES,), in_specs=in_specs, out_specs=ou...  146 us
    pallas_call x1, Pallas kernels, end_call(): pl.pallas_call(kernel, out_shape=(Sd((n, 2, R, 128), f32), Sd((512, 1536)...  76.3 us
    sub x6, other arithmetic, adamw(): weight - learn_rate * (mean_hat / (jnp.sqrt(var_hat) + adam_eps) + decay_...  10.1 us

profile of v4, /device:TPU:0, one launch (start us, length us, event | category | flops | bytes accessed | tf_op | source)
XLA Modules:
  0.0 429.3 jit_solution(17888214311140626022)
XLA Ops:
  0.7 0.0 copy-start
  0.7 1.4 pad.13.hp
  2.1 1.5 dynamic_update_slice.9
  3.6 0.8 dynamic_update_slice.10
  4.4 0.8 dynamic_update_slice.11.small_ref
  5.2 0.0 copy-start.11
  5.2 0.8 slice.49
  6.0 0.6 pad_bitcast_fusion.edge_ref
  6.6 1.1 convert_element_type.13
  7.7 0.1 reshape.92
  7.8 0.8 copy.59
  8.6 0.1 convert_element_type.12
  8.7 0.2 concatenate.12
  9.0 0.1 reshape.91
  9.1 0.9 copy.58
  10.0 168.7 %front.1 = (f32[26,528,256]{2,1,0:T(8,128)}, bf16[26,2,2,2,2,192,128]{6,5,4,3,2,1,0:T(8,128)(2,1)}, bf16[6,2,2,2,2,384,128]{6,5,4,3,2,1,0:T(8,128)(2,1)}, f32[12...) custom-call(bf16[26,2,48,128]{3,2,1,0:T(8,128)(2,1)} %bitcast.43, ...), custom_call_target="tpu_custom_call" | custom-call | tf_op jit(solution)/shard_map/front/pallas_call | solution.py:1344
  178.8 2.6 copy.51
  181.4 145.8 %back.1 = (bf16[12,512,256]{2,1,0:T(8,128)(2,1)}, bf16[512,3072]{1,0:T(8,128)(2,1)}, bf16[14,512,256]{2,1,0:T(8,128)(2,1)}, f32[13,8,256]{2,1,0:T(8,128)}, f32[8...) custom-call(f32[12,512,256]{2,1,0:T(8,128)} %get-tuple-element.53.mixed, ...), custom_call_target="tpu_custom_call" | custom-call | tf_op jit(solution)/shard_map/back/pallas_call | solution.py:994
  327.2 0.8 slice_bitcast_fusion.2
  328.0 0.9 slice_reduce_fusion
  328.9 0.1 reshape_squeeze.6
  329.0 0.1 reduce_sum.9
  329.1 0.1 pad_maximum_fusion.1
  329.2 0.6 pad.14.hg_ref
  329.8 0.0 copy-start.23
  329.8 0.0 copy-start.24
  329.8 0.0 copy-start.13
  329.8 0.0 copy-start.17
  329.8 0.0 copy-start.18
  329.9 0.0 copy-start.15
  329.9 0.0 copy-start.16
  329.9 76.3 %end.1 = (f32[14,2,48,128]{3,2,1,0:T(8,128)}, bf16[512,1536]{1,0:T(8,128)(2,1)}, f32[512,1536]{1,0:T(8,128)}, f32[8,256]{1,0:T(8,128)}) custom-call(bf16[4,2,192,512]{3,2,1,0:T(8,128)(2,1)} %bitcast.39, bf16[14,512,256]{2,1,0:T(8,128)(2,1)} %get-tuple-element.65.dcp_ref, bf16[12,512,256]{2,1,0:T(8,128)(2,1)} %get-tuple-element.66.dz_ref, ...), custom_call_target="tpu_custom_call" | custom-call | tf_op jit(solution)/shard_map/end/pallas_call | solution.py:1100
  406.2 0.7 slice_reduce_fusion.1
  406.9 0.1 reshape_squeeze.7
  407.0 0.0 copy-start.14
  407.0 1.3 multiply_subtract_fusion.4
  408.3 1.3 multiply_subtract_fusion.5
  409.7 0.6 multiply_subtract_fusion.3
  410.3 1.4 multiply_subtract_fusion.2
  411.7 0.8 fusion.13
  412.5 1.1 slice.54
  413.7 0.4 copy.54
  414.0 0.6 reshape.101
  414.6 1.5 copy-done.8
  416.1 0.1 fusion.12
  416.2 0.3 copy.55
  416.5 0.5 reshape.103
  417.0 0.0 copy-start.5
  417.0 0.0 copy-start.4
  417.0 0.0 copy-start.9
  417.1 0.3 copy.53
  417.4 0.0 copy-start.10
  417.4 0.5 reshape.100
  417.9 0.5 copy-done.4
  418.3 0.2 copy-done.9
  418.5 0.2 copy-done.10
  418.7 1.5 multiply_subtract_fusion.1
  420.2 0.2 copy-done.1
  420.4 0.4 slice-done
  420.8 0.4 copy-done.7
  421.2 4.0 multiply_subtract_fusion
  425.2 1.1 copy.65
  426.3 1.3 copy-done.2
  427.6 1.7 copy.66
  (36 shorter events, 0.2 us)
Async XLA Ops:
  0.7 7.9 %copy-start = (f32[48,6448]{1,0:T(8,128)S(1)}, f32[48,6448]{1,0:T(8,128)}, u32[]{:S(2)}) copy-start(f32[48,6448]{1,0:T(8,128)} %param.22) | copy-start | bytes 3714052
  5.2 3.5 copy-start.11
  329.8 77.2 %copy-start.19 = (f32[96]{0:T(128)S(1)}, f32[96]{0:T(128)}, u32[]{:S(2)}) copy-start(f32[96]{0:T(128)} %param.34) | copy-start | bytes 1156
  329.8 77.2 %copy-start.21 = (f32[96]{0:T(128)S(1)}, f32[96]{0:T(128)}, u32[]{:S(2)}) copy-start(f32[96]{0:T(128)} %param.35) | copy-start | bytes 1156
  329.8 77.2 %copy-start.22 = (f32[96]{0:T(128)S(1)}, f32[96]{0:T(128)}, u32[]{:S(2)}) copy-start(f32[96]{0:T(128)} %param.36) | copy-start | bytes 1156
  329.8 78.5 %copy-start.20 = (f32[48]{0:T(128)S(1)}, f32[48]{0:T(128)}, u32[]{:S(2)}) copy-start(f32[48]{0:T(128)} %param.31) | copy-start | bytes 580
  329.8 78.5 %copy-start.23 = (f32[48]{0:T(128)S(1)}, f32[48]{0:T(128)}, u32[]{:S(2)}) copy-start(f32[48]{0:T(128)} %param.32) | copy-start | bytes 580
  329.8 78.5 %copy-start.24 = (f32[48]{0:T(128)S(1)}, f32[48]{0:T(128)}, u32[]{:S(2)}) copy-start(f32[48]{0:T(128)} %param.33) | copy-start | bytes 580
  329.8 79.8 %copy-start.13 = (f32[3,48]{1,0:T(4,128)S(1)}, f32[3,48]{1,0:T(4,128)}, u32[]{:S(2)}) copy-start(f32[3,48]{1,0:T(4,128)} %param.37) | copy-start | bytes 1732
  329.8 79.8 %copy-start.17 = (f32[3,48]{1,0:T(4,128)S(1)}, f32[3,48]{1,0:T(4,128)}, u32[]{:S(2)}) copy-start(f32[3,48]{1,0:T(4,128)} %param.38) | copy-start | bytes 1732
  329.8 79.8 %copy-start.18 = (f32[3,48]{1,0:T(4,128)S(1)}, f32[3,48]{1,0:T(4,128)}, u32[]{:S(2)}) copy-start(f32[3,48]{1,0:T(4,128)} %param.39) | copy-start | bytes 1732
  329.8 80.4 %copy-start.12 = (f32[5,104]{1,0:T(8,128)S(1)}, f32[5,104]{1,0:T(8,128)}, u32[]{:S(2)}) copy-start(f32[5,104]{1,0:T(8,128)} %param.28) | copy-start | bytes 6244
  329.9 80.4 %copy-start.15 = (f32[5,104]{1,0:T(8,128)S(1)}, f32[5,104]{1,0:T(8,128)}, u32[]{:S(2)}) copy-start(f32[5,104]{1,0:T(8,128)} %param.29) | copy-start | bytes 6244
  329.9 80.4 %copy-start.16 = (f32[5,104]{1,0:T(8,128)S(1)}, f32[5,104]{1,0:T(8,128)}, u32[]{:S(2)}) copy-start(f32[5,104]{1,0:T(8,128)} %param.30) | copy-start | bytes 6244
  407.0 6.7 %copy-start.14 = (f32[3,48]{1,0:T(4,128)}, f32[3,48]{1,0:T(4,128)S(1)}, u32[]{:S(2)}) copy-start(f32[3,48]{1,0:T(4,128)S(1)} %reshape_squeeze.7) | copy-start | bytes 1732
  414.6 1.6 copy-start.3
  414.6 1.5 copy-start.8
  417.0 3.2 copy-start.5
  417.0 1.3 copy-start.4
  417.0 1.4 copy-start.9
  417.4 1.3 copy-start.10
  418.7 1.7 copy-start.1
  418.7 2.1 slice-start
  418.7 2.5 copy-start.7
  421.2 4.0 copy-start.6
  425.2 2.5 copy-start.2

commit v5 on v4

--- a/solution.py
+++ b/solution.py
@@ -401,17 +401,6 @@
             self.c4(i, s).wait_send()
 
 
-def arrange(in_proj, out_proj, conv_params, norm_gain, gate_gain, line):
-    w = in_proj.astype(bf)
-    w = jnp.concatenate([w[:, 6400:], jnp.zeros((48, 208), bf), w[:, 6144:6400], w[:, 3072:6144], w[:, :3072]], axis=1)
-    src_in = w.reshape(48, 26, 2, 128).transpose(1, 2, 0, 3)
-    src_out = out_proj.astype(bf).reshape(96, 6, 2, 128).transpose(1, 2, 0, 3)
-    small = jnp.zeros((8, 256), f32)
-    for rows, row, width in ((conv_params, 0, 104), (norm_gain[None], 5, 48), (gate_gain[None], 6, 96)):
-        small = lax.dynamic_update_slice(small, rows, (row, lax.rem(line * width, 128)))
-    return src_in, src_out, small
-
-
 TILES = 12
 NN, NT, TN_ = (((1,), (0,)), ((), ())), (((1,), (1,)), ((), ())), (((0,), (0,)), ((), ()))
 
@@ -570,8 +559,8 @@
 V = pltpu.VMEM
 
 
-def sb1_start(b_r, c_r, dst_acc, dc_acc, dds_acc, xu_acc, st_s, ct_s):
-    for a in (dst_acc, dc_acc, dds_acc, xu_acc):
+def sb1_start(b_r, c_r, dst_acc, dc_acc, dds_acc, xu_acc, skips, st_s, ct_s):
+    for a in (dst_acc, dc_acc, dds_acc, xu_acc, skips):
         a[...] = jnp.zeros_like(a)
     for g in range(2):
         b, c = b_r[256 * g:256 * g + 256], c_r[256 * g:256 * g + 256]
@@ -582,7 +571,7 @@
 
 
 def sb1_tile(j, mixed, z, dn, x, ent, gain, ds, step, dst, hp, rq, dxa_s, dz_o, dz_s, ol_o, lhs_s, rows_o,
-             dst_acc, dc_acc, dds_acc, xu_acc, st_s, ct_s, part):
+             dst_acc, dc_acc, dds_acc, xu_acc, skips, st_s, ct_s, part):
     rds = rolled(ds[...], j)
     dsc = spread(rds)
     stc = spread(rolled(step[...], j))
@@ -645,8 +634,8 @@
         xu_acc[r] += to_heads(xx * u, spot)
         dxa_s[j, r] = skip * dy + stc[r] * u
     rows_o[j, 0:1] = dgain
-    rows_o[j, 1:2] = dskip
-    rows_o[j, 2:8] = jnp.zeros((6, 256), f32)
+    rows_o[j, 1:8] = jnp.zeros((7, 256), f32)
+    skips[...] += to_heads(jnp.broadcast_to(dskip, (8, 256)), spot)
     turned = jnp.concatenate(turned, 1)
     for k in range(16):
         at = 16 * j + k
@@ -713,7 +702,7 @@
             dcp_o[j + 2, 256 * g:256 * g + 256] = din[g].astype(bf)
         pass_edge(j, prev, din)
 
-    def final(bcin, bchalo, bctaps, raw, ds, step, b_r, c_r, hp, dst_acc, dc_acc, dds_acc, xu_acc):
+    def final(bcin, bchalo, bctaps, raw, ds, step, b_r, c_r, hp, dst_acc, dc_acc, dds_acc, xu_acc, skips):
         fill_pad(pad2, bcin[0], bchalo[0])
         dco2 = []
         for g, co in enumerate(conv(pad2, bctaps)):
@@ -749,7 +738,7 @@
         dcp_o[0, :, 0:128] = draw.astype(bf)
         dcp_o[0, :, 128:256] = jnp.zeros((512, 128), bf)
         hg_o[0:1] = jnp.sum(drate * st * speed, axis=0, keepdims=True)
-        hg_o[1:2] = jnp.zeros((1, 128), f32)
+        hg_o[1:2] = skips[0:1]
         hg_o[2:3] = jnp.sum(draw, axis=0, keepdims=True)
         hg_o[3:8] = jnp.zeros((5, 128), f32)
 
@@ -786,14 +775,14 @@
 class Reduce:
     def __init__(self, me, n, rows, refs, skew):
         self.me, self.n, self.rows, self.sk, self.slots, self.ring = me, n, rows, skew, skew + 1, skew + 2
-        (self.own0, self.own1, self.own2, self.own3, self.s0, self.s1, self.s2, self.s3, self.r0, self.r1, self.r2, self.r3,
+        (self.own1, self.own2, self.own3, self.s0, self.s1, self.s2, self.s3, self.r0, self.r1, self.r2, self.r3,
          self.o0, self.o1, self.o2, self.o3, self.i0, self.i1, self.i2, self.i3, self.free) = refs
 
     @staticmethod
     def scratch(n, rows, skew):
         V, D, k = pltpu.VMEM, pltpu.SemaphoreType.DMA, skew + 1
         z = 4 * rows
-        return [V((k, 2, 2, 2, z, 128), f32), V((k, 2, 2, z, 128), f32), V((k, 2, z, 128), f32), V((k, 2, rows, 128), f32),
+        return [V((k, 2, 2, z, 128), f32), V((k, 2, z, 128), f32), V((k, 2, rows, 128), f32),
                 V((k, 2, 2, 2, z, 128), f32), V((k, 2, 2, z, 128), bf), V((k, 2, z, 128), bf), V((k, 3, 2, rows, 128), bf),
                 V((skew + 2, 2, 2, 2, z, 128), f32), V((n, 2, 2, z, 128), bf), V((n, 2, z, 128), bf), V((n, 3, 2, rows, 128), bf),
                 D((k,)), D((k, 2)), D((k, 2)), D((k, 3)), D((n,)), D((n, 2)), D((n, 2)), D((n, 3)), pltpu.SemaphoreType.REGULAR]
@@ -810,7 +799,7 @@
     def c3(self, i, s, k):
         return send(self.s3.at[s, k - 1], self.r3.at[i, k - 1], self.o3.at[s, k - 1], self.i3.at[i, k - 1], self.me.z_peer(k))
 
-    def step(self, it, product, out_ref):
+    def step(self, it, product, put):
         n, sk, ns, R = self.n, self.sk, self.slots, self.rows
         me, x, y, z, c = self.me, self.me.x, self.me.y, self.me.z, self.me.c
 
@@ -823,31 +812,37 @@
         def zero(i, s):
             @pl.when(i >= ns)
             def _(): self.c0(i, s).wait_send()
-            part = product(i, 1 - c)
+            part = product(i, 1 - c, ((0, 0), (0, 1), (1, 0), (1, 1))).reshape(2, 2, 4 * R, 256)
             for h in range(2):
                 self.s0[s, h] = part[..., h * 128:(h + 1) * 128]
             @pl.when(i >= self.ring)
             def _(): pl.semaphore_wait(self.free, 1)
             self.c0(i, s).start()
-            part = product(i, c)
-            for h in range(2):
-                self.own0[s, h] = part[..., h * 128:(h + 1) * 128]
 
         def first(i, s):
-            own0, r0, own1 = self.own0, self.r0, self.own1
+            r0, own1, s1 = self.r0, self.own1, self.s1
             q = lax.rem(i, self.ring)
             @pl.when(i >= ns)
             def _():
                 for h in range(2): self.c1(i, s, h).wait_send()
+            blocks = [(yy, xx) for xx in (1 - x, x) for yy in (1 - y, y)]
+            part = product(i, c, blocks)
             self.c0(i, s).wait_recv()
-            for a in range(2):
-                self.s1[s, 0, a] = (own0[s, 0, a, 1 - x] + r0[q, 0, a, 1 - x]).astype(bf)
-            self.c1(i, s, 0).start()
-            self.s1[s, 1] = (own0[s, 1, 1 - y] + r0[q, 1, 1 - y]).astype(bf)
-            self.c1(i, s, 1).start()
-            for a in range(2):
-                own1[s, 0, a] = own0[s, 0, a, x] + r0[q, 0, a, x]
-            own1[s, 1] = own0[s, 1, y] + r0[q, 1, y]
+            for k, (yy, xx) in enumerate(blocks):
+                a = part[k, :, :128] + r0[q, 0, yy, xx]
+                b = part[k, :, 128:] + r0[q, 1, yy, xx]
+                if k < 2:
+                    s1[s, 0, yy] = a.astype(bf)
+                else:
+                    own1[s, 0, yy] = a
+                if k % 2 == 0:
+                    s1[s, 1, xx] = b.astype(bf)
+                else:
+                    own1[s, 1, xx] = b
+                if k == 1:
+                    self.c1(i, s, 0).start()
+                if k == 2:
+                    self.c1(i, s, 1).start()
             pl.semaphore_signal(self.free, inc=1, device_id=me.core_peer, device_id_type=MESH)
 
         def second(i, s):
@@ -880,11 +875,9 @@
             for k in (1, 2, 3): self.c3(i, s, k).wait_recv()
             acc = self.own3[s]
             for k in range(3): acc = acc + self.r3[i, k].astype(f32)
-            out_ref[i] = acc
-
-        if product is not None:
-            stage(0, zero)
-        stage(1, first); stage(2, second); stage(3, third); stage(4, last)
+            put(i, acc)
+
+        stage(0, zero); stage(1, first); stage(2, second); stage(3, third); stage(4, last)
 
     def finish(self):
         for j in range(self.slots):
@@ -914,8 +907,8 @@
     n, R, sk = 24, 48, 1
 
     def kernel(mixed, z, dn, x, gain, cin, halo, taps, ent, ds, step, dst, b_r, c_r, hp, rq, bcin, bchalo, bctaps, raw, low_t, cot,
-               dz_o, ol_o, dcp_o, cg_o, hg_o, rows_o, sums,
-               dst_acc, dc_acc, dds_acc, xu_acc, st_s, ct_s, got, part, out, out_sem, in_sem,
+               dz_o, ol_o, dcp_o, cg_o, hg_o, rows_o, zsum, osum,
+               dst_acc, dc_acc, dds_acc, xu_acc, skips, st_s, ct_s, got, part, out, out_sem, in_sem,
                pad, pad2, dpad, dpad2, db_s, xut_s, de_s, prv, lst, edge_in, e_out, e_in,
                dxa_s, dz_s, rhs, lhs_s, *refs):
         j = pl.program_id(0)
@@ -924,26 +917,38 @@
         red = Reduce(me, n, R, refs, sk)
         two_start, two_tile, two_final = sb2_make(me, dcp_o, cg_o, hg_o, pad, pad2, dpad, dpad2, db_s, xut_s, de_s, prv, lst, edge_in, e_out, e_in)
 
+        def product(i, core, blocks):
+            li = i // 12 * (1 + lax.rem(i, 2))
+            rows = [lhs_s[li, 2 * yy + xx, core].reshape(4 * R, 512) for yy, xx in blocks]
+            return jnp.dot(jnp.concatenate(rows, 0), rhs[lax.rem(i, 2)], preferred_element_type=f32).reshape(4, 4 * R, 256)
+
+        def put(i, acc):
+            both = jnp.concatenate([acc[0], acc[1]], 1)
+            @pl.when(i < 12)
+            def _(): zsum[:, pl.ds(pl.multiple_of(i * 256, 256), 256)] = both
+            @pl.when(i >= 12)
+            def _():
+                k = i - 12
+                osum[pl.ds(pl.multiple_of(lax.rem(k, 2) * 48, 16), 48), pl.ds(pl.multiple_of(k // 2 * 256, 256), 256)] = both
+
         def rs(it):
-            outer = it // 12
-            li = outer * (1 + lax.rem(it, 2))
             @pl.when(it < 12)
-            def _(): rhs[...] = dz_s[...]
+            def _(): rhs[lax.rem(it, 2)] = dz_s[...]
             @pl.when((it >= 12) & (it < n))
-            def _(): rhs[...] = cot[:, pl.ds(pl.multiple_of((it - 12) // 2 * 256, 256), 256)]
-            red.step(it, lambda i, c: jnp.dot(lhs_s[li, :, c].reshape(16 * R, 512), rhs[...], preferred_element_type=f32).reshape(2, 2, 4 * R, 256), sums)
+            def _(): rhs[lax.rem(it, 2)] = cot[:, pl.ds(pl.multiple_of((it - 12) // 2 * 256, 256), 256)]
+            red.step(it, product, put)
 
         @pl.when(j == 0)
         def _():
             greet(me.near())
             line.start()
-            sb1_start(b_r, c_r, dst_acc, dc_acc, dds_acc, xu_acc, st_s, ct_s)
+            sb1_start(b_r, c_r, dst_acc, dc_acc, dds_acc, xu_acc, skips, st_s, ct_s)
             lhs_s[0] = low_t[...]
 
         @pl.when(j < TILES)
         def _():
             sb1_tile(j, mixed, z, dn, x, ent, gain, ds, step, dst, hp, rq, dxa_s, dz_o, dz_s, ol_o, lhs_s, rows_o,
-                     dst_acc, dc_acc, dds_acc, xu_acc, st_s, ct_s, part)
+                     dst_acc, dc_acc, dds_acc, xu_acc, skips, st_s, ct_s, part)
         line.four_of_seven(j)
 
         @pl.when(j == TILES)
@@ -956,9 +961,9 @@
 
         @pl.when(j == 2 * TILES - 1)
         def _():
-            two_final(bcin, bchalo, bctaps, raw, ds, step, b_r, c_r, hp, dst_acc, dc_acc, dds_acc, xu_acc)
+            two_final(bcin, bchalo, bctaps, raw, ds, step, b_r, c_r, hp, dst_acc, dc_acc, dds_acc, xu_acc, skips)
             line.finish()
-            lax.fori_loop(n, n + 4 * sk, lambda it, _: (rs_drain(red, it, sums), 0)[1], 0)
+            lax.fori_loop(n, n + 4 * sk, lambda it, _: (rs(it), 0)[1], 0)
             red.finish()
 
     D = pltpu.SemaphoreType.DMA
@@ -980,25 +985,21 @@
     out_specs = (
         pl.BlockSpec((1, 512, 256), lambda j: (p1(j), 0, 0)),
         pl.BlockSpec((512, 256), lambda j: (0, p1(j))),
-        one_time(14, 512, 256), one_time(13, 8, 256), one_time(8, 128), one_time(12, 8, 256), one_time(24, 2, 48, 128),
-    )
-    out_shape = (S((12, 512, 256), bf), S((512, 3072), bf), S((14, 512, 256), bf), S((13, 8, 256), f32), S((8, 128), f32), S((12, 8, 256), f32), S((24, 2, 48, 128), f32))
+        one_time(14, 512, 256), one_time(13, 8, 256), one_time(8, 128), one_time(12, 8, 256), one_time(48, 3072), one_time(96, 1536),
+    )
+    out_shape = (S((12, 512, 256), bf), S((512, 3072), bf), S((14, 512, 256), bf), S((13, 8, 256), f32), S((8, 128), f32), S((12, 8, 256), f32), S((48, 3072), f32), S((96, 1536), f32))
     scratch = (
-        [V((2, 3, 128, 128), f32), V((512, 128), f32), V((512, 128), f32), V((512, 128), f32), V((2, 3, 128, 128), f32), V((2, 128, 256), f32)]
+        [V((2, 3, 128, 128), f32), V((512, 128), f32), V((512, 128), f32), V((512, 128), f32), V((8, 128), f32), V((2, 3, 128, 128), f32), V((2, 128, 256), f32)]
         + Chain.scratch()
         + [V((2, 264, 256), f32), V((2, 264, 256), f32), V((2, 272, 256), f32), V((2, 272, 256), f32), V((512, 128), f32), V((512, 128), f32), V((2, 8, 128), f32),
            V((13, 16, 256), bf), V((13, 16, 256), f32), V((13, 16, 256), bf), D((13,)), D((13,))]
-        + [V((12, 512, 256), f32), V((512, 256), bf), V((512, 256), bf), V((3, 4, 2, 4, 48, 512), bf)]
+        + [V((12, 512, 256), f32), V((512, 256), bf), V((2, 512, 256), bf), V((3, 4, 2, 4, 48, 512), bf)]
         + Reduce.scratch(n, R, sk)
     )
     return pl.pallas_call(
         kernel, grid=(2 * TILES,), in_specs=in_specs, out_specs=out_specs, out_shape=out_shape, scratch_shapes=scratch,
         compiler_params=pltpu.CompilerParams(vmem_limit_bytes=63 << 20, collective_id=collective_id, has_side_effects=True), name="back",
     )(mixed, proj, dn, x, par, proj, proj, par, ent, ds, step, dst, b, c, hp, rq, proj, proj, par, proj, low_t.reshape(4, 2, 4, 48, 512), cot)
-
-
-def rs_drain(red, it, sums):
-    red.step(it, None, sums)
 
 
 def end_call(low_t, dcp, dz, ol, win, wout, tok, cot, par, cg, rows, hg, collective_id, skew=2):
@@ -1044,13 +1045,23 @@
             flat[5:6, 0:1536] = norm
             for j in range(12):
                 flat[6:7, 256 * j:256 * j + 256] = rows_ref[j, 0:1]
+            turned = pltpu.roll(hg_ref[...], 64, 1)
+            heads = jnp.concatenate([hg_ref[0:1] + turned[2:3], hg_ref[1:2]], 1)
             for o in range(32):
                 b = [(o * w // 128) * 128 for w in (104, 48, 96)]
                 mail[o, 0:5] = flat[0:5, b[0]:b[0] + 256]
                 mail[o, 5:6] = flat[5:6, b[1]:b[1] + 256]
                 mail[o, 6:7] = flat[6:7, b[2]:b[2] + 256]
-                mail[o, 7:8] = hg_ref[0:1]
+                mail[o, 7:8] = heads
             lax.fori_loop(1, 32, lambda k, _: (post(k).start(), 0)[1], 0)
+
+        def product(i, core, blocks):
+            rows = [lhs[2 * yy + xx, core] for yy, xx in blocks]
+            return jnp.dot(jnp.concatenate(rows, 0), dcp_ref[i], preferred_element_type=f32).reshape(4, 4 * R, 256)
+
+        def put(i, acc):
+            at = jnp.where(i == 0, 13 * 256, jnp.where(i == 1, 12 * 256, (i - 2) * 256))
+            sums[:, pl.ds(pl.multiple_of(at, 256), 256)] = jnp.concatenate([acc[0], acc[1]], 1)
 
         def dgrad(t, q, dp):
             s = lax.rem(t, 2)
@@ -1058,7 +1069,7 @@
             return lax.dot_general(dp, w, (((1,), (1,)), ((), ())), preferred_element_type=f32)
 
         def loop(it, _):
-            red.step(it, lambda i, c: jnp.dot(lhs[:, c].reshape(16 * R, 512), dcp_ref[i], preferred_element_type=f32).reshape(2, 2, 4 * R, 256), sums)
+            red.step(it, product, put)
             @pl.when(it < n)
             def _():
                 @pl.when(it + 1 < n)
@@ -1098,7 +1109,7 @@
     D, Sd = pltpu.SemaphoreType.DMA, jax.ShapeDtypeStruct
     vm, hb = pl.BlockSpec(memory_space=pltpu.VMEM), pl.BlockSpec(memory_space=pl.ANY)
     return pl.pallas_call(
-        kernel, out_shape=(Sd((n, 2, R, 128), f32), Sd((512, 1536), bf), Sd((512, 1536), f32), Sd((8, 256), f32)),
+        kernel, out_shape=(Sd((R, n * 256), f32), Sd((512, 1536), bf), Sd((512, 1536), f32), Sd((8, 256), f32)),
         in_specs=[vm] * 4 + [hb] * 2 + [vm] * 6, out_specs=(vm, vm, vm, vm),
         scratch_shapes=[V((2, 2, 2, 2, 2, 2, 192, 128), bf), D((2, 2)), V((2, 2, 2, 2, 2, 384, 128), bf), D((2,)),
                         V((512, 1536), f32), V((8, 3584), f32), V((32, 8, 256), f32), V((31, 8, 256), f32), D((31,)), D((31,))]
@@ -1178,16 +1189,17 @@
         a2[r] += gain * jnp.concatenate([dn[2 * j, r], dn[2 * j + 1, r]], 1) * gated
 
 
-def front_call(src_in, src_out, small, tokens, edge, cotangent, hp, collective_id, skew=2):
-    NI, NO = src_in.shape[0], src_out.shape[0]
+def front_call(in_proj, out_proj, conv_params, norm_gain, gate_gain, head_params, tokens, cotangent, collective_id, skew=2):
+    NI, NO = 26, 6
+    AT = [6400, 6144] + [3072 + 256 * p for p in range(12)] + [256 * p for p in range(12)]
     T, DM = tokens.shape
     TE = T + 16
     FIRST = NI - TILES
     Z0 = FIRST + NO
 
-    def kernel(src_in, src_out, small_ref, tok_ref, edge_ref, cot_ref, hp,
-               proj_hbm, win, wout, x_hbm, mixed_hbm, low_hbm, dn_hbm, par_ref, ent_o, step_o, ds_o, dst_o, b_o, c_o, rq_o,
-               sm, low_e, edge_in, pbuf, wbuf, obuf, x_s, yi_s, dn_ref, a1, a2, pad, s_s, bt_s, got, part, out, out_sem, in_sem, *sems):
+    def kernel(in_ref, out_ref, conv_ref, norm_ref, gate_ref, head_ref, tok_ref, cot_ref,
+               proj_hbm, win, wout, x_hbm, mixed_hbm, low_hbm, dn_hbm, hp, par_ref, ent_o, step_o, ds_o, dst_o, b_o, c_o, rq_o,
+               src_in, src_out, small_ref, edge_ref, low_t, sm, low_e, edge_in, pbuf, wbuf, obuf, x_s, yi_s, dn_ref, a1, a2, pad, s_s, bt_s, got, part, out, out_sem, in_sem, *sems):
         gs, os_, zs, (sm_out, sm_in, ed_out, ed_in, pb_sem, wl_sem, ol_sem, x_sem, mx_sem, dn_sem, low_sem) = sems[:9], sems[9:18], sems[18:27], sems[27:]
         me = Place()
         bar = pltpu.get_barrier_semaphore()
@@ -1201,6 +1213,28 @@
         gz = Gather(me, NI - FIRST, src_in, win, zs, skew, FIRST)
         line = Chain(me, 1, got, part, out, out_sem, in_sem, keeper(ds_o))
 
+        def take(p):
+            if p == 0:
+                src_in[0] = jnp.zeros((2, 48, 128), bf)
+                src_in[0, 0, :, 0:48] = in_ref[:, 6400:6448].astype(bf)
+            else:
+                for h in range(2):
+                    src_in[p, h] = in_ref[:, AT[p] + 128 * h:AT[p] + 128 * h + 128].astype(bf)
+        small_ref[...] = jnp.zeros_like(small_ref)
+        small_ref[0:5, 0:104] = conv_ref[...]
+        small_ref[5:6, 0:48] = norm_ref[...]
+        small_ref[6:7, 0:96] = gate_ref[...]
+        row = lax.broadcasted_iota(jnp.int32, (8, 256), 0)
+        first, second, third = (pltpu.roll(small_ref[...], lax.rem(me.line * w, 128), 1) for w in (104, 48, 96))
+        small_ref[...] = jnp.where(row < 5, first, jnp.where(row == 5, second, third))
+        row = lax.broadcasted_iota(jnp.int32, (16, DM), 0)
+        ends = [tok_ref[256 * g + 240:256 * g + 256].astype(f32) for g in range(2)]
+        edge_ref[...] = jnp.where(row < 8, pltpu.roll(ends[0], 3, 0), pltpu.roll(ends[1], 11, 0)).astype(bf)
+        hp[...] = jnp.zeros_like(hp)
+        hp[0:3, 0:48] = head_ref[...]
+        take(0)
+        take(1)
+
         def small_copy(k):
             return send(small_ref, sm.at[me.line], sm_out.at[k - 1], sm_in.at[k - 1], me.any_peer(k))
         def edge_copy():
@@ -1210,6 +1244,10 @@
         sm[me.line] = small_ref[...]
         ga.step(0)
         ga.step(1)
+        for p in range(2, NI): take(p)
+        for p in range(NO):
+            for h in range(2):
+                src_out[p, h] = out_ref[:, 256 * p + 128 * h:256 * p + 128 * h + 128].astype(bf)
         line.start()
         a1[...] = jnp.zeros_like(a1)
         a2[...] = jnp.zeros_like(a2)
@@ -1233,9 +1271,8 @@
             return 0
         lax.fori_loop(0, T // 64, nloop, 0)
         low_e[T:] = norm(edge_in[...].astype(f32) * keep)
-        low_copy = pltpu.make_async_copy(low_e.at[0:T], low_hbm, low_sem)
+        low_copy = pltpu.make_async_copy(low_t, low_hbm, low_sem)
         dn_copy = pltpu.make_async_copy(dn_ref, dn_hbm, dn_sem)
-        low_copy.start()
 
         def two(i): return lax.rem(i, 2)
         def pcopy(i): return pltpu.make_async_copy(pbuf.at[two(i)], proj_hbm.at[i], pb_sem.at[two(i)])
@@ -1261,6 +1298,12 @@
             def _(): ga.step(it)
             gb.step(it - FIRST)
             gz.step(it - Z0)
+            @pl.when((it >= 2) & (it < 6))
+            def _():
+                rows = pl.ds(pl.multiple_of((it - 2) * 128, 128), 128)
+                low_t[:, rows] = low_e[rows].astype(f32).T.astype(bf)
+            @pl.when(it == 6)
+            def _(): low_copy.start()
             a = it - LAG
             @pl.when((a >= 0) & (a < FIRST))
             def _():
@@ -1343,38 +1386,33 @@
     col = S((T, 128), f32)
     return pl.pallas_call(
         kernel,
-        out_shape=(S((NI, TE, 256), f32), S(wi, bf), S(wo, bf), tile, tile, S((T, DM), bf), S((24, T, 128), f32), S((8, 7936), f32),
+        out_shape=(S((NI, TE, 256), f32), S(wi, bf), S(wo, bf), tile, tile, S((DM, T), bf), S((24, T, 128), f32), S((8, 128), f32), S((8, 7936), f32),
                    S((TILES, 2, 128, 256), bf), col, col, S((TILES, 8, T), f32), col, col, S((2, T, 128), f32)),
-        in_specs=[vm] * 7,
-        out_specs=(hb,) * 7 + (vm,) * 8,
-        scratch_shapes=[V((32, 8, 256), f32), V((TE, DM), bf), V((16, DM), bf), V((2, TE, 256), f32), V((2,) + wi[1:], bf), V((2,) + wo[1:], bf),
+        in_specs=[vm] * 8,
+        out_specs=(hb,) * 7 + (vm,) * 9,
+        scratch_shapes=[V((NI, 2, 48, 128), bf), V((NO, 2, 96, 128), bf), V((8, 256), f32), V((16, DM), bf), V((DM, T), bf), V((32, 8, 256), f32), V((TE, DM), bf), V((16, DM), bf), V((2, TE, 256), f32), V((2,) + wi[1:], bf), V((2,) + wo[1:], bf),
                         V((TILES, T, 256), f32), V((TILES, T, 256), f32), V((24, T, 128), f32), V((T, 256), f32), V((T, 256), f32), V((2, 264, 256), f32), V((2, 3, 128, 128), f32), V((2, 128, 256), f32)]
         + Chain.scratch() + Gather.sems(FIRST, skew) + Gather.sems(NO, skew) + Gather.sems(TILES, skew)
         + [D((31,)), D((31,)), D, D, D((2,)), D((2,)), D((2,)), D((TILES,)), D((TILES,)), D, D],
         compiler_params=pltpu.CompilerParams(collective_id=collective_id, has_side_effects=True, vmem_limit_bytes=63 << 20),
         name="front",
-    )(src_in, src_out, small, tokens, edge, cotangent, hp)
+    )(in_proj, out_proj, conv_params, norm_gain, gate_gain, head_params, tokens, cotangent)
 
 
 def fast(adamw, tokens, cotangent, in_proj, in_mom, in_var, out_proj, out_mom, out_var, conv_params, conv_mom, conv_var,
          norm_gain, norm_mom, norm_var, gate_gain, gate_mom, gate_var, head_params, head_mom, head_var):
     line = lax.axis_index("dp") * 4 + lax.axis_index("seq")
-    src_in, src_out, small = arrange(in_proj, out_proj, conv_params, norm_gain, gate_gain, line)
-    edge = jnp.pad(tokens[:, 253:], ((0, 0), (0, 5), (0, 0))).reshape(16, 1536)
     tok, cot = tokens.reshape(512, 1536), cotangent.reshape(512, 1536)
-    hp = jnp.pad(head_params, ((0, 5), (0, 80)))
-    proj, win, wout, x, mixed, low, dn, par, ent, step, ds, dst, b, c, rq = front_call(src_in, src_out, small, tok, edge, cot, hp, 1)
-    low_t = low.T
-    dz, ol, dcp, cg, hg, rows, sums = back_call(mixed, proj, dn, x, par, ent, ds, step, dst, b, c, hp, rq, low_t, cot, 5)
-    skip = jnp.sum(rows[:, 1].reshape(48, 64), axis=1)
-    heads = jnp.pad(jnp.concatenate([hg[0, :48], skip, hg[2, :48]])[None], ((0, 7), (0, 112)))
-    last, block, tokens_grad, small_sum = end_call(low_t, dcp, dz, ol, win, wout, tok, cot, par, cg, rows, heads, 3)
-    out_grad = sums[12:].reshape(6, 2, 2, 48, 128).transpose(1, 3, 0, 2, 4).reshape(96, 1536)
-    in_grad = jnp.concatenate([sums[:12].transpose(2, 0, 1, 3).reshape(48, 3072), jnp.concatenate([last[2:], last[1:2], last[:1]]).transpose(2, 0, 1, 3).reshape(48, 3584)[:, :3376]], axis=1)
+    proj, win, wout, x, mixed, low_t, dn, hp, par, ent, step, ds, dst, b, c, rq = front_call(
+        in_proj, out_proj, conv_params, norm_gain[None], gate_gain[None], head_params, tok, cot, 1
+    )
+    dz, ol, dcp, cg, hg, rows, z_sum, out_grad = back_call(mixed, proj, dn, x, par, ent, ds, step, dst, b, c, hp, rq, low_t, cot, 5)
+    last, block, tokens_grad, small_sum = end_call(low_t, dcp, dz, ol, win, wout, tok, cot, par, cg, rows, hg, 3)
+    in_grad = jnp.concatenate([z_sum, last[:, :3376]], axis=1)
     tokens_grad = tokens_grad.reshape(2, 256, 1536)
     mine = lambda row, n, w: lax.dynamic_slice(small_sum, (row, lax.rem(line * w, 128)), (n, w))
     conv_grad, norm_grad, gate_grad = mine(0, 5, 104), mine(5, 1, 48)[0], mine(6, 1, 96)[0]
-    head_grad = small_sum[7, :144].reshape(3, 48)
+    head_grad = jnp.stack([small_sum[7, 0:48], small_sum[7, 128:176], small_sum[7, 64:112]])
     res = [(in_proj, in_mom, in_var, in_grad, 0.1), (out_proj, out_mom, out_var, out_grad, 0.1), (conv_params, conv_mom, conv_var, conv_grad, 0.1),
            (norm_gain, norm_mom, norm_var, norm_grad, 0.0), (gate_gain, gate_mom, gate_var, gate_grad, 0.0), (head_params, head_mom, head_var, head_grad, 0.0)]
     new = [v for a in res for v in adamw(*a)]

time: 430 us -> 402 us (0.935)
  local copies, waits for them, and re-layouts: 25.9 us -> 7.58 us
  Pallas kernels: 391 us -> 385 us
where the time goes in v5:
time: 402 us
  Pallas kernels  385 us (96%)
  other arithmetic  8.4 us (2%)
  local copies, waits for them, and re-layouts  7.58 us (2%)
    pallas_call x1, Pallas kernels, front_call(): pl.pallas_call(kernel, out_shape=(S((NI, TE, 256), f32), S(wi, bf), S(wo,...  169 us
    pallas_call x1, Pallas kernels, back_call(): pl.pallas_call(kernel, grid=(2 * TILES,), in_specs=in_specs, out_specs=ou...  143 us
    pallas_call x1, Pallas kernels, end_call(): pl.pallas_call(kernel, out_shape=(Sd((R, n * 256), f32), Sd((512, 1536),...  73.3 us
    sub x6, other arithmetic, adamw(): weight - learn_rate * (mean_hat / (jnp.sqrt(var_hat) + adam_eps) + decay_...  8.4 us

profile of v5, /device:TPU:0, one launch (start us, length us, event | category | flops | bytes accessed | tf_op | source)
XLA Modules:
  0.0 402.0 jit_solution(8364316945546549441)
XLA Ops:
  0.7 168.8 %front.1 = (f32[26,528,256]{2,1,0:T(8,128)}, bf16[26,2,2,2,2,192,128]{6,5,4,3,2,1,0:T(8,128)(2,1)}, bf16[6,2,2,2,2,384,128]{6,5,4,3,2,1,0:T(8,128)(2,1)}, f32[12...) custom-call(f32[48,6448]{1,0:T(8,128)} %in_ref.1, ...), custom_call_target="tpu_custom_call" | custom-call | tf_op jit(solution)/shard_map/front/pallas_call | solution.py:1387
  169.5 143.0 %back.1 = (bf16[12,512,256]{2,1,0:T(8,128)(2,1)}, bf16[512,3072]{1,0:T(8,128)(2,1)}, bf16[14,512,256]{2,1,0:T(8,128)(2,1)}, f32[13,8,256]{2,1,0:T(8,128)}, f32[8...) custom-call(f32[12,512,256]{2,1,0:T(8,128)} %get-tuple-element.55.mixed, ...), custom_call_target="tpu_custom_call" | custom-call | tf_op jit(solution)/shard_map/back/pallas_call | solution.py:999
  312.5 0.0 copy-start.9
  312.5 0.0 copy-start.15
  312.5 0.0 copy-start.16
  312.5 0.0 copy-start.5
  312.5 73.3 %end.1 = (f32[48,3584]{1,0:T(8,128)}, bf16[512,1536]{1,0:T(8,128)(2,1)}, f32[512,1536]{1,0:T(8,128)}, f32[8,256]{1,0:T(8,128)}) custom-call(bf16[4,2,192,512]{3,2,1,0:T(8,128)(2,1)} %bitcast.20, bf16[14,512,256]{2,1,0:T(8,128)(2,1)} %get-tuple-element.68.dcp_ref, bf16[12,512,256]{2,1,0:T(8,128)(2,1)} %get-tuple-element.69.dz_ref, ...), custom_call_target="tpu_custom_call" | custom-call | tf_op jit(solution)/shard_map/end/pallas_call | solution.py:1111
  385.9 0.0 copy-start
  385.9 0.9 fusion.12
  386.7 0.0 copy-done.9
  386.7 0.0 copy-done.15
  386.7 0.0 copy-done.16
  386.7 0.6 multiply_subtract_fusion.3
  387.4 1.1 slice.12
  388.5 0.0 copy-done.5
  388.5 0.0 copy-done
  388.5 0.0 copy-start.8
  388.5 0.0 copy-start.10
  388.5 0.0 copy-start.11
  388.6 0.0 copy-start.12
  388.6 0.0 copy-start.13
  388.6 0.0 copy-start.17
  388.6 0.0 copy-start.18
  388.6 0.0 copy-start.14
  388.6 0.0 copy-start.19
  388.6 0.0 copy-start.20
  388.6 0.0 copy-start.2
  388.6 0.0 copy-start.3
  388.7 0.0 copy-start.6
  388.7 0.0 copy-start.7
  388.7 4.4 %multiply_subtract_fusion = (f32[48,6448]{1,0:T(8,128)}, f32[48,6448]{1,0:T(8,128)}, f32[48,6448]{1,0:T(8,128)}, f32[48,6448]{1,0:T(8,128)}) fusion(f32[48,6448]{1,0:T(8,128)S(1)} %copy-done, f32[48,6448]{1,0:T(8,128)} %param.23, f32[48,6448]{1,0:T(8,128)} %param.24, f32[48,3376]{1,0:T(8,128)S(1)} %slice.12, f32[48,3072]{1,0:T(8,128)S(1)} %copy-done.5), kind=kLoop, calls=%fused_computation.3 | loop fusion | flops 4952064 | bytes 9904128 | tf_op jit(solution)/shard_map/sub | solution.py:84
  393.0 0.0 copy-done.8
  393.0 0.0 copy-done.10
  393.0 0.0 copy-done.11
  393.1 0.0 copy-done.12
  393.1 0.7 multiply_subtract_fusion.2
  393.8 0.0 copy-done.13
  393.8 0.0 copy-done.17
  393.8 0.0 copy-done.18
  393.8 0.6 multiply_subtract_fusion.5
  394.4 0.0 copy-done.14
  394.4 0.0 copy-done.19
  394.4 0.0 copy-done.20
  394.4 0.6 multiply_subtract_fusion.4
  395.0 0.0 copy-done.2
  395.0 0.0 copy-done.3
  395.0 0.0 copy-done.6
  395.0 0.0 copy-done.7
  395.0 0.0 copy-start.4
  395.0 1.5 multiply_subtract_fusion.1
  396.5 0.5 copy-done.4
  397.1 0.0 copy-start.1
  397.1 1.1 copy.49
  398.2 1.3 copy-done.1
  399.5 1.7 copy.50
  401.2 0.8 copy.51
Async XLA Ops:
  312.5 74.2 %copy-start.9 = (f32[3,48]{1,0:T(4,128)S(1)}, f32[3,48]{1,0:T(4,128)}, u32[]{:S(2)}) copy-start(f32[3,48]{1,0:T(4,128)} %head_ref.1) | copy-start | bytes 1732
  312.5 74.2 %copy-start.15 = (f32[3,48]{1,0:T(4,128)S(1)}, f32[3,48]{1,0:T(4,128)}, u32[]{:S(2)}) copy-start(f32[3,48]{1,0:T(4,128)} %param.38) | copy-start | bytes 1732
  312.5 74.2 %copy-start.16 = (f32[3,48]{1,0:T(4,128)S(1)}, f32[3,48]{1,0:T(4,128)}, u32[]{:S(2)}) copy-start(f32[3,48]{1,0:T(4,128)} %param.39) | copy-start | bytes 1732
  312.5 76.0 %copy-start.5 = (f32[48,3072]{1,0:T(8,128)S(1)}, f32[48,3072]{1,0:T(8,128)}, u32[]{:S(2)}) copy-start(f32[48,3072]{1,0:T(8,128)} %get-tuple-element.78) | copy-start | bytes 1769476
  385.9 2.6 copy-start
  388.5 4.5 %copy-start.8 = (f32[5,104]{1,0:T(8,128)S(1)}, f32[5,104]{1,0:T(8,128)}, u32[]{:S(2)}) copy-start(f32[5,104]{1,0:T(8,128)} %conv_ref.1) | copy-start | bytes 6244
  388.5 4.5 %copy-start.10 = (f32[8,256]{1,0:T(8,128)S(1)}, f32[8,256]{1,0:T(8,128)}, u32[]{:S(2)}) copy-start(f32[8,256]{1,0:T(8,128)} %get-tuple-element.81) | copy-start | bytes 24580
  388.5 4.5 %copy-start.11 = (f32[5,104]{1,0:T(8,128)S(1)}, f32[5,104]{1,0:T(8,128)}, u32[]{:S(2)}) copy-start(f32[5,104]{1,0:T(8,128)} %param.29) | copy-start | bytes 6244
  388.6 4.5 %copy-start.12 = (f32[5,104]{1,0:T(8,128)S(1)}, f32[5,104]{1,0:T(8,128)}, u32[]{:S(2)}) copy-start(f32[5,104]{1,0:T(8,128)} %param.30) | copy-start | bytes 6244
  388.6 5.2 %copy-start.13 = (f32[48]{0:T(128)S(1)}, f32[48]{0:T(128)}, u32[]{:S(2)}) copy-start(f32[48]{0:T(128)} %param.31) | copy-start | bytes 580
  388.6 5.2 %copy-start.17 = (f32[48]{0:T(128)S(1)}, f32[48]{0:T(128)}, u32[]{:S(2)}) copy-start(f32[48]{0:T(128)} %param.32) | copy-start | bytes 580
  388.6 5.2 %copy-start.18 = (f32[48]{0:T(128)S(1)}, f32[48]{0:T(128)}, u32[]{:S(2)}) copy-start(f32[48]{0:T(128)} %param.33) | copy-start | bytes 580
  388.6 5.8 %copy-start.14 = (f32[96]{0:T(128)S(1)}, f32[96]{0:T(128)}, u32[]{:S(2)}) copy-start(f32[96]{0:T(128)} %param.34) | copy-start | bytes 1156
  388.6 5.8 %copy-start.19 = (f32[96]{0:T(128)S(1)}, f32[96]{0:T(128)}, u32[]{:S(2)}) copy-start(f32[96]{0:T(128)} %param.35) | copy-start | bytes 1156
  388.6 5.8 %copy-start.20 = (f32[96]{0:T(128)S(1)}, f32[96]{0:T(128)}, u32[]{:S(2)}) copy-start(f32[96]{0:T(128)} %param.36) | copy-start | bytes 1156
  388.6 6.4 %copy-start.2 = (f32[96,1536]{1,0:T(8,128)S(1)}, f32[96,1536]{1,0:T(8,128)}, u32[]{:S(2)}) copy-start(f32[96,1536]{1,0:T(8,128)} %out_ref.1) | copy-start | bytes 1769476
  388.6 6.4 %copy-start.3 = (f32[96,1536]{1,0:T(8,128)S(1)}, f32[96,1536]{1,0:T(8,128)}, u32[]{:S(2)}) copy-start(f32[96,1536]{1,0:T(8,128)} %get-tuple-element.137) | copy-start | bytes 1769476
  388.7 6.4 %copy-start.6 = (f32[96,1536]{1,0:T(8,128)S(1)}, f32[96,1536]{1,0:T(8,128)}, u32[]{:S(2)}) copy-start(f32[96,1536]{1,0:T(8,128)} %param.26) | copy-start | bytes 1769476
  388.7 6.4 %copy-start.7 = (f32[96,1536]{1,0:T(8,128)S(1)}, f32[96,1536]{1,0:T(8,128)}, u32[]{:S(2)}) copy-start(f32[96,1536]{1,0:T(8,128)} %param.27) | copy-start | bytes 1769476
  395.0 2.0 copy-start.4
  397.1 2.5 copy-start.1

commit v6 on v5

--- a/solution.py
+++ b/solution.py
@@ -702,7 +702,7 @@
             dcp_o[j + 2, 256 * g:256 * g + 256] = din[g].astype(bf)
         pass_edge(j, prev, din)
 
-    def final(bcin, bchalo, bctaps, raw, ds, step, b_r, c_r, hp, dst_acc, dc_acc, dds_acc, xu_acc, skips):
+    def final(bcin, bchalo, bctaps, raw, ds, step, b_r, c_r, hp, dst_acc, dc_acc, dds_acc, xu_acc, skips, pause):
         fill_pad(pad2, bcin[0], bchalo[0])
         dco2 = []
         for g, co in enumerate(conv(pad2, bctaps)):
@@ -713,11 +713,13 @@
             dc = dc + jnp.concatenate([mul(dst_acc[g, 0].T, b[:128]), mul(dst_acc[g, 1].T, b[128:]) + mul(dst_acc[g, 2].T, b[:128])], 0)
             s = sig(co)
             dco2.append(jnp.concatenate([db, dc], 1) * (s * (1.0 + co * (1.0 - s))))
+        pause(0)
         grads, din, prev = conv_back(pad2, dpad2, dco2, bctaps)
         cg_o[12] = grads
         for g in range(2):
             dcp_o[1, 256 * g:256 * g + 256] = din[g].astype(bf)
         pass_edge(TILES, prev, din)
+        pause(1)
         st = step[...]
         xut = xut_s[...]
         speed = -jnp.exp(hp[0:1])
@@ -906,17 +908,20 @@
 def back_call(mixed, proj, dn, x, par, ent, ds, step, dst, b, c, hp, rq, low_t, cot, collective_id):
     n, R, sk = 24, 48, 1
 
-    def kernel(mixed, z, dn, x, gain, cin, halo, taps, ent, ds, step, dst, b_r, c_r, hp, rq, bcin, bchalo, bctaps, raw, low_t, cot,
+    def kernel(mixed, z, dn, x, gain, cin, halo, taps, ent, ds, step, dst, b_r, c_r, hp, rq, bcin, bchalo, bctaps, raw, low_h, cot_h,
                dz_o, ol_o, dcp_o, cg_o, hg_o, rows_o, zsum, osum,
                dst_acc, dc_acc, dds_acc, xu_acc, skips, st_s, ct_s, got, part, out, out_sem, in_sem,
                pad, pad2, dpad, dpad2, db_s, xut_s, de_s, prv, lst, edge_in, e_out, e_in,
-               dxa_s, dz_s, rhs, lhs_s, *refs):
+               dxa_s, dz_s, rhs, lhs_s, cot, low_sem, cot_sem, *refs):
         j = pl.program_id(0)
         me = Place()
         line = Chain(me, -1, got, part, out, out_sem, in_sem, keeper(ds))
         red = Reduce(me, n, R, refs, sk)
         two_start, two_tile, two_final = sb2_make(me, dcp_o, cg_o, hg_o, pad, pad2, dpad, dpad2, db_s, xut_s, de_s, prv, lst, edge_in, e_out, e_in)
 
+        low_copy = pltpu.make_async_copy(low_h, lhs_s.at[0], low_sem)
+        cot_copy = pltpu.make_async_copy(cot_h, cot, cot_sem)
+
         def product(i, core, blocks):
             li = i // 12 * (1 + lax.rem(i, 2))
             rows = [lhs_s[li, 2 * yy + xx, core].reshape(4 * R, 512) for yy, xx in blocks]
@@ -934,16 +939,20 @@
         def rs(it):
             @pl.when(it < 12)
             def _(): rhs[lax.rem(it, 2)] = dz_s[...]
+            @pl.when(it == 12)
+            def _(): cot_copy.wait()
             @pl.when((it >= 12) & (it < n))
             def _(): rhs[lax.rem(it, 2)] = cot[:, pl.ds(pl.multiple_of((it - 12) // 2 * 256, 256), 256)]
             red.step(it, product, put)
 
         @pl.when(j == 0)
         def _():
+            low_copy.start()
+            cot_copy.start()
             greet(me.near())
             line.start()
             sb1_start(b_r, c_r, dst_acc, dc_acc, dds_acc, xu_acc, skips, st_s, ct_s)
-            lhs_s[0] = low_t[...]
+            low_copy.wait()
 
         @pl.when(j < TILES)
         def _():
@@ -961,9 +970,9 @@
 
         @pl.when(j == 2 * TILES - 1)
         def _():
-            two_final(bcin, bchalo, bctaps, raw, ds, step, b_r, c_r, hp, dst_acc, dc_acc, dds_acc, xu_acc, skips)
+            two_final(bcin, bchalo, bctaps, raw, ds, step, b_r, c_r, hp, dst_acc, dc_acc, dds_acc, xu_acc, skips, lambda k: rs(jnp.int32(n + k)))
             line.finish()
-            lax.fori_loop(n, n + 4 * sk, lambda it, _: (rs(it), 0)[1], 0)
+            lax.fori_loop(n + 2, n + 4 * sk, lambda it, _: (rs(it), 0)[1], 0)
             red.finish()
 
     D = pltpu.SemaphoreType.DMA
@@ -980,7 +989,7 @@
         pl.BlockSpec((1, 16, 256), lambda j: (2 + p2(j), 32, 0)),
         pl.BlockSpec((8, 256), lambda j: (0, p2(j))),
         one_time(12, 2, 128, 256), tok, tok, one_time(12, 8, 512), tok, tok, one_time(8, 128), one_time(2, 512, 128),
-        BC, BCH, BCT, RAW, one_time(4, 2, 4, 48, 512), one_time(512, 1536),
+        BC, BCH, BCT, RAW, pl.BlockSpec(memory_space=pl.ANY), pl.BlockSpec(memory_space=pl.ANY),
     ]
     out_specs = (
         pl.BlockSpec((1, 512, 256), lambda j: (p1(j), 0, 0)),
@@ -993,7 +1002,7 @@
         + Chain.scratch()
         + [V((2, 264, 256), f32), V((2, 264, 256), f32), V((2, 272, 256), f32), V((2, 272, 256), f32), V((512, 128), f32), V((512, 128), f32), V((2, 8, 128), f32),
            V((13, 16, 256), bf), V((13, 16, 256), f32), V((13, 16, 256), bf), D((13,)), D((13,))]
-        + [V((12, 512, 256), f32), V((512, 256), bf), V((2, 512, 256), bf), V((3, 4, 2, 4, 48, 512), bf)]
+        + [V((12, 512, 256), f32), V((512, 256), bf), V((2, 512, 256), bf), V((3, 4, 2, 4, 48, 512), bf), V((512, 1536), bf), D, D]
         + Reduce.scratch(n, R, sk)
     )
     return pl.pallas_call(
@@ -1005,8 +1014,8 @@
 def end_call(low_t, dcp, dz, ol, win, wout, tok, cot, par, cg, rows, hg, collective_id, skew=2):
     n, R = 14, 48
 
-    def kernel(lhs, dcp_ref, dz_ref, ol_ref, win_hbm, wout_hbm, tok, cot, par_ref, cg_ref, rows_ref, hg_ref, sums, blk, tg, small_o,
-               wbuf, wsem, obuf, osem, dn, flat, mail, box, m_out, m_in, *refs):
+    def kernel(lhs_h, dcp_h, dz_h, ol_h, win_hbm, wout_hbm, tok_h, cot_h, par_ref, cg_ref, rows_ref, hg_ref, sums, blk_h, tg_h, small_o,
+               lhs, dcp_ref, dz_ref, ol_ref, tok, cot, blk, tg, in_sem, dcp_sem, dz_sem, out_sem, wbuf, wsem, obuf, osem, dn, flat, mail, box, m_out, m_in, *refs):
         me = Place()
         def wcopy(t, p): return pltpu.make_async_copy(win_hbm.at[p], wbuf.at[lax.rem(t, 2), 0 if p is t else 1], wsem.at[lax.rem(t, 2), 0 if p is t else 1])
         def ocopy(i): return pltpu.make_async_copy(wout_hbm.at[i], obuf.at[lax.rem(i, 2)], osem.at[lax.rem(i, 2)])
@@ -1014,7 +1023,20 @@
             wcopy(t, t).start()
             @pl.when(t < 12)
             def _(): wcopy(t, t + 14).start()
+        def dcp_copy(p): return pltpu.make_async_copy(dcp_h.at[p], dcp_ref.at[p], dcp_sem.at[p])
+        def dz_copy(p): return pltpu.make_async_copy(dz_h.at[p], dz_ref.at[p], dz_sem.at[p])
+        whole = [pltpu.make_async_copy(a, b, in_sem.at[k]) for k, (a, b) in enumerate(((lhs_h, lhs), (tok_h, tok), (cot_h, cot), (ol_h, ol_ref)))]
+        tg_copy = pltpu.make_async_copy(tg, tg_h, out_sem.at[0])
+        blk_copy = pltpu.make_async_copy(blk, blk_h, out_sem.at[1])
+        whole[0].start()
         fetch(jnp.int32(0))
+        def pull(p, _):
+            dcp_copy(p).start()
+            @pl.when(p < 12)
+            def _(): dz_copy(p).start()
+            return 0
+        lax.fori_loop(0, n, pull, 0)
+        for copy in whole[1:]: copy.start()
         ocopy(jnp.int32(0)).start()
         ocopy(jnp.int32(1)).start()
         bar = pltpu.get_barrier_semaphore()
@@ -1063,29 +1085,33 @@
             at = jnp.where(i == 0, 13 * 256, jnp.where(i == 1, 12 * 256, (i - 2) * 256))
             sums[:, pl.ds(pl.multiple_of(at, 256), 256)] = jnp.concatenate([acc[0], acc[1]], 1)
 
-        def dgrad(t, q, dp):
-            s = lax.rem(t, 2)
-            w = jnp.concatenate([wbuf[s, q, h].reshape(1536, 128) for h in range(2)], axis=1)
-            return lax.dot_general(dp, w, (((1,), (1,)), ((), ())), preferred_element_type=f32)
+        def weights(t, q):
+            return jnp.concatenate([wbuf[lax.rem(t, 2), q, h].reshape(1536, 128) for h in range(2)], axis=1)
 
         def loop(it, _):
+            @pl.when(it < n)
+            def _(): dcp_copy(it).wait()
+            @pl.when(it < 12)
+            def _(): dz_copy(it).wait()
             red.step(it, product, put)
             @pl.when(it < n)
             def _():
                 @pl.when(it + 1 < n)
                 def _(): fetch(it + 1)
                 wcopy(it, it).wait()
-                r = dgrad(it, 0, dcp_ref[it])
-                @pl.when(it == 0)
-                def _(): dn[...] = r
-                @pl.when(it > 0)
-                def _(): dn[...] += r
             @pl.when(it < 12)
             def _():
                 wcopy(it, it + 14).wait()
-                dn[...] += dgrad(it, 1, dz_ref[it])
+                both = jnp.concatenate([dcp_ref[it], dz_ref[it]], 1)
+                dn[...] += lax.dot_general(both, jnp.concatenate([weights(it, 0), weights(it, 1)], 1), NT, preferred_element_type=f32)
+            @pl.when((it >= 12) & (it < n))
+            def _():
+                dn[...] += lax.dot_general(dcp_ref[it], weights(it, 0), NT, preferred_element_type=f32)
             @pl.when(it == n)
-            def _(): tail()
+            def _():
+                for copy in whole[1:]: copy.wait()
+                tail()
+                tg_copy.start()
             @pl.when((it >= n) & (it < n + 6))
             def _():
                 i = it - n
@@ -1096,7 +1122,11 @@
                 blk[:, at] = (tok[:, at].astype(f32) + jnp.dot(ol_ref[...], w, preferred_element_type=f32)).astype(bf)
                 @pl.when(i + 2 < 6)
                 def _(): ocopy(i + 2).start()
+            @pl.when(it == n + 5)
+            def _(): blk_copy.start()
             return 0
+        dn[...] = jnp.zeros_like(dn)
+        whole[0].wait()
         lax.fori_loop(0, n + 4 * skew, loop, 0)
         small_o[...] = mail[me.line]
         def take(k, _):
@@ -1104,14 +1134,17 @@
             small_o[...] += box[k - 1]
             return 0
         lax.fori_loop(1, 32, take, 0)
+        tg_copy.wait()
+        blk_copy.wait()
         red.finish()
 
     D, Sd = pltpu.SemaphoreType.DMA, jax.ShapeDtypeStruct
     vm, hb = pl.BlockSpec(memory_space=pltpu.VMEM), pl.BlockSpec(memory_space=pl.ANY)
     return pl.pallas_call(
         kernel, out_shape=(Sd((R, n * 256), f32), Sd((512, 1536), bf), Sd((512, 1536), f32), Sd((8, 256), f32)),
-        in_specs=[vm] * 4 + [hb] * 2 + [vm] * 6, out_specs=(vm, vm, vm, vm),
-        scratch_shapes=[V((2, 2, 2, 2, 2, 2, 192, 128), bf), D((2, 2)), V((2, 2, 2, 2, 2, 384, 128), bf), D((2,)),
+        in_specs=[hb] * 8 + [vm] * 4, out_specs=(vm, hb, hb, vm),
+        scratch_shapes=[V((4, 2, 192, 512), bf), V((14, 512, 256), bf), V((12, 512, 256), bf), V((512, 3072), bf), V((512, 1536), bf), V((512, 1536), bf), V((512, 1536), bf), V((512, 1536), f32),
+                        D((4,)), D((14,)), D((12,)), D((2,)), V((2, 2, 2, 2, 2, 2, 192, 128), bf), D((2, 2)), V((2, 2, 2, 2, 2, 384, 128), bf), D((2,)),
                         V((512, 1536), f32), V((8, 3584), f32), V((32, 8, 256), f32), V((31, 8, 256), f32), D((31,)), D((31,))]
         + Reduce.scratch(n, R, skew),
         compiler_params=pltpu.CompilerParams(collective_id=collective_id, has_side_effects=True, vmem_limit_bytes=63 << 20), name="end",

time: 402 us -> 393 us (0.978)
  Pallas kernels: 385 us -> 376 us
    pallas_call x1, Pallas kernels: 73.3 us -> 68 us  [end_call(): pl.pallas_call(kernel, out_shape=(Sd((R, n * 256), f32), Sd((512, 1536),...]
where the time goes in v6:
time: 393 us
  Pallas kernels  376 us (96%)
  other arithmetic  8.4 us (2%)
  local copies, waits for them, and re-layouts  7.58 us (2%)
    pallas_call x1, Pallas kernels, front_call(): pl.pallas_call(kernel, out_shape=(S((NI, TE, 256), f32), S(wi, bf), S(wo,...  169 us
    pallas_call x1, Pallas kernels, back_call(): pl.pallas_call(kernel, grid=(2 * TILES,), in_specs=in_specs, out_specs=ou...  139 us
    pallas_call x1, Pallas kernels, end_call(): pl.pallas_call(kernel, out_shape=(Sd((R, n * 256), f32), Sd((512, 1536),...  68 us
    sub x6, other arithmetic, adamw(): weight - learn_rate * (mean_hat / (jnp.sqrt(var_hat) + adam_eps) + decay_...  8.4 us

profile of v6, /device:TPU:0, one launch (start us, length us, event | category | flops | bytes accessed | tf_op | source)
XLA Modules:
  0.0 392.9 jit_solution(6481255513476624909)
XLA Ops:
  0.7 168.8 %front.1 = (f32[26,528,256]{2,1,0:T(8,128)}, bf16[26,2,2,2,2,192,128]{6,5,4,3,2,1,0:T(8,128)(2,1)}, bf16[6,2,2,2,2,384,128]{6,5,4,3,2,1,0:T(8,128)(2,1)}, f32[12...) custom-call(f32[48,6448]{1,0:T(8,128)} %in_ref.1, ...), custom_call_target="tpu_custom_call" | custom-call | tf_op jit(solution)/shard_map/front/pallas_call | solution.py:1420
  169.5 139.2 %back.1 = (bf16[12,512,256]{2,1,0:T(8,128)(2,1)}, bf16[512,3072]{1,0:T(8,128)(2,1)}, bf16[14,512,256]{2,1,0:T(8,128)(2,1)}, f32[13,8,256]{2,1,0:T(8,128)}, f32[8...) custom-call(f32[12,512,256]{2,1,0:T(8,128)} %get-tuple-element.55.mixed, ...), custom_call_target="tpu_custom_call" | custom-call | tf_op jit(solution)/shard_map/back/pallas_call | solution.py:1008
  308.7 0.0 copy-start.9
  308.7 0.0 copy-start.15
  308.7 0.0 copy-start.16
  308.7 0.0 copy-start.5
  308.7 68.0 %end.1 = (f32[48,3584]{1,0:T(8,128)}, bf16[512,1536]{1,0:T(8,128)(2,1)}, f32[512,1536]{1,0:T(8,128)}, f32[8,256]{1,0:T(8,128)}) custom-call(bf16[4,2,192,512]{3,2,1,0:T(8,128)(2,1)} %bitcast.20, bf16[14,512,256]{2,1,0:T(8,128)(2,1)} %get-tuple-element.68.dcp_h, bf16[12,512,256]{2,1,0:T(8,128)(2,1)} %get-tuple-element.69.dz_h, ...), custom_call_target="tpu_custom_call" | custom-call | tf_op jit(solution)/shard_map/end/pallas_call | solution.py:1143
  376.7 0.0 copy-start
  376.7 0.9 fusion.12
  377.6 0.0 copy-done.9
  377.6 0.0 copy-done.15
  377.6 0.0 copy-done.16
  377.6 0.6 multiply_subtract_fusion.3
  378.2 1.1 slice.12
  379.4 0.0 copy-done.5
  379.4 0.0 copy-done
  379.4 0.0 copy-start.8
  379.4 0.0 copy-start.10
  379.4 0.0 copy-start.11
  379.4 0.0 copy-start.12
  379.4 0.0 copy-start.13
  379.4 0.0 copy-start.17
  379.5 0.0 copy-start.18
  379.5 0.0 copy-start.14
  379.5 0.0 copy-start.19
  379.5 0.0 copy-start.20
  379.5 0.0 copy-start.2
  379.5 0.0 copy-start.3
  379.5 0.0 copy-start.6
  379.5 0.0 copy-start.7
  379.5 4.4 %multiply_subtract_fusion = (f32[48,6448]{1,0:T(8,128)}, f32[48,6448]{1,0:T(8,128)}, f32[48,6448]{1,0:T(8,128)}, f32[48,6448]{1,0:T(8,128)}) fusion(f32[48,6448]{1,0:T(8,128)S(1)} %copy-done, f32[48,6448]{1,0:T(8,128)} %param.23, f32[48,6448]{1,0:T(8,128)} %param.24, f32[48,3376]{1,0:T(8,128)S(1)} %slice.12, f32[48,3072]{1,0:T(8,128)S(1)} %copy-done.5), kind=kLoop, calls=%fused_computation.3 | loop fusion | flops 4952064 | bytes 9904128 | tf_op jit(solution)/shard_map/sub | solution.py:84
  383.9 0.0 copy-done.8
  383.9 0.0 copy-done.10
  383.9 0.0 copy-done.11
  383.9 0.0 copy-done.12
  383.9 0.7 multiply_subtract_fusion.2
  384.6 0.0 copy-done.13
  384.6 0.0 copy-done.17
  384.6 0.0 copy-done.18
  384.6 0.6 multiply_subtract_fusion.5
  385.3 0.0 copy-done.14
  385.3 0.0 copy-done.19
  385.3 0.0 copy-done.20
  385.3 0.6 multiply_subtract_fusion.4
  385.9 0.0 copy-done.2
  385.9 0.0 copy-done.3
  385.9 0.0 copy-done.6
  385.9 0.0 copy-done.7
  385.9 0.0 copy-start.4
  385.9 1.5 multiply_subtract_fusion.1
  387.4 0.5 copy-done.4
  387.9 0.0 copy-start.1
  387.9 1.1 copy.49
  389.1 1.3 copy-done.1
  390.4 1.7 copy.50
  392.1 0.8 copy.51
Async XLA Ops:
  308.7 68.9 %copy-start.9 = (f32[3,48]{1,0:T(4,128)S(1)}, f32[3,48]{1,0:T(4,128)}, u32[]{:S(2)}) copy-start(f32[3,48]{1,0:T(4,128)} %head_ref.1) | copy-start | bytes 1732
  308.7 68.9 %copy-start.15 = (f32[3,48]{1,0:T(4,128)S(1)}, f32[3,48]{1,0:T(4,128)}, u32[]{:S(2)}) copy-start(f32[3,48]{1,0:T(4,128)} %param.38) | copy-start | bytes 1732
  308.7 68.9 %copy-start.16 = (f32[3,48]{1,0:T(4,128)S(1)}, f32[3,48]{1,0:T(4,128)}, u32[]{:S(2)}) copy-start(f32[3,48]{1,0:T(4,128)} %param.39) | copy-start | bytes 1732
  308.7 70.6 %copy-start.5 = (f32[48,3072]{1,0:T(8,128)S(1)}, f32[48,3072]{1,0:T(8,128)}, u32[]{:S(2)}) copy-start(f32[48,3072]{1,0:T(8,128)} %get-tuple-element.78) | copy-start | bytes 1769476
  376.7 2.6 copy-start
  379.4 4.5 %copy-start.8 = (f32[5,104]{1,0:T(8,128)S(1)}, f32[5,104]{1,0:T(8,128)}, u32[]{:S(2)}) copy-start(f32[5,104]{1,0:T(8,128)} %conv_ref.1) | copy-start | bytes 6244
  379.4 4.5 %copy-start.10 = (f32[8,256]{1,0:T(8,128)S(1)}, f32[8,256]{1,0:T(8,128)}, u32[]{:S(2)}) copy-start(f32[8,256]{1,0:T(8,128)} %get-tuple-element.81) | copy-start | bytes 24580
  379.4 4.5 %copy-start.11 = (f32[5,104]{1,0:T(8,128)S(1)}, f32[5,104]{1,0:T(8,128)}, u32[]{:S(2)}) copy-start(f32[5,104]{1,0:T(8,128)} %param.29) | copy-start | bytes 6244
  379.4 4.5 %copy-start.12 = (f32[5,104]{1,0:T(8,128)S(1)}, f32[5,104]{1,0:T(8,128)}, u32[]{:S(2)}) copy-start(f32[5,104]{1,0:T(8,128)} %param.30) | copy-start | bytes 6244
  379.4 5.2 %copy-start.13 = (f32[48]{0:T(128)S(1)}, f32[48]{0:T(128)}, u32[]{:S(2)}) copy-start(f32[48]{0:T(128)} %param.31) | copy-start | bytes 580
  379.4 5.2 %copy-start.17 = (f32[48]{0:T(128)S(1)}, f32[48]{0:T(128)}, u32[]{:S(2)}) copy-start(f32[48]{0:T(128)} %param.32) | copy-start | bytes 580
  379.5 5.2 %copy-start.18 = (f32[48]{0:T(128)S(1)}, f32[48]{0:T(128)}, u32[]{:S(2)}) copy-start(f32[48]{0:T(128)} %param.33) | copy-start | bytes 580
  379.5 5.8 %copy-start.14 = (f32[96]{0:T(128)S(1)}, f32[96]{0:T(128)}, u32[]{:S(2)}) copy-start(f32[96]{0:T(128)} %param.34) | copy-start | bytes 1156
  379.5 5.8 %copy-start.19 = (f32[96]{0:T(128)S(1)}, f32[96]{0:T(128)}, u32[]{:S(2)}) copy-start(f32[96]{0:T(128)} %param.35) | copy-start | bytes 1156
  379.5 5.8 %copy-start.20 = (f32[96]{0:T(128)S(1)}, f32[96]{0:T(128)}, u32[]{:S(2)}) copy-start(f32[96]{0:T(128)} %param.36) | copy-start | bytes 1156
  379.5 6.4 %copy-start.2 = (f32[96,1536]{1,0:T(8,128)S(1)}, f32[96,1536]{1,0:T(8,128)}, u32[]{:S(2)}) copy-start(f32[96,1536]{1,0:T(8,128)} %out_ref.1) | copy-start | bytes 1769476
  379.5 6.4 %copy-start.3 = (f32[96,1536]{1,0:T(8,128)S(1)}, f32[96,1536]{1,0:T(8,128)}, u32[]{:S(2)}) copy-start(f32[96,1536]{1,0:T(8,128)} %get-tuple-element.137) | copy-start | bytes 1769476
  379.5 6.4 %copy-start.6 = (f32[96,1536]{1,0:T(8,128)S(1)}, f32[96,1536]{1,0:T(8,128)}, u32[]{:S(2)}) copy-start(f32[96,1536]{1,0:T(8,128)} %param.26) | copy-start | bytes 1769476
  379.5 6.4 %copy-start.7 = (f32[96,1536]{1,0:T(8,128)S(1)}, f32[96,1536]{1,0:T(8,128)}, u32[]{:S(2)}) copy-start(f32[96,1536]{1,0:T(8,128)} %param.27) | copy-start | bytes 1769476
  385.9 2.0 copy-start.4
  387.9 2.5 copy-start.1
